TPU v7x, 256 devices: a whole 4x4x8 slice. The times are simulated.
256 devices in a mesh: gx: 32 (over x, z_hi, core), gy: 8 (over y, z_lo).
Axes of the slice: x: 4, y: 4, z: 8 (z_hi: 4, z_lo: 2; z = z_hi * 2 + z_lo), core: 2. Of those that a mesh axis runs over, the one named last changes fastest.
Arguments:
- positions: float32 [3, 32, 16, 12, 128], P(None, 'gx', 'gy'), may hold values from 0 to 1
- velocities: float32 [3, 32, 16, 12, 128], P(None, 'gx', 'gy'), may hold values from -8 to 8
- counts: int32 [32, 16, 12], P('gx', 'gy'), may hold values from 64 to 128
Outputs:
- positions_out: float32 [3, 32, 16, 12, 128], P(None, 'gx', 'gy')
- velocities_out: float32 [3, 32, 16, 12, 128], P(None, 'gx', 'gy')
- forces_out: float32 [3, 32, 16, 12, 128], P(None, 'gx', 'gy')
Inputs may be any that keep to these rules, and one draw needn't show every extreme that they name: `counts`: the number of atoms in a cell; slots from that number up to 128 are empty.
All inputs are finite; a program needn't handle non-finite values.
Results may differ from a plain program's by a relative error of at most 0.0001.
Values sent between devices are 32-bit elements; how exact they have to be, the bound alone decides.
No kernel may reach another device: no remote copies, remote signals or barrier semaphores. Data moves between devices by JAX's collectives and lax.ppermute only.
A program may use at most 64 MiB of HBM per device.

v0:
```python
import jax
import jax.numpy as jnp
from jax import lax
from jax.sharding import PartitionSpec as P

STEPS = 2


TIME_STEP = 0.05
DENSITY_SCALE = 0.0625
PAIR_SCALE = 0.0625


def with_halo(value, sides, width):
    for axis, dim in sides:
        devices, length = (lax.axis_size(axis), value.shape[dim])
        up = [(i, (i + 1) % devices) for i in range(devices)]
        down = [(j, i) for i, j in up]
        last = lax.slice_in_dim(value, length - width, length, axis=dim)
        first = lax.slice_in_dim(value, 0, width, axis=dim)
        before = lax.ppermute(last, axis, up)
        after = lax.ppermute(first, axis, down)
        value = jnp.concatenate([before, value, after], axis=dim)
    return value


def offset_triple(offset_id):
    return (offset_id // 9, offset_id // 3 % 3, offset_id % 3)


def neighbour_block(extended, offset_id):
    first, second, third = offset_triple(offset_id)
    target = (extended.shape[1] - 2, extended.shape[2] - 2, extended.shape[3] - 2)
    return extended[
        :, first : first + target[0], second : second + target[1], third : third + target[2], :
    ]


def pair_terms(center, extended, filled, offset_id):
    slots = center.shape[-1]
    neighbours = neighbour_block(extended, offset_id)
    present = neighbour_block(filled, offset_id)[0]
    triple = offset_triple(offset_id)
    parts = []
    for component in range(3):
        moved = neighbours[component] + float(triple[component] - 1)
        parts.append(moved[..., None, :] - center[component][..., :, None])
    square = parts[0] * parts[0] + parts[1] * parts[1] + parts[2] * parts[2]
    reach = jnp.maximum(1.0 - square, 0.0)
    weights_mask = present[..., None, :]
    if offset_id == 13:
        weights_mask = weights_mask * (1.0 - jnp.eye(slots, dtype=center.dtype))
    return (parts, reach, weights_mask)


def density_pass(center, extended, filled):
    running = jnp.zeros(center.shape[1:], center.dtype)
    for offset_id in range(27):
        parts, reach, weights_mask = pair_terms(center, extended, filled, offset_id)
        running = running + jnp.sum(weights_mask * reach * reach, axis=-1)
    return DENSITY_SCALE * running


def force_pass(center, present_own, slope_own, extended, filled, slope_ext):
    running = jnp.zeros(center.shape, center.dtype)
    for offset_id in range(27):
        parts, reach, weights_mask = pair_terms(center, extended, filled, offset_id)
        slope_near = neighbour_block(slope_ext, offset_id)[0]
        both = slope_own[..., :, None] + slope_near[..., None, :]
        coupling = (
            weights_mask * reach * (-2.0 * DENSITY_SCALE * both - 4.0 * PAIR_SCALE * reach * reach)
        )
        running = running + 2.0 * jnp.stack(
            [jnp.sum(coupling * parts[component], axis=-1) for component in range(3)]
        )
    return running * present_own[None]


def slots_filled(amount, slots):
    places = lax.broadcasted_iota(amount.dtype, amount.shape + (slots,), amount.ndim)
    return (places < amount[..., None]).astype(amount.dtype)


def wrap_depth(field):
    return jnp.concatenate([field[:, :, :, -1:], field, field[:, :, :, :1]], axis=3)


def import_cells(positions, amount):
    extended, reached = (
        with_halo(positions, (("gx", 1), ("gy", 2)), 1),
        with_halo(amount, (("gx", 1), ("gy", 2)), 1),
    )
    return (wrap_depth(extended), wrap_depth(reached))


def forces_both_sides(positions, amount):
    slots = positions.shape[-1]
    extended, reached = import_cells(positions, amount[None])
    filled = slots_filled(reached, slots)
    filled_own = slots_filled(amount, slots)
    density = density_pass(positions, extended, filled)
    slope = -0.5 / jnp.sqrt(1.0 + density)
    slope_halo = with_halo(slope[None], (("gx", 1), ("gy", 2)), 1)
    slope_ext = wrap_depth(slope_halo)
    return force_pass(positions, filled_own, slope, extended, filled, slope_ext)


def forces_of(positions, amount):
    return forces_both_sides(positions, amount)


def shards(positions, velocities, counts):
    amount = counts.astype(jnp.float32)
    pushed = forces_of(positions, amount)

    def verlet_step(step_index, state):
        places, speeds, pulled = state
        speeds = speeds + 0.5 * TIME_STEP * pulled
        places = places + TIME_STEP * speeds
        pulled = forces_of(places, amount)
        speeds = speeds + 0.5 * TIME_STEP * pulled
        return (places, speeds, pulled)

    positions, velocities, pushed = lax.fori_loop(
        0, STEPS, verlet_step, (positions, velocities, pushed)
    )
    return (positions, velocities, pushed)


def solution(mesh):
    in_specs = (
        P(None, "gx", "gy", None, None),
        P(None, "gx", "gy", None, None),
        P("gx", "gy", None),
    )
    out_specs = (
        P(None, "gx", "gy", None, None),
        P(None, "gx", "gy", None, None),
        P(None, "gx", "gy", None, None),
    )
    return jax.shard_map(shards, mesh=mesh, in_specs=in_specs, out_specs=out_specs, check_vma=False)
```

profile of v0, /device:TPU:1, one launch (start us, length us, event | category | flops | bytes accessed | tf_op | source)
XLA Modules:
  0.0 415.7 jit_solution(16522572573106478832)
XLA Ops:
  67.4 7.8 %fusion.404 = (f32[2,12,128]{2,1,0:T(8,128)S(1)}, f32[2,12,128]{2,1,0:T(8,128)S(1)}, f32[2,12,128]{2,1,0:T(8,128)S(1)}, f32[2,12,128]{2,1,0:T(8,128)S(1)}, f32[2...) fusion(f32[2,12,128]{2,1,0:T(8,128)S(1)} %get-tuple-element.574, ...), kind=kLoop, calls=%fused_computation.1067 | loop fusion | flops 27497472 | bytes 360448 | tf_op jit(solution)/shard_map/reduce_sum | solution.py:74
  75.2 7.8 %fusion.396 = (f32[2,12,128]{2,1,0:T(8,128)S(1)}, f32[2,12,128]{2,1,0:T(8,128)S(1)}, f32[2,12,128]{2,1,0:T(8,128)S(1)}, f32[2,12,128]{2,1,0:T(8,128)S(1)}, f32[2...) fusion(f32[2,12,128]{2,1,0:T(8,128)S(1)} %get-tuple-element.639, ...), kind=kLoop, calls=%fused_computation.1059 | loop fusion | flops 27104256 | bytes 344064 | tf_op jit(solution)/shard_map/reduce_sum | solution.py:74
  83.0 7.8 %fusion.388 = (f32[2,12,128]{2,1,0:T(8,128)S(1)}, f32[2,12,128]{2,1,0:T(8,128)S(1)}, f32[2,12,128]{2,1,0:T(8,128)S(1)}, f32[2,12,128]{2,1,0:T(8,128)S(1)}, f32[2...) fusion(f32[2,12,128]{2,1,0:T(8,128)S(1)} %get-tuple-element.726, ...), kind=kLoop, calls=%fused_computation.1051 | loop fusion | flops 27104256 | bytes 344064 | tf_op jit(solution)/shard_map/reduce_sum | solution.py:74
  90.8 7.8 %fusion.380 = (f32[2,12,128]{2,1,0:T(8,128)S(1)}, f32[2,12,128]{2,1,0:T(8,128)S(1)}, f32[2,12,128]{2,1,0:T(8,128)S(1)}, f32[2,12,128]{2,1,0:T(8,128)S(1)}, f32[2...) fusion(f32[2,12,128]{2,1,0:T(8,128)S(1)} %get-tuple-element.597, ...), kind=kLoop, calls=%fused_computation.1043 | loop fusion | flops 27104256 | bytes 344064 | tf_op jit(solution)/shard_map/reduce_sum | solution.py:74
  98.6 7.8 %fusion.372 = (f32[2,12,128]{2,1,0:T(8,128)S(1)}, f32[2,12,128]{2,1,0:T(8,128)S(1)}, f32[2,12,128]{2,1,0:T(8,128)S(1)}, f32[2,12,128]{2,1,0:T(8,128)S(1)}, f32[2...) fusion(f32[2,12,128]{2,1,0:T(8,128)S(1)} %get-tuple-element.703, ...), kind=kLoop, calls=%fused_computation.1035 | loop fusion | flops 27104256 | bytes 344064 | tf_op jit(solution)/shard_map/reduce_sum | solution.py:74
  106.4 7.8 %fusion.364 = (f32[2,12,128]{2,1,0:T(8,128)S(1)}, f32[2,12,128]{2,1,0:T(8,128)S(1)}, f32[2,12,128]{2,1,0:T(8,128)S(1)}, f32[2,12,128]{2,1,0:T(8,128)S(1)}, f32[2...) fusion(f32[2,12,128]{2,1,0:T(8,128)S(1)} %get-tuple-element.722, ...), kind=kLoop, calls=%fused_computation.1027 | loop fusion | flops 27104256 | bytes 344064 | tf_op jit(solution)/shard_map/reduce_sum | solution.py:74
  114.2 7.8 %fusion.356 = (f32[2,12,128]{2,1,0:T(8,128)S(1)}, f32[2,12,128]{2,1,0:T(8,128)S(1)}, f32[2,12,128]{2,1,0:T(8,128)S(1)}, f32[2,12,128]{2,1,0:T(8,128)S(1)}, f32[2...) fusion(f32[2,12,128]{2,1,0:T(8,128)S(1)} %get-tuple-element.600, ...), kind=kLoop, calls=%fused_computation.1019 | loop fusion | flops 27104256 | bytes 344064 | tf_op jit(solution)/shard_map/reduce_sum | solution.py:74
  122.0 7.8 %fusion.348 = (f32[2,12,128]{2,1,0:T(8,128)S(1)}, f32[2,12,128]{2,1,0:T(8,128)S(1)}, f32[2,12,128]{2,1,0:T(8,128)S(1)}, f32[2,12,128]{2,1,0:T(8,128)S(1)}, f32[2...) fusion(f32[2,12,128]{2,1,0:T(8,128)S(1)} %get-tuple-element.635, ...), kind=kLoop, calls=%fused_computation.1011 | loop fusion | flops 27104256 | bytes 344064 | tf_op jit(solution)/shard_map/reduce_sum | solution.py:74
  129.8 7.8 %fusion.340 = (f32[2,12,128]{2,1,0:T(8,128)S(1)}, f32[2,12,128]{2,1,0:T(8,128)S(1)}, f32[2,12,128]{2,1,0:T(8,128)S(1)}, f32[2,12,128]{2,1,0:T(8,128)S(1)}, f32[2...) fusion(f32[2,12,128]{2,1,0:T(8,128)S(1)} %copy.235, ...), kind=kLoop, calls=%fused_computation.1003 | loop fusion | flops 27104256 | bytes 344064 | tf_op jit(solution)/shard_map/reduce_sum | solution.py:74
  137.8 275.8 %while.16 = (s32[]{:T(128)}, f32[3,1,2,12,128]{4,3,2,1,0:T(8,128)S(1)}, f32[3,1,2,12,128]{4,3,2,1,0:T(8,128)S(1)}, f32[3,1,2,12,128]{4,3,2,1,0:T(8,128)S(1)}, f3...) while((s32[]{:T(128)}, f32[3,1,2,12,128]{4,3,2,1,0:T(8,128)S(1)}, ...), condition=%wide.region_217.0_spmd, body=%wide.region_108.0_spmd.sunk | while | flops 385606656 | bytes 13978765 | solution.py:124
  152.7 7.2 %collective-permute-start = (f32[3,1,2,12,128]{4,3,2,1,0:T(8,128)S(1)}, f32[3,1,2,12,128]{4,3,2,1,0:T(8,128)S(1)}, u32[]{:S(2)}, u32[]{:S(2)}) collective-permute-start(f32[3,1,2,12,128]{4,3,2,1,0:T(8,128)S(1)} %multiply_add_fusion.5), channel_id=1, source_target_pairs={{8,0},{16,8},{24,16},{32,24},{40,32},{48,40},{56,48},{64,56},{72,6... | collective-permute-start | bytes 110600 | tf_op jit(solution)/shard_map/while/body/eval_jaxpr/ppermute | solution.py:22
  200.2 8.5 %collective-permute-start.4 = (f32[1,1,2,12,128]{4,3,2,1,0:T(8,128)S(1)}, f32[1,1,2,12,128]{4,3,2,1,0:T(8,128)S(1)}, u32[]{:S(2)}, u32[]{:S(2)}) collective-permute-start(f32[1,1,2,12,128]{4,3,2,1,0:T(8,128)S(1)} %fusion.728), channel_id=1, source_target_pairs={{8,0},{16,8},{24,16},{32,24},{40,32},{48,40},{56,48},{64,56},{72,6... | collective-permute-start | bytes 36872 | tf_op jit(solution)/shard_map/while/body/eval_jaxpr/ppermute | solution.py:22
  215.4 7.8 %fusion.739 = (f32[2,12,128]{2,1,0:T(8,128)S(1)}, f32[2,12,128]{2,1,0:T(8,128)S(1)}, f32[2,12,128]{2,1,0:T(8,128)S(1)}, f32[2,12,128]{2,1,0:T(8,128)S(1)}, f32[2...) fusion(f32[2,12,128]{2,1,0:T(8,128)S(1)} %get-tuple-element.113, ...), kind=kLoop, calls=%fused_computation.309.clone.1 | loop fusion | flops 27497472 | bytes 360448 | tf_op jit(solution)/shard_map/while/body/eval_jaxpr/reduce_sum | solution.py:74
  223.2 7.8 %fusion.740 = (f32[2,12,128]{2,1,0:T(8,128)S(1)}, f32[2,12,128]{2,1,0:T(8,128)S(1)}, f32[2,12,128]{2,1,0:T(8,128)S(1)}, f32[2,12,128]{2,1,0:T(8,128)S(1)}, f32[2...) fusion(f32[2,12,128]{2,1,0:T(8,128)S(1)} %get-tuple-element.111, ...), kind=kLoop, calls=%fused_computation.301.clone.1 | loop fusion | flops 27104256 | bytes 344064 | tf_op jit(solution)/shard_map/while/body/eval_jaxpr/reduce_sum | solution.py:74
  231.1 7.8 %fusion.738 = (f32[2,12,128]{2,1,0:T(8,128)S(1)}, f32[2,12,128]{2,1,0:T(8,128)S(1)}, f32[2,12,128]{2,1,0:T(8,128)S(1)}, f32[2,12,128]{2,1,0:T(8,128)S(1)}, f32[2...) fusion(f32[2,12,128]{2,1,0:T(8,128)S(1)} %get-tuple-element.111, ...), kind=kLoop, calls=%fused_computation.293.clone.1 | loop fusion | flops 27104256 | bytes 344064 | tf_op jit(solution)/shard_map/while/body/eval_jaxpr/reduce_sum | solution.py:74
  238.9 7.8 %fusion.737 = (f32[2,12,128]{2,1,0:T(8,128)S(1)}, f32[2,12,128]{2,1,0:T(8,128)S(1)}, f32[2,12,128]{2,1,0:T(8,128)S(1)}, f32[2,12,128]{2,1,0:T(8,128)S(1)}, f32[2...) fusion(f32[2,12,128]{2,1,0:T(8,128)S(1)} %get-tuple-element.112, ...), kind=kLoop, calls=%fused_computation.285.clone.1 | loop fusion | flops 27104256 | bytes 344064 | tf_op jit(solution)/shard_map/while/body/eval_jaxpr/reduce_sum | solution.py:74
  246.7 7.8 %fusion.736 = (f32[2,12,128]{2,1,0:T(8,128)S(1)}, f32[2,12,128]{2,1,0:T(8,128)S(1)}, f32[2,12,128]{2,1,0:T(8,128)S(1)}, f32[2,12,128]{2,1,0:T(8,128)S(1)}, f32[2...) fusion(f32[2,12,128]{2,1,0:T(8,128)S(1)} %get-tuple-element.109, ...), kind=kLoop, calls=%fused_computation.277.clone.1 | loop fusion | flops 27104256 | bytes 344064 | tf_op jit(solution)/shard_map/while/body/eval_jaxpr/reduce_sum | solution.py:74
  254.5 7.8 %fusion.735 = (f32[2,12,128]{2,1,0:T(8,128)S(1)}, f32[2,12,128]{2,1,0:T(8,128)S(1)}, f32[2,12,128]{2,1,0:T(8,128)S(1)}, f32[2,12,128]{2,1,0:T(8,128)S(1)}, f32[2...) fusion(f32[2,12,128]{2,1,0:T(8,128)S(1)} %get-tuple-element.107, ...), kind=kLoop, calls=%fused_computation.269.clone.1 | loop fusion | flops 27104256 | bytes 344064 | tf_op jit(solution)/shard_map/while/body/eval_jaxpr/reduce_sum | solution.py:74
  262.3 7.8 %fusion.734 = (f32[2,12,128]{2,1,0:T(8,128)S(1)}, f32[2,12,128]{2,1,0:T(8,128)S(1)}, f32[2,12,128]{2,1,0:T(8,128)S(1)}, f32[2,12,128]{2,1,0:T(8,128)S(1)}, f32[2...) fusion(f32[2,12,128]{2,1,0:T(8,128)S(1)} %get-tuple-element.105, ...), kind=kLoop, calls=%fused_computation.261.clone.1 | loop fusion | flops 27104256 | bytes 344064 | tf_op jit(solution)/shard_map/while/body/eval_jaxpr/reduce_sum | solution.py:74
  270.1 7.8 %fusion.733 = (f32[2,12,128]{2,1,0:T(8,128)S(1)}, f32[2,12,128]{2,1,0:T(8,128)S(1)}, f32[2,12,128]{2,1,0:T(8,128)S(1)}, f32[2,12,128]{2,1,0:T(8,128)S(1)}, f32[2...) fusion(f32[2,12,128]{2,1,0:T(8,128)S(1)} %get-tuple-element.101, ...), kind=kLoop, calls=%fused_computation.253.clone.1 | loop fusion | flops 27104256 | bytes 344064 | tf_op jit(solution)/shard_map/while/body/eval_jaxpr/reduce_sum | solution.py:74
  277.9 7.8 %fusion.732 = (f32[2,12,128]{2,1,0:T(8,128)S(1)}, f32[2,12,128]{2,1,0:T(8,128)S(1)}, f32[2,12,128]{2,1,0:T(8,128)S(1)}, f32[2,12,128]{2,1,0:T(8,128)S(1)}, f32[2...) fusion(f32[2,12,128]{2,1,0:T(8,128)S(1)} %get-tuple-element.101, ...), kind=kLoop, calls=%fused_computation.245.clone.1 | loop fusion | flops 27104256 | bytes 344064 | tf_op jit(solution)/shard_map/while/body/eval_jaxpr/reduce_sum | solution.py:74
  286.0 6.9 %collective-permute-start = (f32[3,1,2,12,128]{4,3,2,1,0:T(8,128)S(1)}, f32[3,1,2,12,128]{4,3,2,1,0:T(8,128)S(1)}, u32[]{:S(2)}, u32[]{:S(2)}) collective-permute-start(f32[3,1,2,12,128]{4,3,2,1,0:T(8,128)S(1)} %multiply_add_fusion.5), channel_id=1, source_target_pairs={{8,0},{16,8},{24,16},{32,24},{40,32},{48,40},{56,48},{64,56},{72,6... | collective-permute-start | bytes 110600 | tf_op jit(solution)/shard_map/while/body/eval_jaxpr/ppermute | solution.py:22
  329.1 7.2 %collective-permute-start.4 = (f32[1,1,2,12,128]{4,3,2,1,0:T(8,128)S(1)}, f32[1,1,2,12,128]{4,3,2,1,0:T(8,128)S(1)}, u32[]{:S(2)}, u32[]{:S(2)}) collective-permute-start(f32[1,1,2,12,128]{4,3,2,1,0:T(8,128)S(1)} %fusion.728), channel_id=1, source_target_pairs={{8,0},{16,8},{24,16},{32,24},{40,32},{48,40},{56,48},{64,56},{72,6... | collective-permute-start | bytes 36872 | tf_op jit(solution)/shard_map/while/body/eval_jaxpr/ppermute | solution.py:22
  343.1 7.8 %fusion.739 = (f32[2,12,128]{2,1,0:T(8,128)S(1)}, f32[2,12,128]{2,1,0:T(8,128)S(1)}, f32[2,12,128]{2,1,0:T(8,128)S(1)}, f32[2,12,128]{2,1,0:T(8,128)S(1)}, f32[2...) fusion(f32[2,12,128]{2,1,0:T(8,128)S(1)} %get-tuple-element.113, ...), kind=kLoop, calls=%fused_computation.309.clone.1 | loop fusion | flops 27497472 | bytes 360448 | tf_op jit(solution)/shard_map/while/body/eval_jaxpr/reduce_sum | solution.py:74
  350.9 7.8 %fusion.740 = (f32[2,12,128]{2,1,0:T(8,128)S(1)}, f32[2,12,128]{2,1,0:T(8,128)S(1)}, f32[2,12,128]{2,1,0:T(8,128)S(1)}, f32[2,12,128]{2,1,0:T(8,128)S(1)}, f32[2...) fusion(f32[2,12,128]{2,1,0:T(8,128)S(1)} %get-tuple-element.111, ...), kind=kLoop, calls=%fused_computation.301.clone.1 | loop fusion | flops 27104256 | bytes 344064 | tf_op jit(solution)/shard_map/while/body/eval_jaxpr/reduce_sum | solution.py:74
  358.7 7.8 %fusion.738 = (f32[2,12,128]{2,1,0:T(8,128)S(1)}, f32[2,12,128]{2,1,0:T(8,128)S(1)}, f32[2,12,128]{2,1,0:T(8,128)S(1)}, f32[2,12,128]{2,1,0:T(8,128)S(1)}, f32[2...) fusion(f32[2,12,128]{2,1,0:T(8,128)S(1)} %get-tuple-element.111, ...), kind=kLoop, calls=%fused_computation.293.clone.1 | loop fusion | flops 27104256 | bytes 344064 | tf_op jit(solution)/shard_map/while/body/eval_jaxpr/reduce_sum | solution.py:74
  366.5 7.8 %fusion.737 = (f32[2,12,128]{2,1,0:T(8,128)S(1)}, f32[2,12,128]{2,1,0:T(8,128)S(1)}, f32[2,12,128]{2,1,0:T(8,128)S(1)}, f32[2,12,128]{2,1,0:T(8,128)S(1)}, f32[2...) fusion(f32[2,12,128]{2,1,0:T(8,128)S(1)} %get-tuple-element.112, ...), kind=kLoop, calls=%fused_computation.285.clone.1 | loop fusion | flops 27104256 | bytes 344064 | tf_op jit(solution)/shard_map/while/body/eval_jaxpr/reduce_sum | solution.py:74
  374.3 7.8 %fusion.736 = (f32[2,12,128]{2,1,0:T(8,128)S(1)}, f32[2,12,128]{2,1,0:T(8,128)S(1)}, f32[2,12,128]{2,1,0:T(8,128)S(1)}, f32[2,12,128]{2,1,0:T(8,128)S(1)}, f32[2...) fusion(f32[2,12,128]{2,1,0:T(8,128)S(1)} %get-tuple-element.109, ...), kind=kLoop, calls=%fused_computation.277.clone.1 | loop fusion | flops 27104256 | bytes 344064 | tf_op jit(solution)/shard_map/while/body/eval_jaxpr/reduce_sum | solution.py:74
  382.1 7.8 %fusion.735 = (f32[2,12,128]{2,1,0:T(8,128)S(1)}, f32[2,12,128]{2,1,0:T(8,128)S(1)}, f32[2,12,128]{2,1,0:T(8,128)S(1)}, f32[2,12,128]{2,1,0:T(8,128)S(1)}, f32[2...) fusion(f32[2,12,128]{2,1,0:T(8,128)S(1)} %get-tuple-element.107, ...), kind=kLoop, calls=%fused_computation.269.clone.1 | loop fusion | flops 27104256 | bytes 344064 | tf_op jit(solution)/shard_map/while/body/eval_jaxpr/reduce_sum | solution.py:74
  389.9 7.8 %fusion.734 = (f32[2,12,128]{2,1,0:T(8,128)S(1)}, f32[2,12,128]{2,1,0:T(8,128)S(1)}, f32[2,12,128]{2,1,0:T(8,128)S(1)}, f32[2,12,128]{2,1,0:T(8,128)S(1)}, f32[2...) fusion(f32[2,12,128]{2,1,0:T(8,128)S(1)} %get-tuple-element.105, ...), kind=kLoop, calls=%fused_computation.261.clone.1 | loop fusion | flops 27104256 | bytes 344064 | tf_op jit(solution)/shard_map/while/body/eval_jaxpr/reduce_sum | solution.py:74
  397.8 7.8 %fusion.733 = (f32[2,12,128]{2,1,0:T(8,128)S(1)}, f32[2,12,128]{2,1,0:T(8,128)S(1)}, f32[2,12,128]{2,1,0:T(8,128)S(1)}, f32[2,12,128]{2,1,0:T(8,128)S(1)}, f32[2...) fusion(f32[2,12,128]{2,1,0:T(8,128)S(1)} %get-tuple-element.101, ...), kind=kLoop, calls=%fused_computation.253.clone.1 | loop fusion | flops 27104256 | bytes 344064 | tf_op jit(solution)/shard_map/while/body/eval_jaxpr/reduce_sum | solution.py:74
  405.6 7.8 %fusion.732 = (f32[2,12,128]{2,1,0:T(8,128)S(1)}, f32[2,12,128]{2,1,0:T(8,128)S(1)}, f32[2,12,128]{2,1,0:T(8,128)S(1)}, f32[2,12,128]{2,1,0:T(8,128)S(1)}, f32[2...) fusion(f32[2,12,128]{2,1,0:T(8,128)S(1)} %get-tuple-element.101, ...), kind=kLoop, calls=%fused_computation.245.clone.1 | loop fusion | flops 27104256 | bytes 344064 | tf_op jit(solution)/shard_map/while/body/eval_jaxpr/reduce_sum | solution.py:74
  (179 shorter events, 158.7 us)
Async XLA Ops:
  1.3 11.1 %collective-permute-start.8 = (f32[1,1,2,12]{3,2,1,0:T(2,128)S(1)}, f32[1,1,2,12]{3,2,1,0:T(2,128)S(1)}, u32[]{:S(2)}, u32[]{:S(2)}) collective-permute-start(f32[1,1,2,12]{3,2,1,0:T(2,128)S(1)} %get-tuple-element.717), channel_id=1, source_target_pairs={{0,8},{8,16},{16,24},{24,32},{32,40},{40,48},{48,56},{56,64},{64,7... | collective-permute-start | bytes 296 | tf_op jit(solution)/shard_map/ppermute | solution.py:21
  5.7 6.7 %collective-permute-start.9 = (f32[1,1,2,12]{3,2,1,0:T(2,128)S(1)}, f32[1,1,2,12]{3,2,1,0:T(2,128)S(1)}, u32[]{:S(2)}, u32[]{:S(2)}) collective-permute-start(f32[1,1,2,12]{3,2,1,0:T(2,128)S(1)} %get-tuple-element.717), channel_id=1, source_target_pairs={{8,0},{16,8},{24,16},{32,24},{40,32},{48,40},{56,48},{64,56},{72,6... | collective-permute-start | bytes 296 | tf_op jit(solution)/shard_map/ppermute | solution.py:22
  6.5 10.9 %collective-permute-start.12 = (f32[3,1,2,12,128]{4,3,2,1,0:T(8,128)S(1)}, f32[3,1,2,12,128]{4,3,2,1,0:T(8,128)S(1)}, u32[]{:S(2)}, u32[]{:S(2)}) collective-permute-start(f32[3,1,2,12,128]{4,3,2,1,0:T(8,128)S(1)} %copy.241), channel_id=1, source_target_pairs={{0,8},{8,16},{16,24},{24,32},{32,40},{40,48},{48,56},{56,64},{64,7... | collective-permute-start | bytes 110600 | tf_op jit(solution)/shard_map/ppermute | solution.py:21
  9.1 9.0 %collective-permute-start.13 = (f32[3,1,2,12,128]{4,3,2,1,0:T(8,128)S(1)}, f32[3,1,2,12,128]{4,3,2,1,0:T(8,128)S(1)}, u32[]{:S(2)}, u32[]{:S(2)}) collective-permute-start(f32[3,1,2,12,128]{4,3,2,1,0:T(8,128)S(1)} %copy.241), channel_id=1, source_target_pairs={{8,0},{16,8},{24,16},{32,24},{40,32},{48,40},{56,48},{64,56},{72,6... | collective-permute-start | bytes 110600 | tf_op jit(solution)/shard_map/ppermute | solution.py:22
  12.4 4.6 %collective-permute-start.10 = (f32[1,3,1,12]{3,2,1,0:T(1,128)S(1)}, f32[1,3,1,12]{3,2,1,0:T(1,128)S(1)}, u32[]{:S(2)}, u32[]{:S(2)}) collective-permute-start(f32[1,3,1,12]{3,2,1,0:T(1,128)S(1)} %get-tuple-element.714), channel_id=1, source_target_pairs={{0,1},{1,2},{2,3},{3,4},{4,5},{5,6},{6,7},{7,0},{8,9},{9,10},{10,1... | collective-permute-start | bytes 440 | tf_op jit(solution)/shard_map/ppermute | solution.py:21
  13.2 3.8 collective-permute-start.11
  17.4 0.8 copy-start
  18.2 5.5 %collective-permute-start.14 = (f32[3,3,1,12,128]{4,3,2,1,0:T(8,128)S(1)}, f32[3,3,1,12,128]{4,3,2,1,0:T(8,128)S(1)}, u32[]{:S(2)}, u32[]{:S(2)}) collective-permute-start(f32[3,3,1,12,128]{4,3,2,1,0:T(8,128)S(1)} %get-tuple-element.648), channel_id=1, source_target_pairs={{0,1},{1,2},{2,3},{3,4},{4,5},{5,6},{6,7},{7,0},{8,9},{9,10},{10,1... | collective-permute-start | bytes 165896 | tf_op jit(solution)/shard_map/ppermute | solution.py:21
  19.8 3.9 collective-permute-start.15
  52.4 8.6 %copy-start.1 = (f32[3,1,2,12,128]{4,2,3,1,0:T(2,128)S(1)}, f32[3,1,2,12,128]{4,2,3,1,0:T(2,128)}, u32[]{:S(2)}) copy-start(f32[3,1,2,12,128]{4,2,3,1,0:T(2,128)} %param.6) | copy-start | bytes 110596
  52.5 9.0 %collective-permute-start.16 = (f32[1,1,2,12,128]{4,3,2,1,0:T(8,128)S(1)}, f32[1,1,2,12,128]{4,3,2,1,0:T(8,128)S(1)}, u32[]{:S(2)}, u32[]{:S(2)}) collective-permute-start(f32[1,1,2,12,128]{4,3,2,1,0:T(8,128)S(1)} %fusion.670), channel_id=1, source_target_pairs={{0,8},{8,16},{16,24},{24,32},{32,40},{40,48},{48,56},{56,64},{64,7... | collective-permute-start | bytes 36872 | tf_op jit(solution)/shard_map/ppermute | solution.py:21
  55.8 5.9 %collective-permute-start.17 = (f32[1,1,2,12,128]{4,3,2,1,0:T(8,128)S(1)}, f32[1,1,2,12,128]{4,3,2,1,0:T(8,128)S(1)}, u32[]{:S(2)}, u32[]{:S(2)}) collective-permute-start(f32[1,1,2,12,128]{4,3,2,1,0:T(8,128)S(1)} %fusion.670), channel_id=1, source_target_pairs={{8,0},{16,8},{24,16},{32,24},{40,32},{48,40},{56,48},{64,56},{72,6... | collective-permute-start | bytes 36872 | tf_op jit(solution)/shard_map/ppermute | solution.py:22
  61.8 5.5 %collective-permute-start.18 = (f32[1,3,1,12,128]{4,3,2,1,0:T(8,128)S(1)}, f32[1,3,1,12,128]{4,3,2,1,0:T(8,128)S(1)}, u32[]{:S(2)}, u32[]{:S(2)}) collective-permute-start(f32[1,3,1,12,128]{4,3,2,1,0:T(8,128)S(1)} %get-tuple-element.701), channel_id=1, source_target_pairs={{0,1},{1,2},{2,3},{3,4},{4,5},{5,6},{6,7},{7,0},{8,9},{9,10},{10,1... | collective-permute-start | bytes 55304 | tf_op jit(solution)/shard_map/ppermute | solution.py:21
  63.1 4.2 %collective-permute-start.19 = (f32[1,3,1,12,128]{4,3,2,1,0:T(8,128)S(1)}, f32[1,3,1,12,128]{4,3,2,1,0:T(8,128)S(1)}, u32[]{:S(2)}, u32[]{:S(2)}) collective-permute-start(f32[1,3,1,12,128]{4,3,2,1,0:T(8,128)S(1)} %get-tuple-element.702), channel_id=1, source_target_pairs={{1,0},{2,1},{3,2},{4,3},{5,4},{6,5},{7,6},{0,7},{9,8},{10,9},{11,1... | collective-permute-start | bytes 55304 | tf_op jit(solution)/shard_map/ppermute | solution.py:22
  152.7 8.1 %collective-permute-start = (f32[3,1,2,12,128]{4,3,2,1,0:T(8,128)S(1)}, f32[3,1,2,12,128]{4,3,2,1,0:T(8,128)S(1)}, u32[]{:S(2)}, u32[]{:S(2)}) collective-permute-start(f32[3,1,2,12,128]{4,3,2,1,0:T(8,128)S(1)} %multiply_add_fusion.5), channel_id=1, source_target_pairs={{8,0},{16,8},{24,16},{32,24},{40,32},{48,40},{56,48},{64,56},{72,6... | collective-permute-start | bytes 110600 | tf_op jit(solution)/shard_map/while/body/eval_jaxpr/ppermute | solution.py:22
  159.9 5.8 %collective-permute-start.1 = (f32[3,1,2,12,128]{4,3,2,1,0:T(8,128)S(1)}, f32[3,1,2,12,128]{4,3,2,1,0:T(8,128)S(1)}, u32[]{:S(2)}, u32[]{:S(2)}) collective-permute-start(f32[3,1,2,12,128]{4,3,2,1,0:T(8,128)S(1)} %multiply_add_fusion.5), channel_id=1, source_target_pairs={{0,8},{8,16},{16,24},{24,32},{32,40},{40,48},{48,56},{56,64},{64,7... | collective-permute-start | bytes 110600 | tf_op jit(solution)/shard_map/while/body/eval_jaxpr/ppermute | solution.py:21
  165.8 5.7 %collective-permute-start.2 = (f32[3,3,1,12,128]{4,3,2,1,0:T(8,128)S(1)}, f32[3,3,1,12,128]{4,3,2,1,0:T(8,128)S(1)}, u32[]{:S(2)}, u32[]{:S(2)}) collective-permute-start(f32[3,3,1,12,128]{4,3,2,1,0:T(8,128)S(1)} %get-tuple-element.1012), channel_id=1, source_target_pairs={{0,1},{1,2},{2,3},{3,4},{4,5},{5,6},{6,7},{7,0},{8,9},{9,10},{10,1... | collective-permute-start | bytes 165896 | tf_op jit(solution)/shard_map/while/body/eval_jaxpr/ppermute | solution.py:21
  166.7 4.8 %collective-permute-start.3 = (f32[3,3,1,12,128]{4,3,2,1,0:T(8,128)S(1)}, f32[3,3,1,12,128]{4,3,2,1,0:T(8,128)S(1)}, u32[]{:S(2)}, u32[]{:S(2)}) collective-permute-start(f32[3,3,1,12,128]{4,3,2,1,0:T(8,128)S(1)} %get-tuple-element.1014), channel_id=1, source_target_pairs={{1,0},{2,1},{3,2},{4,3},{5,4},{6,5},{7,6},{0,7},{9,8},{10,9},{11,1... | collective-permute-start | bytes 165896 | tf_op jit(solution)/shard_map/while/body/eval_jaxpr/ppermute | solution.py:22
  200.2 9.3 %collective-permute-start.4 = (f32[1,1,2,12,128]{4,3,2,1,0:T(8,128)S(1)}, f32[1,1,2,12,128]{4,3,2,1,0:T(8,128)S(1)}, u32[]{:S(2)}, u32[]{:S(2)}) collective-permute-start(f32[1,1,2,12,128]{4,3,2,1,0:T(8,128)S(1)} %fusion.728), channel_id=1, source_target_pairs={{8,0},{16,8},{24,16},{32,24},{40,32},{48,40},{56,48},{64,56},{72,6... | collective-permute-start | bytes 36872 | tf_op jit(solution)/shard_map/while/body/eval_jaxpr/ppermute | solution.py:22
  208.7 1.2 collective-permute-start.5
  209.9 5.4 %collective-permute-start.7 = (f32[1,3,1,12,128]{4,3,2,1,0:T(8,128)S(1)}, f32[1,3,1,12,128]{4,3,2,1,0:T(8,128)S(1)}, u32[]{:S(2)}, u32[]{:S(2)}) collective-permute-start(f32[1,3,1,12,128]{4,3,2,1,0:T(8,128)S(1)} %get-tuple-element.1151), channel_id=1, source_target_pairs={{0,1},{1,2},{2,3},{3,4},{4,5},{5,6},{6,7},{7,0},{8,9},{9,10},{10,1... | collective-permute-start | bytes 55304 | tf_op jit(solution)/shard_map/while/body/eval_jaxpr/ppermute | solution.py:21
  210.0 5.4 %collective-permute-start.6 = (f32[1,3,1,12,128]{4,3,2,1,0:T(8,128)S(1)}, f32[1,3,1,12,128]{4,3,2,1,0:T(8,128)S(1)}, u32[]{:S(2)}, u32[]{:S(2)}) collective-permute-start(f32[1,3,1,12,128]{4,3,2,1,0:T(8,128)S(1)} %get-tuple-element.1150), channel_id=1, source_target_pairs={{1,0},{2,1},{3,2},{4,3},{5,4},{6,5},{7,6},{0,7},{9,8},{10,9},{11,1... | collective-permute-start | bytes 55304 | tf_op jit(solution)/shard_map/while/body/eval_jaxpr/ppermute | solution.py:22
  286.0 7.8 %collective-permute-start = (f32[3,1,2,12,128]{4,3,2,1,0:T(8,128)S(1)}, f32[3,1,2,12,128]{4,3,2,1,0:T(8,128)S(1)}, u32[]{:S(2)}, u32[]{:S(2)}) collective-permute-start(f32[3,1,2,12,128]{4,3,2,1,0:T(8,128)S(1)} %multiply_add_fusion.5), channel_id=1, source_target_pairs={{8,0},{16,8},{24,16},{32,24},{40,32},{48,40},{56,48},{64,56},{72,6... | collective-permute-start | bytes 110600 | tf_op jit(solution)/shard_map/while/body/eval_jaxpr/ppermute | solution.py:22
  292.9 1.2 collective-permute-start.1
  294.2 6.1 %collective-permute-start.2 = (f32[3,3,1,12,128]{4,3,2,1,0:T(8,128)S(1)}, f32[3,3,1,12,128]{4,3,2,1,0:T(8,128)S(1)}, u32[]{:S(2)}, u32[]{:S(2)}) collective-permute-start(f32[3,3,1,12,128]{4,3,2,1,0:T(8,128)S(1)} %get-tuple-element.1012), channel_id=1, source_target_pairs={{0,1},{1,2},{2,3},{3,4},{4,5},{5,6},{6,7},{7,0},{8,9},{9,10},{10,1... | collective-permute-start | bytes 165896 | tf_op jit(solution)/shard_map/while/body/eval_jaxpr/ppermute | solution.py:21
  294.3 6.0 %collective-permute-start.3 = (f32[3,3,1,12,128]{4,3,2,1,0:T(8,128)S(1)}, f32[3,3,1,12,128]{4,3,2,1,0:T(8,128)S(1)}, u32[]{:S(2)}, u32[]{:S(2)}) collective-permute-start(f32[3,3,1,12,128]{4,3,2,1,0:T(8,128)S(1)} %get-tuple-element.1014), channel_id=1, source_target_pairs={{1,0},{2,1},{3,2},{4,3},{5,4},{6,5},{7,6},{0,7},{9,8},{10,9},{11,1... | collective-permute-start | bytes 165896 | tf_op jit(solution)/shard_map/while/body/eval_jaxpr/ppermute | solution.py:22
  329.1 8.1 %collective-permute-start.4 = (f32[1,1,2,12,128]{4,3,2,1,0:T(8,128)S(1)}, f32[1,1,2,12,128]{4,3,2,1,0:T(8,128)S(1)}, u32[]{:S(2)}, u32[]{:S(2)}) collective-permute-start(f32[1,1,2,12,128]{4,3,2,1,0:T(8,128)S(1)} %fusion.728), channel_id=1, source_target_pairs={{8,0},{16,8},{24,16},{32,24},{40,32},{48,40},{56,48},{64,56},{72,6... | collective-permute-start | bytes 36872 | tf_op jit(solution)/shard_map/while/body/eval_jaxpr/ppermute | solution.py:22
  336.3 1.2 collective-permute-start.5
  337.5 5.5 %collective-permute-start.7 = (f32[1,3,1,12,128]{4,3,2,1,0:T(8,128)S(1)}, f32[1,3,1,12,128]{4,3,2,1,0:T(8,128)S(1)}, u32[]{:S(2)}, u32[]{:S(2)}) collective-permute-start(f32[1,3,1,12,128]{4,3,2,1,0:T(8,128)S(1)} %get-tuple-element.1151), channel_id=1, source_target_pairs={{0,1},{1,2},{2,3},{3,4},{4,5},{5,6},{6,7},{7,0},{8,9},{9,10},{10,1... | collective-permute-start | bytes 55304 | tf_op jit(solution)/shard_map/while/body/eval_jaxpr/ppermute | solution.py:21
  337.6 5.4 %collective-permute-start.6 = (f32[1,3,1,12,128]{4,3,2,1,0:T(8,128)S(1)}, f32[1,3,1,12,128]{4,3,2,1,0:T(8,128)S(1)}, u32[]{:S(2)}, u32[]{:S(2)}) collective-permute-start(f32[1,3,1,12,128]{4,3,2,1,0:T(8,128)S(1)} %get-tuple-element.1150), channel_id=1, source_target_pairs={{1,0},{2,1},{3,2},{4,3},{5,4},{6,5},{7,6},{0,7},{9,8},{10,9},{11,1... | collective-permute-start | bytes 55304 | tf_op jit(solution)/shard_map/while/body/eval_jaxpr/ppermute | solution.py:22
where the time goes:
time: 423 us; the launch traced here: 416 us
  other arithmetic  299 us (71%)
  starting transfers between devices  75.9 us (18%)
  waiting for transfers between devices  19.9 us (5%)
  loops' own time  15.4 us (4%)
  local copies, waits for them, and re-layouts  4.53 us (1%)
    reduce_sum x27, other arithmetic, force_pass(): jnp.sum(coupling * parts[component], axis=-1)  210 us
    reduce_sum x21, other arithmetic, density_pass(): running = running + jnp.sum(weights_mask * reach * reach, axis=-1)  85.1 us
    ppermute x14, starting transfers between devices, with_halo(): after = lax.ppermute(first, axis, down)  60.6 us
    ppermute x14, waiting for transfers between devices, with_halo(): before = lax.ppermute(last, axis, up)  16.5 us
    another operation x1, loops' own time, shards(): lax.fori_loop(0, STEPS, verlet_step, (positions, velocities, pushed))  15.4 us
    ppermute x14, starting transfers between devices, with_halo(): before = lax.ppermute(last, axis, up)  15.3 us
  transfers between devices with their start and end apart: 28, of which 17 were waited for; matrix products, arithmetic and copies ran while one was open for 1% of the time, Pallas kernels for 0%

commit v1 on v0

v1 whole, which is shorter than its diff:
```python
import functools

import jax
import jax.numpy as jnp
from jax import lax
from jax.experimental import pallas as pl
from jax.experimental.pallas import tpu as pltpu
from jax.sharding import PartitionSpec as P

STEPS = 2
TIME_STEP = 0.05
DENSITY_SCALE = 0.0625
FAR = 1000.0

NZ = 12
SLOTS = 128
KF = 48
COLUMNS = 12
FIRST = (0, 3)
NEAR = 9
CHUNK = 16


def split3(value):
    high = value.astype(jnp.bfloat16).astype(jnp.float32)
    rest = value - high
    middle = rest.astype(jnp.bfloat16).astype(jnp.float32)
    return high, middle, rest - middle


def stacked(values):
    row = lax.broadcasted_iota(jnp.int32, (8, SLOTS), 0)
    result = jnp.zeros((8, SLOTS), jnp.float32)
    for k, value in enumerate(values):
        result = jnp.where(row == k, value, result)
    return result


def cell_rows(ref, p, jy, c):
    return [
        jnp.broadcast_to(ref[k, p, jy, pl.ds(c, 1), :], (8, SLOTS)) for k in range(3)
    ]


def build_features(ext_ref, slope_ref, near_bf, exact, own_bf):
    def per_cell(c, carry):
        for jy in range(4):
            for p in range(3):
                x, y, z = cell_rows(ext_ref, p, jy, c)
                x, y, z = x + (p - 1.5), y + float(jy - 1), z - 0.5
                norm = 1.0 - (x * x + y * y + z * z)
                high, middle, low = split3(stacked([x, y, z, norm, 1.0]))
                features = jnp.concatenate([high, high, middle, middle, high, low], axis=0)
                place = (jy * 3 + p) * SLOTS
                near_bf[c, :, place : place + SLOTS] = features.astype(jnp.bfloat16)
                if exact is not None:
                    slope = jnp.broadcast_to(0.5 * slope_ref[p, jy, pl.ds(c, 1), :], (8, SLOTS))
                    exact[c, jy * 3 + p] = stacked([x, y, z, slope])
        for iy in range(2):
            x, y, z = cell_rows(ext_ref, 1, iy + 1, c)
            x, y = x - 0.5, y + float(iy)
            for r in range(3):
                zr = z - (r - 0.5)
                norm = -(x * x + y * y + zr * zr)
                high, middle, low = split3(stacked([2.0 * x, 2.0 * y, 2.0 * zr, 1.0, norm]))
                features = jnp.concatenate([high, middle, high, middle, low, high], axis=0)
                own_bf[c, iy, r] = features.T.astype(jnp.bfloat16)
        return carry

    lax.fori_loop(0, NZ, per_cell, 0)


def slab_of(c, r):
    return lax.rem(c + (r + NZ - 1), NZ)


def density_kernel(ext_ref, slope_ref, near_bf, own_bf):
    build_features(ext_ref, None, near_bf, None, own_bf)

    def per_cell(c, carry):
        for iy in range(2):
            total = jnp.zeros((SLOTS, SLOTS), jnp.float32)
            for r in range(3):
                slab = slab_of(c, r)
                own = own_bf[c, iy, r]
                for at in range(0, NEAR, 2):
                    width = min(2, NEAR - at)
                    place = (FIRST[iy] + at) * SLOTS
                    near = near_bf[slab, :, place : place + width * SLOTS]
                    reach = jnp.maximum(
                        jnp.dot(own, near, preferred_element_type=jnp.float32), 0.0
                    )
                    square = reach * reach
                    for k in range(width):
                        total = total + square[:, k * SLOTS : (k + 1) * SLOTS]
            density = DENSITY_SCALE * (jnp.sum(total.T, axis=0, keepdims=True) - 1.0)
            slope_ref[iy, pl.ds(c, 1), :] = -0.5 * lax.rsqrt(1.0 + jnp.maximum(density, 0.0))
        return carry

    lax.fori_loop(0, NZ, per_cell, 0)


def force_kernel(
    ext_ref, slope_ref, force_ref, near_bf, exact, own_bf, reach_a, reach_b, sums
):
    build_features(ext_ref, slope_ref, near_bf, exact, own_bf)
    reaches = (reach_a, reach_b)

    def reach_of(c, iy, r, at, width):
        place = (FIRST[iy] + at) * SLOTS
        near = near_bf[slab_of(c, r), :, place : place + width * SLOTS]
        place = (r * NEAR + at) * SLOTS
        reaches[iy][:, place : place + width * SLOTS] = jnp.maximum(
            jnp.dot(own_bf[c, iy, r], near, preferred_element_type=jnp.float32), 0.0
        )

    tiles = [(r, at, min(2, NEAR - at)) for r in range(3) for at in range(0, NEAR, 2)]
    for tile in tiles:
        reach_of(0, 0, *tile)

    def per_cell(c, carry):
        for iy in range(2):
            ahead = [(c, 1)] if iy == 0 else [(lax.rem(c + 1, NZ), 0)]
            slope_own = jnp.broadcast_to(
                0.5 * slope_ref[1, iy + 1, pl.ds(c, 1), :], (SLOTS, SLOTS)
            ).T
            step = 0
            pending = list(tiles)
            for start in range(0, SLOTS, CHUNK):
                shape = (CHUNK, SLOTS)
                total = [jnp.zeros(shape, jnp.float32) for _ in range(4)]
                slope_i = slope_own[start : start + CHUNK]
                for r in range(3):
                    slab = slab_of(c, r)
                    weight = jnp.zeros(shape, jnp.float32)
                    for at in range(NEAR):
                        if step % 14 == 0 and pending:
                            reach_of(*ahead[0], *pending.pop(0))
                        step += 1
                        x, y, z, slope = (
                            jnp.broadcast_to(exact[slab, FIRST[iy] + at, k : k + 1, :], shape)
                            for k in range(4)
                        )
                        place = (r * NEAR + at) * SLOTS
                        w = reaches[iy][start : start + CHUNK, place : place + SLOTS]
                        coupling = w * ((w * w + slope) + slope_i)
                        weight = weight + coupling
                        total[0] = total[0] + coupling * x
                        total[1] = total[1] + coupling * y
                        total[2] = total[2] + coupling * z
                    total[3] = total[3] + weight
                    if r != 1:
                        total[2] = total[2] + float(r - 1) * weight
                for k in range(4):
                    sums[k, start : start + CHUNK, :] = total[k]
            assert not pending
            folded = [jnp.sum(sums[k].T, axis=0, keepdims=True) for k in range(4)]
            own = (
                ext_ref[0, 1, iy + 1, pl.ds(c, 1), :] - 0.5,
                ext_ref[1, 1, iy + 1, pl.ds(c, 1), :] + float(iy),
                ext_ref[2, 1, iy + 1, pl.ds(c, 1), :] - 0.5,
            )
            for k in range(3):
                force_ref[k, iy, pl.ds(c, 1), :] = -0.5 * (folded[k] - own[k] * folded[3])
        return carry

    lax.fori_loop(0, NZ, per_cell, 0)


VMEM = pl.BlockSpec(memory_space=pltpu.VMEM)
FEATURES = [
    pltpu.VMEM((NZ, KF, COLUMNS * SLOTS), jnp.bfloat16),
    pltpu.VMEM((NZ, 2, 3, SLOTS, KF), jnp.bfloat16),
]


def density_call(ext):
    return pl.pallas_call(
        density_kernel,
        out_shape=jax.ShapeDtypeStruct((2, NZ, SLOTS), jnp.float32),
        in_specs=[VMEM],
        out_specs=VMEM,
        scratch_shapes=FEATURES,
        compiler_params=pltpu.CompilerParams(vmem_limit_bytes=40 * 2**20),
        cost_estimate=pl.CostEstimate(flops=10**9, bytes_accessed=10**6, transcendentals=0),
    )(ext)


def force_call(ext, slope_ext):
    reach = pltpu.VMEM((SLOTS, 3 * NEAR * SLOTS), jnp.float32)
    return pl.pallas_call(
        force_kernel,
        out_shape=jax.ShapeDtypeStruct((3, 2, NZ, SLOTS), jnp.float32),
        in_specs=[VMEM, VMEM],
        out_specs=VMEM,
        scratch_shapes=[
            FEATURES[0],
            pltpu.VMEM((NZ, COLUMNS, 8, SLOTS), jnp.float32),
            FEATURES[1],
            reach,
            reach,
            pltpu.VMEM((4, SLOTS, SLOTS), jnp.float32),
        ],
        compiler_params=pltpu.CompilerParams(vmem_limit_bytes=40 * 2**20),
        cost_estimate=pl.CostEstimate(flops=10**9, bytes_accessed=10**6, transcendentals=0),
    )(ext, slope_ext)


def swap(value, axis, odd):
    n = lax.axis_size(axis)
    partner = [(i + 1 if i % 2 == odd else i - 1) % n for i in range(n)]
    return lax.ppermute(value, axis, [(i, partner[i]) for i in range(n)])


def with_halo(value):
    even = lax.axis_index("gy") % 2 == 0
    first, last = value[..., :1, :, :], value[..., 1:, :, :]
    near = swap(jnp.where(even, last, first), "gy", 0)
    far = swap(jnp.where(even, first, last), "gy", 1)
    below, above = jnp.where(even, far, near), jnp.where(even, near, far)
    row = jnp.concatenate([below, value, above], axis=-3)
    even = lax.axis_index("gx") % 2 == 0
    near = swap(row, "gx", 0)
    far = swap(row, "gx", 1)
    before, after = jnp.where(even, far, near), jnp.where(even, near, far)
    return jnp.stack([before, row, after], axis=-4)


def shards(positions, velocities, counts):
    positions, velocities = positions[:, 0], velocities[:, 0]
    places = lax.broadcasted_iota(jnp.int32, (2, NZ, SLOTS), 2)
    present = (places < counts[0][..., None])[None]

    def forces_of(positions):
        ext = with_halo(jnp.where(present, positions, FAR))
        slope = density_call(ext)
        return jnp.where(present, force_call(ext, with_halo(slope)), 0.0)

    pushed = forces_of(positions)
    for _ in range(STEPS):
        velocities = velocities + 0.5 * TIME_STEP * pushed
        positions = positions + TIME_STEP * velocities
        pushed = forces_of(positions)
        velocities = velocities + 0.5 * TIME_STEP * pushed
    return (positions[:, None], velocities[:, None], pushed[:, None])


def solution(mesh):
    in_specs = (
        P(None, "gx", "gy", None, None),
        P(None, "gx", "gy", None, None),
        P("gx", "gy", None),
    )
    out_specs = (P(None, "gx", "gy", None, None),) * 3
    return jax.shard_map(shards, mesh=mesh, in_specs=in_specs, out_specs=out_specs, check_vma=False)
```

time: 423 us -> 193 us (0.46); the launches traced: 416 us -> 193 us
  other arithmetic: 299 us -> 1.25 us
  Pallas kernels: 0 us -> 100 us
  starting transfers between devices: 75.9 us -> 42 us
  waiting for transfers between devices: 19.9 us -> 46.2 us
  loops' own time: 15.4 us -> 0 us
    reduce_sum x48 -> x0, other arithmetic: 296 us -> none  [the longest x27 210 us: force_pass(): jnp.sum(coupling * parts[component], axis=-1)]
    pallas_call x0 -> x6, Pallas kernels: none -> 100 us  [the longest x3 68.5 us: force_call(): pl.pallas_call(force_kernel, out_shape=jax.ShapeDtypeStruct((3, 2, NZ, SL...]
    ppermute x28 -> x24, starting transfers between devices: 75.9 us -> 42 us  [swap(): return lax.ppermute(value, axis, [(i, partner[i]) for i in range(n)])]
    ppermute x28 -> x24, waiting for transfers between devices: 19.9 us -> 46.2 us  [swap(): return lax.ppermute(value, axis, [(i, partner[i]) for i in range(n)])]
    another operation x1 -> x0, loops' own time: 15.4 us -> none  [shards(): lax.fori_loop(0, STEPS, verlet_step, (positions, velocities, pushed))]
  transfers between devices with their start and end apart: 28 -> 24, of which waited for: 17 -> 18; matrix products, arithmetic and copies ran while one was open for 1% -> 0% of each run, Pallas kernels for 0% -> 0%
where the time goes in v1:
time: 193 us
  Pallas kernels  100 us (52%)
  waiting for transfers between devices  46.2 us (24%)
  starting transfers between devices  42 us (22%)
  local copies, waits for them, and re-layouts  2.63 us (1%)
    pallas_call x3, Pallas kernels, force_call(): pl.pallas_call(force_kernel, out_shape=jax.ShapeDtypeStruct((3, 2, NZ, SL...  68.5 us
    ppermute x24, waiting for transfers between devices, swap(): return lax.ppermute(value, axis, [(i, partner[i]) for i in range(n)])  46.2 us
    ppermute x24, starting transfers between devices, swap(): return lax.ppermute(value, axis, [(i, partner[i]) for i in range(n)])  42 us
    pallas_call x3, Pallas kernels, density_call(): pl.pallas_call(density_kernel, out_shape=jax.ShapeDtypeStruct((2, NZ, SLO...  31.6 us
  transfers between devices with their start and end apart: 24, of which 18 were waited for; matrix products, arithmetic and copies ran while one was open for 0% of the time, Pallas kernels for 0%

profile of v1, /device:TPU:1, one launch (start us, length us, event | category | flops | bytes accessed | tf_op | source)
XLA Modules:
  0.0 193.1 jit_solution(17735322273890298525)
XLA Ops:
  2.2 5.0 %collective-permute-start = (f32[3,1,12,128]{3,2,1,0:T(8,128)S(1)}, f32[3,1,12,128]{3,2,1,0:T(8,128)S(1)}, u32[]{:S(2)}, u32[]{:S(2)}) collective-permute-start(f32[3,1,12,128]{3,2,1,0:T(8,128)S(1)} %get-tuple-element.38), channel_id=1, source_target_pairs={{0,7},{1,2},{2,1},{3,4},{4,3},{5,6},{6,5},{7,0},{8,15},{9,10},{10,... | collective-permute-start | bytes 55304 | tf_op jit(solution)/shard_map/ppermute | solution.py:212
  7.2 1.2 collective-permute-done
  8.4 1.8 collective-permute-done.1
  10.2 1.9 collective-permute-start.3
  12.1 3.0 %collective-permute-start.2 = (f32[3,4,12,128]{3,2,1,0:T(8,128)S(1)}, f32[3,4,12,128]{3,2,1,0:T(8,128)S(1)}, u32[]{:S(2)}, u32[]{:S(2)}) collective-permute-start(f32[3,4,12,128]{3,2,1,0:T(8,128)S(1)} %get-tuple-element.19), channel_id=1, source_target_pairs={{0,248},{8,16},{16,8},{24,32},{32,24},{40,48},{48,40},{56,64},{64,... | collective-permute-start | bytes 221192 | tf_op jit(solution)/shard_map/ppermute | solution.py:212
  15.1 3.0 %collective-permute-done.2 = f32[3,4,12,128]{3,2,1,0:T(8,128)S(1)} collective-permute-done((f32[3,4,12,128]{3,2,1,0:T(8,128)S(1)}, f32[3,4,12,128]{3,2,1,0:T(8,128)S(1)}, u32[]{:S(2)}, u32[]{:S(2)}) %collective-permute-start.2) | collective-permute-done | bytes 73760 | tf_op jit(solution)/shard_map/ppermute | solution.py:212
  18.2 10.5 %shard_map.58 = f32[2,12,128]{2,1,0:T(8,128)S(1)} custom-call(f32[3,3,4,12,128]{4,3,2,1,0:T(8,128)S(1)} %copy.9.ext_ref), custom_call_target="tpu_custom_call" | custom-call | flops 1000000000 | bytes 1000000 | tf_op jit(solution)/shard_map/pallas_call | solution.py:178
  28.7 1.2 collective-permute-start.4
  29.9 3.5 %collective-permute-done.4 = f32[1,12,128]{2,1,0:T(8,128)S(1)} collective-permute-done((f32[1,12,128]{2,1,0:T(8,128)S(1)}, f32[1,12,128]{2,1,0:T(8,128)S(1)}, u32[]{:S(2)}, u32[]{:S(2)}) %collective-permute-start.4) | collective-permute-done | bytes 6176 | tf_op jit(solution)/shard_map/ppermute | solution.py:212
  33.5 6.3 %collective-permute-start.7 = (f32[4,12,128]{2,1,0:T(8,128)S(1)}, f32[4,12,128]{2,1,0:T(8,128)S(1)}, u32[]{:S(2)}, u32[]{:S(2)}) collective-permute-start(f32[4,12,128]{2,1,0:T(8,128)S(1)} %get-tuple-element.45), channel_id=1, source_target_pairs={{0,8},{8,0},{16,24},{24,16},{32,40},{40,32},{48,56},{56,48},{64,72... | collective-permute-start | bytes 73736 | tf_op jit(solution)/shard_map/ppermute | solution.py:212
  40.6 3.4 %collective-permute-done.6 = f32[4,12,128]{2,1,0:T(8,128)S(1)} collective-permute-done((f32[4,12,128]{2,1,0:T(8,128)S(1)}, f32[4,12,128]{2,1,0:T(8,128)S(1)}, u32[]{:S(2)}, u32[]{:S(2)}) %collective-permute-start.6) | collective-permute-done | bytes 24608 | tf_op jit(solution)/shard_map/ppermute | solution.py:212
  44.0 22.9 %shard_map.59 = f32[3,2,12,128]{3,2,1,0:T(8,128)S(1)} custom-call(f32[3,3,4,12,128]{4,3,2,1,0:T(8,128)S(1)} %copy.9.ext_ref, f32[3,4,12,128]{3,2,1,0:T(8,128)S(1)} %pad_maximum_fusion.4.slope_ref), custom_call_target="tpu_custom_call" | custom-call | flops 1000000000 | bytes 1000000 | tf_op jit(solution)/shard_map/pallas_call | solution.py:191
  67.0 1.8 collective-permute-start.8
  68.8 3.1 %collective-permute-done.8 = f32[3,1,12,128]{3,2,1,0:T(8,128)S(1)} collective-permute-done((f32[3,1,12,128]{3,2,1,0:T(8,128)S(1)}, f32[3,1,12,128]{3,2,1,0:T(8,128)S(1)}, u32[]{:S(2)}, u32[]{:S(2)}) %collective-permute-start.8) | collective-permute-done | bytes 18464 | tf_op jit(solution)/shard_map/ppermute | solution.py:212
  71.9 4.6 %collective-permute-start.11 = (f32[3,4,12,128]{3,2,1,0:T(8,128)S(1)}, f32[3,4,12,128]{3,2,1,0:T(8,128)S(1)}, u32[]{:S(2)}, u32[]{:S(2)}) collective-permute-start(f32[3,4,12,128]{3,2,1,0:T(8,128)S(1)} %get-tuple-element.17), channel_id=1, source_target_pairs={{0,8},{8,0},{16,24},{24,16},{32,40},{40,32},{48,56},{56,48},{64,72... | collective-permute-start | bytes 221192 | tf_op jit(solution)/shard_map/ppermute | solution.py:212
  77.4 4.8 %collective-permute-done.10 = f32[3,4,12,128]{3,2,1,0:T(8,128)S(1)} collective-permute-done((f32[3,4,12,128]{3,2,1,0:T(8,128)S(1)}, f32[3,4,12,128]{3,2,1,0:T(8,128)S(1)}, u32[]{:S(2)}, u32[]{:S(2)}) %collective-permute-start.10) | collective-permute-done | bytes 73760 | tf_op jit(solution)/shard_map/ppermute | solution.py:212
  82.3 10.5 %shard_map.60 = f32[2,12,128]{2,1,0:T(8,128)S(1)} custom-call(f32[3,3,4,12,128]{4,3,2,1,0:T(8,128)S(1)} %copy.11.ext_ref), custom_call_target="tpu_custom_call" | custom-call | flops 1000000000 | bytes 1000000 | tf_op jit(solution)/shard_map/pallas_call | solution.py:178
  92.8 1.1 collective-permute-start.12
  93.9 3.6 %collective-permute-done.12 = f32[1,12,128]{2,1,0:T(8,128)S(1)} collective-permute-done((f32[1,12,128]{2,1,0:T(8,128)S(1)}, f32[1,12,128]{2,1,0:T(8,128)S(1)}, u32[]{:S(2)}, u32[]{:S(2)}) %collective-permute-start.12) | collective-permute-done | bytes 6176 | tf_op jit(solution)/shard_map/ppermute | solution.py:212
  97.6 4.8 %collective-permute-start.15 = (f32[4,12,128]{2,1,0:T(8,128)S(1)}, f32[4,12,128]{2,1,0:T(8,128)S(1)}, u32[]{:S(2)}, u32[]{:S(2)}) collective-permute-start(f32[4,12,128]{2,1,0:T(8,128)S(1)} %get-tuple-element.43), channel_id=1, source_target_pairs={{0,8},{8,0},{16,24},{24,16},{32,40},{40,32},{48,56},{56,48},{64,72... | collective-permute-start | bytes 73736 | tf_op jit(solution)/shard_map/ppermute | solution.py:212
  103.2 3.4 %collective-permute-done.14 = f32[4,12,128]{2,1,0:T(8,128)S(1)} collective-permute-done((f32[4,12,128]{2,1,0:T(8,128)S(1)}, f32[4,12,128]{2,1,0:T(8,128)S(1)}, u32[]{:S(2)}, u32[]{:S(2)}) %collective-permute-start.14) | collective-permute-done | bytes 24608 | tf_op jit(solution)/shard_map/ppermute | solution.py:212
  106.6 22.8 %shard_map.61 = f32[3,2,12,128]{3,2,1,0:T(8,128)S(1)} custom-call(f32[3,3,4,12,128]{4,3,2,1,0:T(8,128)S(1)} %copy.11.ext_ref, f32[3,4,12,128]{3,2,1,0:T(8,128)S(1)} %pad_maximum_fusion.6.slope_ref), custom_call_target="tpu_custom_call" | custom-call | flops 1000000000 | bytes 1000000 | tf_op jit(solution)/shard_map/pallas_call | solution.py:191
  129.5 1.9 %collective-permute-start.16 = (f32[3,1,12,128]{3,2,1,0:T(8,128)S(1)}, f32[3,1,12,128]{3,2,1,0:T(8,128)S(1)}, u32[]{:S(2)}, u32[]{:S(2)}) collective-permute-start(f32[3,1,12,128]{3,2,1,0:T(8,128)S(1)} %get-tuple-element.30), channel_id=1, source_target_pairs={{0,7},{1,2},{2,1},{3,4},{4,3},{5,6},{6,5},{7,0},{8,15},{9,10},{10,... | collective-permute-start | bytes 55304 | tf_op jit(solution)/shard_map/ppermute | solution.py:212
  131.4 2.9 %collective-permute-done.16 = f32[3,1,12,128]{3,2,1,0:T(8,128)S(1)} collective-permute-done((f32[3,1,12,128]{3,2,1,0:T(8,128)S(1)}, f32[3,1,12,128]{3,2,1,0:T(8,128)S(1)}, u32[]{:S(2)}, u32[]{:S(2)}) %collective-permute-start.16) | collective-permute-done | bytes 18464 | tf_op jit(solution)/shard_map/ppermute | solution.py:212
  134.4 4.7 %collective-permute-start.19 = (f32[3,4,12,128]{3,2,1,0:T(8,128)S(1)}, f32[3,4,12,128]{3,2,1,0:T(8,128)S(1)}, u32[]{:S(2)}, u32[]{:S(2)}) collective-permute-start(f32[3,4,12,128]{3,2,1,0:T(8,128)S(1)} %get-tuple-element.15), channel_id=1, source_target_pairs={{0,8},{8,0},{16,24},{24,16},{32,40},{40,32},{48,56},{56,48},{64,72... | collective-permute-start | bytes 221192 | tf_op jit(solution)/shard_map/ppermute | solution.py:212
  140.0 4.7 %collective-permute-done.18 = f32[3,4,12,128]{3,2,1,0:T(8,128)S(1)} collective-permute-done((f32[3,4,12,128]{3,2,1,0:T(8,128)S(1)}, f32[3,4,12,128]{3,2,1,0:T(8,128)S(1)}, u32[]{:S(2)}, u32[]{:S(2)}) %collective-permute-start.18) | collective-permute-done | bytes 73760 | tf_op jit(solution)/shard_map/ppermute | solution.py:212
  144.8 10.5 %shard_map.62 = f32[2,12,128]{2,1,0:T(8,128)S(1)} custom-call(f32[3,3,4,12,128]{4,3,2,1,0:T(8,128)S(1)} %pad_maximum_fusion.2.ext_ref), custom_call_target="tpu_custom_call" | custom-call | flops 1000000000 | bytes 1000000 | tf_op jit(solution)/shard_map/pallas_call | solution.py:178
  155.4 1.2 collective-permute-start.20
  156.5 3.5 %collective-permute-done.20 = f32[1,12,128]{2,1,0:T(8,128)S(1)} collective-permute-done((f32[1,12,128]{2,1,0:T(8,128)S(1)}, f32[1,12,128]{2,1,0:T(8,128)S(1)}, u32[]{:S(2)}, u32[]{:S(2)}) %collective-permute-start.20) | collective-permute-done | bytes 6176 | tf_op jit(solution)/shard_map/ppermute | solution.py:212
  160.1 4.6 %collective-permute-start.23 = (f32[4,12,128]{2,1,0:T(8,128)S(1)}, f32[4,12,128]{2,1,0:T(8,128)S(1)}, u32[]{:S(2)}, u32[]{:S(2)}) collective-permute-start(f32[4,12,128]{2,1,0:T(8,128)S(1)} %get-tuple-element.41), channel_id=1, source_target_pairs={{0,8},{8,0},{16,24},{24,16},{32,40},{40,32},{48,56},{56,48},{64,72... | collective-permute-start | bytes 73736 | tf_op jit(solution)/shard_map/ppermute | solution.py:212
  165.5 3.4 %collective-permute-done.22 = f32[4,12,128]{2,1,0:T(8,128)S(1)} collective-permute-done((f32[4,12,128]{2,1,0:T(8,128)S(1)}, f32[4,12,128]{2,1,0:T(8,128)S(1)}, u32[]{:S(2)}, u32[]{:S(2)}) %collective-permute-start.22) | collective-permute-done | bytes 24608 | tf_op jit(solution)/shard_map/ppermute | solution.py:212
  168.9 22.8 %shard_map.63 = f32[3,2,12,128]{3,2,1,0:T(8,128)S(1)} custom-call(f32[3,3,4,12,128]{4,3,2,1,0:T(8,128)S(1)} %pad_maximum_fusion.2.ext_ref, f32[3,4,12,128]{3,2,1,0:T(8,128)S(1)} %pad_maximum_fusion.8.slope_ref), custom_call_target="tpu_custom_call" | custom-call | flops 1000000000 | bytes 1000000 | tf_op jit(solution)/shard_map/pallas_call | solution.py:191
  (68 shorter events, 7.7 us)
Async XLA Ops:
  0.6 0.7 copy-start.2
  2.2 6.2 %collective-permute-start = (f32[3,1,12,128]{3,2,1,0:T(8,128)S(1)}, f32[3,1,12,128]{3,2,1,0:T(8,128)S(1)}, u32[]{:S(2)}, u32[]{:S(2)}) collective-permute-start(f32[3,1,12,128]{3,2,1,0:T(8,128)S(1)} %get-tuple-element.38), channel_id=1, source_target_pairs={{0,7},{1,2},{2,1},{3,4},{4,3},{5,6},{6,5},{7,0},{8,15},{9,10},{10,... | collective-permute-start | bytes 55304 | tf_op jit(solution)/shard_map/ppermute | solution.py:212
  7.2 3.0 %collective-permute-start.1 = (f32[3,1,12,128]{3,2,1,0:T(8,128)S(1)}, f32[3,1,12,128]{3,2,1,0:T(8,128)S(1)}, u32[]{:S(2)}, u32[]{:S(2)}) collective-permute-start(f32[3,1,12,128]{3,2,1,0:T(8,128)S(1)} %get-tuple-element.39), channel_id=1, source_target_pairs={{0,1},{1,0},{2,3},{3,2},{4,5},{5,4},{6,7},{7,6},{8,9},{9,8},{10,11... | collective-permute-start | bytes 55304 | tf_op jit(solution)/shard_map/ppermute | solution.py:212
  10.2 4.9 %collective-permute-start.3 = (f32[3,4,12,128]{3,2,1,0:T(8,128)S(1)}, f32[3,4,12,128]{3,2,1,0:T(8,128)S(1)}, u32[]{:S(2)}, u32[]{:S(2)}) collective-permute-start(f32[3,4,12,128]{3,2,1,0:T(8,128)S(1)} %get-tuple-element.19), channel_id=1, source_target_pairs={{0,8},{8,0},{16,24},{24,16},{32,40},{40,32},{48,56},{56,48},{64,72... | collective-permute-start | bytes 221192 | tf_op jit(solution)/shard_map/ppermute | solution.py:212
  12.1 6.0 %collective-permute-start.2 = (f32[3,4,12,128]{3,2,1,0:T(8,128)S(1)}, f32[3,4,12,128]{3,2,1,0:T(8,128)S(1)}, u32[]{:S(2)}, u32[]{:S(2)}) collective-permute-start(f32[3,4,12,128]{3,2,1,0:T(8,128)S(1)} %get-tuple-element.19), channel_id=1, source_target_pairs={{0,248},{8,16},{16,8},{24,32},{32,24},{40,48},{48,40},{56,64},{64,... | collective-permute-start | bytes 221192 | tf_op jit(solution)/shard_map/ppermute | solution.py:212
  28.7 4.7 %collective-permute-start.4 = (f32[1,12,128]{2,1,0:T(8,128)S(1)}, f32[1,12,128]{2,1,0:T(8,128)S(1)}, u32[]{:S(2)}, u32[]{:S(2)}) collective-permute-start(f32[1,12,128]{2,1,0:T(8,128)S(1)} %get-tuple-element.56), channel_id=1, source_target_pairs={{0,7},{1,2},{2,1},{3,4},{4,3},{5,6},{6,5},{7,0},{8,15},{9,10},{10,... | collective-permute-start | bytes 18440 | tf_op jit(solution)/shard_map/ppermute | solution.py:212
  29.9 3.5 %collective-permute-start.5 = (f32[1,12,128]{2,1,0:T(8,128)S(1)}, f32[1,12,128]{2,1,0:T(8,128)S(1)}, u32[]{:S(2)}, u32[]{:S(2)}) collective-permute-start(f32[1,12,128]{2,1,0:T(8,128)S(1)} %get-tuple-element.57), channel_id=1, source_target_pairs={{0,1},{1,0},{2,3},{3,2},{4,5},{5,4},{6,7},{7,6},{8,9},{9,8},{10,11... | collective-permute-start | bytes 18440 | tf_op jit(solution)/shard_map/ppermute | solution.py:212
  33.5 7.1 %collective-permute-start.7 = (f32[4,12,128]{2,1,0:T(8,128)S(1)}, f32[4,12,128]{2,1,0:T(8,128)S(1)}, u32[]{:S(2)}, u32[]{:S(2)}) collective-permute-start(f32[4,12,128]{2,1,0:T(8,128)S(1)} %get-tuple-element.45), channel_id=1, source_target_pairs={{0,8},{8,0},{16,24},{24,16},{32,40},{40,32},{48,56},{56,48},{64,72... | collective-permute-start | bytes 73736 | tf_op jit(solution)/shard_map/ppermute | solution.py:212
  39.7 4.2 %collective-permute-start.6 = (f32[4,12,128]{2,1,0:T(8,128)S(1)}, f32[4,12,128]{2,1,0:T(8,128)S(1)}, u32[]{:S(2)}, u32[]{:S(2)}) collective-permute-start(f32[4,12,128]{2,1,0:T(8,128)S(1)} %get-tuple-element.45), channel_id=1, source_target_pairs={{0,248},{8,16},{16,8},{24,32},{32,24},{40,48},{48,40},{56,64},{64,... | collective-permute-start | bytes 73736 | tf_op jit(solution)/shard_map/ppermute | solution.py:212
  44.0 22.9 %copy-start = (f32[3,1,2,12,128]{4,2,3,1,0:T(2,128)S(1)}, f32[3,1,2,12,128]{4,2,3,1,0:T(2,128)}, u32[]{:S(2)}) copy-start(f32[3,1,2,12,128]{4,2,3,1,0:T(2,128)} %param.4) | copy-start | bytes 110596
  44.0 22.9 %copy-start.1 = (f32[3,1,2,12,128]{4,2,3,1,0:T(2,128)S(1)}, f32[3,1,2,12,128]{4,2,3,1,0:T(2,128)}, u32[]{:S(2)}) copy-start(f32[3,1,2,12,128]{4,2,3,1,0:T(2,128)} %param.3) | copy-start | bytes 110596
  67.0 4.9 %collective-permute-start.8 = (f32[3,1,12,128]{3,2,1,0:T(8,128)S(1)}, f32[3,1,12,128]{3,2,1,0:T(8,128)S(1)}, u32[]{:S(2)}, u32[]{:S(2)}) collective-permute-start(f32[3,1,12,128]{3,2,1,0:T(8,128)S(1)} %get-tuple-element.34), channel_id=1, source_target_pairs={{0,7},{1,2},{2,1},{3,4},{4,3},{5,6},{6,5},{7,0},{8,15},{9,10},{10,... | collective-permute-start | bytes 55304 | tf_op jit(solution)/shard_map/ppermute | solution.py:212
  68.8 3.1 %collective-permute-start.9 = (f32[3,1,12,128]{3,2,1,0:T(8,128)S(1)}, f32[3,1,12,128]{3,2,1,0:T(8,128)S(1)}, u32[]{:S(2)}, u32[]{:S(2)}) collective-permute-start(f32[3,1,12,128]{3,2,1,0:T(8,128)S(1)} %get-tuple-element.35), channel_id=1, source_target_pairs={{0,1},{1,0},{2,3},{3,2},{4,5},{5,4},{6,7},{7,6},{8,9},{9,8},{10,11... | collective-permute-start | bytes 55304 | tf_op jit(solution)/shard_map/ppermute | solution.py:212
  71.9 5.6 %collective-permute-start.11 = (f32[3,4,12,128]{3,2,1,0:T(8,128)S(1)}, f32[3,4,12,128]{3,2,1,0:T(8,128)S(1)}, u32[]{:S(2)}, u32[]{:S(2)}) collective-permute-start(f32[3,4,12,128]{3,2,1,0:T(8,128)S(1)} %get-tuple-element.17), channel_id=1, source_target_pairs={{0,8},{8,0},{16,24},{24,16},{32,40},{40,32},{48,56},{56,48},{64,72... | collective-permute-start | bytes 221192 | tf_op jit(solution)/shard_map/ppermute | solution.py:212
  76.5 5.7 %collective-permute-start.10 = (f32[3,4,12,128]{3,2,1,0:T(8,128)S(1)}, f32[3,4,12,128]{3,2,1,0:T(8,128)S(1)}, u32[]{:S(2)}, u32[]{:S(2)}) collective-permute-start(f32[3,4,12,128]{3,2,1,0:T(8,128)S(1)} %get-tuple-element.17), channel_id=1, source_target_pairs={{0,248},{8,16},{16,8},{24,32},{32,24},{40,48},{48,40},{56,64},{64,... | collective-permute-start | bytes 221192 | tf_op jit(solution)/shard_map/ppermute | solution.py:212
  92.8 4.7 %collective-permute-start.12 = (f32[1,12,128]{2,1,0:T(8,128)S(1)}, f32[1,12,128]{2,1,0:T(8,128)S(1)}, u32[]{:S(2)}, u32[]{:S(2)}) collective-permute-start(f32[1,12,128]{2,1,0:T(8,128)S(1)} %get-tuple-element.52), channel_id=1, source_target_pairs={{0,7},{1,2},{2,1},{3,4},{4,3},{5,6},{6,5},{7,0},{8,15},{9,10},{10,... | collective-permute-start | bytes 18440 | tf_op jit(solution)/shard_map/ppermute | solution.py:212
  93.9 3.6 %collective-permute-start.13 = (f32[1,12,128]{2,1,0:T(8,128)S(1)}, f32[1,12,128]{2,1,0:T(8,128)S(1)}, u32[]{:S(2)}, u32[]{:S(2)}) collective-permute-start(f32[1,12,128]{2,1,0:T(8,128)S(1)} %get-tuple-element.53), channel_id=1, source_target_pairs={{0,1},{1,0},{2,3},{3,2},{4,5},{5,4},{6,7},{7,6},{8,9},{9,8},{10,11... | collective-permute-start | bytes 18440 | tf_op jit(solution)/shard_map/ppermute | solution.py:212
  97.6 5.6 %collective-permute-start.15 = (f32[4,12,128]{2,1,0:T(8,128)S(1)}, f32[4,12,128]{2,1,0:T(8,128)S(1)}, u32[]{:S(2)}, u32[]{:S(2)}) collective-permute-start(f32[4,12,128]{2,1,0:T(8,128)S(1)} %get-tuple-element.43), channel_id=1, source_target_pairs={{0,8},{8,0},{16,24},{24,16},{32,40},{40,32},{48,56},{56,48},{64,72... | collective-permute-start | bytes 73736 | tf_op jit(solution)/shard_map/ppermute | solution.py:212
  102.3 4.2 %collective-permute-start.14 = (f32[4,12,128]{2,1,0:T(8,128)S(1)}, f32[4,12,128]{2,1,0:T(8,128)S(1)}, u32[]{:S(2)}, u32[]{:S(2)}) collective-permute-start(f32[4,12,128]{2,1,0:T(8,128)S(1)} %get-tuple-element.43), channel_id=1, source_target_pairs={{0,248},{8,16},{16,8},{24,32},{32,24},{40,48},{48,40},{56,64},{64,... | collective-permute-start | bytes 73736 | tf_op jit(solution)/shard_map/ppermute | solution.py:212
  129.5 4.9 %collective-permute-start.16 = (f32[3,1,12,128]{3,2,1,0:T(8,128)S(1)}, f32[3,1,12,128]{3,2,1,0:T(8,128)S(1)}, u32[]{:S(2)}, u32[]{:S(2)}) collective-permute-start(f32[3,1,12,128]{3,2,1,0:T(8,128)S(1)} %get-tuple-element.30), channel_id=1, source_target_pairs={{0,7},{1,2},{2,1},{3,4},{4,3},{5,6},{6,5},{7,0},{8,15},{9,10},{10,... | collective-permute-start | bytes 55304 | tf_op jit(solution)/shard_map/ppermute | solution.py:212
  131.4 2.9 %collective-permute-start.17 = (f32[3,1,12,128]{3,2,1,0:T(8,128)S(1)}, f32[3,1,12,128]{3,2,1,0:T(8,128)S(1)}, u32[]{:S(2)}, u32[]{:S(2)}) collective-permute-start(f32[3,1,12,128]{3,2,1,0:T(8,128)S(1)} %get-tuple-element.31), channel_id=1, source_target_pairs={{0,1},{1,0},{2,3},{3,2},{4,5},{5,4},{6,7},{7,6},{8,9},{9,8},{10,11... | collective-permute-start | bytes 55304 | tf_op jit(solution)/shard_map/ppermute | solution.py:212
  134.4 5.6 %collective-permute-start.19 = (f32[3,4,12,128]{3,2,1,0:T(8,128)S(1)}, f32[3,4,12,128]{3,2,1,0:T(8,128)S(1)}, u32[]{:S(2)}, u32[]{:S(2)}) collective-permute-start(f32[3,4,12,128]{3,2,1,0:T(8,128)S(1)} %get-tuple-element.15), channel_id=1, source_target_pairs={{0,8},{8,0},{16,24},{24,16},{32,40},{40,32},{48,56},{56,48},{64,72... | collective-permute-start | bytes 221192 | tf_op jit(solution)/shard_map/ppermute | solution.py:212
  139.1 5.7 %collective-permute-start.18 = (f32[3,4,12,128]{3,2,1,0:T(8,128)S(1)}, f32[3,4,12,128]{3,2,1,0:T(8,128)S(1)}, u32[]{:S(2)}, u32[]{:S(2)}) collective-permute-start(f32[3,4,12,128]{3,2,1,0:T(8,128)S(1)} %get-tuple-element.15), channel_id=1, source_target_pairs={{0,248},{8,16},{16,8},{24,32},{32,24},{40,48},{48,40},{56,64},{64,... | collective-permute-start | bytes 221192 | tf_op jit(solution)/shard_map/ppermute | solution.py:212
  155.4 4.7 %collective-permute-start.20 = (f32[1,12,128]{2,1,0:T(8,128)S(1)}, f32[1,12,128]{2,1,0:T(8,128)S(1)}, u32[]{:S(2)}, u32[]{:S(2)}) collective-permute-start(f32[1,12,128]{2,1,0:T(8,128)S(1)} %get-tuple-element.48), channel_id=1, source_target_pairs={{0,7},{1,2},{2,1},{3,4},{4,3},{5,6},{6,5},{7,0},{8,15},{9,10},{10,... | collective-permute-start | bytes 18440 | tf_op jit(solution)/shard_map/ppermute | solution.py:212
  156.5 3.5 %collective-permute-start.21 = (f32[1,12,128]{2,1,0:T(8,128)S(1)}, f32[1,12,128]{2,1,0:T(8,128)S(1)}, u32[]{:S(2)}, u32[]{:S(2)}) collective-permute-start(f32[1,12,128]{2,1,0:T(8,128)S(1)} %get-tuple-element.49), channel_id=1, source_target_pairs={{0,1},{1,0},{2,3},{3,2},{4,5},{5,4},{6,7},{7,6},{8,9},{9,8},{10,11... | collective-permute-start | bytes 18440 | tf_op jit(solution)/shard_map/ppermute | solution.py:212
  160.1 5.4 %collective-permute-start.23 = (f32[4,12,128]{2,1,0:T(8,128)S(1)}, f32[4,12,128]{2,1,0:T(8,128)S(1)}, u32[]{:S(2)}, u32[]{:S(2)}) collective-permute-start(f32[4,12,128]{2,1,0:T(8,128)S(1)} %get-tuple-element.41), channel_id=1, source_target_pairs={{0,8},{8,0},{16,24},{24,16},{32,40},{40,32},{48,56},{56,48},{64,72... | collective-permute-start | bytes 73736 | tf_op jit(solution)/shard_map/ppermute | solution.py:212
  164.7 4.2 %collective-permute-start.22 = (f32[4,12,128]{2,1,0:T(8,128)S(1)}, f32[4,12,128]{2,1,0:T(8,128)S(1)}, u32[]{:S(2)}, u32[]{:S(2)}) collective-permute-start(f32[4,12,128]{2,1,0:T(8,128)S(1)} %get-tuple-element.41), channel_id=1, source_target_pairs={{0,248},{8,16},{16,8},{24,32},{32,24},{40,48},{48,40},{56,64},{64,... | collective-permute-start | bytes 73736 | tf_op jit(solution)/shard_map/ppermute | solution.py:212

commit v2 on v1

v2 whole, which is shorter than its diff:
```python
import functools

import jax
import jax.numpy as jnp
from jax import lax
from jax.experimental import pallas as pl
from jax.experimental.pallas import tpu as pltpu
from jax.sharding import PartitionSpec as P

STEPS = 2
TIME_STEP = 0.05
DENSITY_SCALE = 0.0625
FAR = 1000.0

NZ = 12
SLOTS = 128
KF = 48
CHUNK = 16
UNROLL = 2
INNER = ((0, 4), (0, 4))
MIDDLE = ((0, 2), (0, 2))
OUTER = ((0, 3), (3, 6))


def split3(value):
    high = value.astype(jnp.bfloat16).astype(jnp.float32)
    rest = value - high
    middle = rest.astype(jnp.bfloat16).astype(jnp.float32)
    return high, middle, rest - middle


def stacked(values):
    row = lax.broadcasted_iota(jnp.int32, (8, SLOTS), 0)
    result = jnp.zeros((8, SLOTS), jnp.float32)
    for k, value in enumerate(values):
        result = jnp.where(row == k, value, result)
    return result


def rows_of(ref, column, c):
    return [
        jnp.broadcast_to(ref[k, column, pl.ds(c, 1), :], (8, SLOTS)) for k in range(3)
    ]


def build_near(near_ref, near_bf):
    def per_cell(c, carry):
        for column in range(near_ref.shape[1]):
            x, y, z = rows_of(near_ref, column, c)
            norm = 1.0 - (x * x + y * y + z * z)
            high, middle, low = split3(stacked([x, y, z, norm, 1.0]))
            features = jnp.concatenate([high, high, middle, middle, high, low], axis=0)
            place = column * SLOTS
            near_bf[c, :, place : place + SLOTS] = features.astype(jnp.bfloat16)
        return carry

    lax.fori_loop(0, NZ, per_cell, 0, unroll=2)


def build_own(own_ref, own_bf):
    def per_cell(c, carry):
        for iy in range(2):
            x, y, z = rows_of(own_ref, iy, c)
            for r in range(3):
                zr = z - float(r - 1)
                norm = -(x * x + y * y + zr * zr)
                high, middle, low = split3(stacked([2.0 * x, 2.0 * y, 2.0 * zr, 1.0, norm]))
                features = jnp.concatenate([high, middle, high, middle, low, high], axis=0)
                own_bf[c, iy, r] = features.T.astype(jnp.bfloat16)
        return carry

    lax.fori_loop(0, NZ, per_cell, 0, unroll=2)


def slab_of(c, r):
    return lax.rem(c + (r + NZ - 1), NZ)


def density_kernel(spans, fresh, own_ref, near_ref, sum_ref, near_bf, *refs):
    if fresh:
        own_bf, totals_a, totals_b = refs
        build_own(own_ref, own_bf)
    else:
        own_bf = own_ref
        totals_a, totals_b = refs
    build_near(near_ref, near_bf)
    totals = (totals_a, totals_b)

    def fold(c, iy):
        sum_ref[iy, pl.ds(c, 1), :] = jnp.sum(totals[iy][...].T, axis=0, keepdims=True)

    def per_cell(c, carry):
        for iy in range(2):
            if iy == 0:
                fold(jnp.maximum(c - 1, 0), 1)
            else:
                fold(c, 0)
            first, last = spans[iy]
            total = jnp.zeros((SLOTS, SLOTS), jnp.float32)
            for r in range(3):
                slab = slab_of(c, r)
                own = own_bf[c, iy, r]
                for at in range(first, last, 2):
                    width = min(2, last - at)
                    near = near_bf[slab, :, at * SLOTS : (at + width) * SLOTS]
                    reach = jnp.maximum(
                        jnp.dot(own, near, preferred_element_type=jnp.float32), 0.0
                    )
                    square = reach * reach
                    for k in range(width):
                        total = total + square[:, k * SLOTS : (k + 1) * SLOTS]
            totals[iy][...] = total
        return carry

    totals_b[...] = jnp.zeros((SLOTS, SLOTS), jnp.float32)
    lax.fori_loop(0, NZ, per_cell, 0, unroll=UNROLL)
    fold(NZ - 1, 1)


def force_kernel(spans, fresh, own_ref, near_ref, own_bf, near_bf, own_slope_ref, *refs):
    if fresh:
        near_slope_ref, force_ref, slope_own, reach_a, reach_b, sums_a, sums_b = refs

        def turn(c, carry):
            for iy in range(2):
                slope_own[c, iy] = jnp.broadcast_to(
                    own_slope_ref[iy, pl.ds(c, 1), :], (SLOTS, SLOTS)
                ).T
            return carry

        lax.fori_loop(0, NZ, turn, 0, unroll=3)
    else:
        slope_own = own_slope_ref
        near_slope_ref, force_ref, reach_a, reach_b, sums_a, sums_b = refs
    reaches = (reach_a, reach_b)
    sums = (sums_a, sums_b)

    def reach_of(c, iy, r, at, width):
        first, last = spans[iy]
        near = near_bf[slab_of(c, r), :, (first + at) * SLOTS : (first + at + width) * SLOTS]
        place = (r * (last - first) + at) * SLOTS
        reaches[iy][:, place : place + width * SLOTS] = jnp.maximum(
            jnp.dot(own_bf[c, iy, r], near, preferred_element_type=jnp.float32), 0.0
        )

    def fold(c, iy):
        folded = [jnp.sum(sums[iy][k].T, axis=0, keepdims=True) for k in range(4)]
        for k in range(3):
            own = own_ref[k, iy, pl.ds(c, 1), :]
            force_ref[k, iy, pl.ds(c, 1), :] = -0.5 * (folded[k] - own * folded[3])

    count = spans[0][1] - spans[0][0]
    tiles = [(r, at, min(2, count - at)) for r in range(3) for at in range(0, count, 2)]
    for tile in tiles:
        reach_of(0, 0, *tile)
    steps = (SLOTS // CHUNK) * 3 * count
    every = max(1, (steps * 3 // 4) // len(tiles))

    def per_cell(c, carry):
        for iy in range(2):
            if iy == 0:
                fold(jnp.maximum(c - 1, 0), 1)
            else:
                fold(c, 0)
            ahead = (c, 1) if iy == 0 else (lax.rem(c + 1, NZ), 0)
            step = 0
            pending = list(tiles)
            first, last = spans[iy]
            for start in range(0, SLOTS, CHUNK):
                shape = (CHUNK, SLOTS)
                total = [jnp.zeros(shape, jnp.float32) for _ in range(4)]
                slope_i = slope_own[c, iy, start : start + CHUNK, :]
                for r in range(3):
                    slab = slab_of(c, r)
                    weight = jnp.zeros(shape, jnp.float32)
                    for at in range(first, last):
                        if step % every == 0 and pending:
                            reach_of(*ahead, *pending.pop(0))
                        step += 1
                        x, y, z = (
                            jnp.broadcast_to(near_ref[k, at, pl.ds(slab, 1), :], shape)
                            for k in range(3)
                        )
                        slope = jnp.broadcast_to(near_slope_ref[at, pl.ds(slab, 1), :], shape)
                        place = (r * count + at - first) * SLOTS
                        w = reaches[iy][start : start + CHUNK, place : place + SLOTS]
                        coupling = w * ((w * w + slope) + slope_i)
                        weight = weight + coupling
                        total[0] = total[0] + coupling * x
                        total[1] = total[1] + coupling * y
                        total[2] = total[2] + coupling * z
                    total[3] = total[3] + weight
                    if r != 1:
                        total[2] = total[2] + float(r - 1) * weight
                for k in range(4):
                    sums[iy][k, start : start + CHUNK, :] = total[k]
            assert not pending
        return carry

    sums_b[...] = jnp.zeros((4, SLOTS, SLOTS), jnp.float32)
    lax.fori_loop(0, NZ, per_cell, 0)
    fold(NZ - 1, 1)


VMEM = pl.BlockSpec(memory_space=pltpu.VMEM)
SQUARE = pltpu.VMEM((SLOTS, SLOTS), jnp.float32)
OWN_FEATURES = jax.ShapeDtypeStruct((NZ, 2, 3, SLOTS, KF), jnp.bfloat16)
OWN_SLOPES = jax.ShapeDtypeStruct((NZ, 2, SLOTS, SLOTS), jnp.float32)


def call(kernel, out_shape, scratch, *operands):
    return pl.pallas_call(
        kernel,
        out_shape=out_shape,
        in_specs=[VMEM] * len(operands),
        out_specs=jax.tree.map(lambda _: VMEM, out_shape),
        scratch_shapes=scratch,
        compiler_params=pltpu.CompilerParams(vmem_limit_bytes=32 * 2**20),
        cost_estimate=pl.CostEstimate(flops=10**9, bytes_accessed=10**6, transcendentals=0),
    )(*operands)


def density_part(own, near, spans):
    fresh = own.dtype == jnp.float32
    out_shape = [
        jax.ShapeDtypeStruct((2, NZ, SLOTS), jnp.float32),
        jax.ShapeDtypeStruct((NZ, KF, near.shape[1] * SLOTS), jnp.bfloat16),
    ]
    if fresh:
        out_shape.append(OWN_FEATURES)
    kernel = functools.partial(density_kernel, spans, fresh)
    return call(kernel, out_shape, [SQUARE, SQUARE], own, near)


def force_part(own, near, own_bf, near_bf, own_slope, near_slope, spans):
    fresh = own_slope.ndim == 3
    out_shape = [jax.ShapeDtypeStruct((3, 2, NZ, SLOTS), jnp.float32)]
    if fresh:
        out_shape.append(OWN_SLOPES)
    count = spans[0][1] - spans[0][0]
    reach = pltpu.VMEM((SLOTS, 3 * count * SLOTS), jnp.float32)
    sums = pltpu.VMEM((4, SLOTS, SLOTS), jnp.float32)
    kernel = functools.partial(force_kernel, spans, fresh)
    return call(
        kernel,
        out_shape,
        [reach, reach, sums, sums],
        own,
        near,
        own_bf,
        near_bf,
        own_slope,
        near_slope,
    )


def swap(value, axis, odd):
    n = lax.axis_size(axis)
    partner = [(i + 1 if i % 2 == odd else i - 1) % n for i in range(n)]
    return lax.ppermute(value, axis, [(i, partner[i]) for i in range(n)])


def along(component, amount):
    unit = [0.0, 0.0, 0.0]
    unit[component] = 1.0
    return jnp.array(unit, jnp.float32).reshape(3, 1, 1, 1) * amount


def exchange_x(value):
    return swap(value, "gx", 0), swap(value, "gx", 1)


def exchange_y(value):
    even = lax.axis_index("gy") % 2 == 0
    first, last = value
    near = swap(jnp.where(even, last, first), "gy", 0)
    far = swap(jnp.where(even, first, last), "gy", 1)
    return near, far


def below_above(received):
    even = lax.axis_index("gy") % 2 == 0
    near, far = received
    return jnp.where(even, far, near), jnp.where(even, near, far)


def rows_along_y(*blocks):
    return [jnp.stack([block[..., iy, :, :] for block in blocks], axis=-3) for iy in range(2)]


def shards(positions, velocities, counts):
    positions, velocities = positions[:, 0], velocities[:, 0]
    places = lax.broadcasted_iota(jnp.int32, (2, NZ, SLOTS), 2)
    present = (places < counts[0][..., None])[None]
    frame = jnp.stack(
        [
            jnp.full((2, 1, 1), -0.5, jnp.float32),
            jnp.array([-1.0, 0.0], jnp.float32).reshape(2, 1, 1),
            jnp.full((2, 1, 1), -0.5, jnp.float32),
        ]
    )
    side = jnp.where(lax.axis_index("gx") % 2 == 0, 1.0, -1.0)

    def forces_of(positions):
        own = jnp.where(present, positions + frame, FAR)
        near, far = exchange_x(own)
        near = near + along(0, side)
        inner = jnp.concatenate([own, near], axis=1)
        square, inner_bf, own_bf = density_part(own, inner, INNER)
        square, far = lax.optimization_barrier((square, far))
        far = far - along(0, side)
        received = exchange_y(rows_along_y(own, near, far))
        part, far_bf = density_part(own_bf, far, MIDDLE)
        part, received = lax.optimization_barrier((part, received))
        below, above = below_above(received)
        outer = jnp.concatenate([below - along(1, 2.0), above + along(1, 2.0)], axis=1)
        last, outer_bf = density_part(own_bf, outer, OUTER)
        density = DENSITY_SCALE * jnp.maximum(square + part + last - 1.0, 0.0)
        slope = -0.25 * lax.rsqrt(1.0 + density)
        near_slope, far_slope = exchange_x(slope)
        inner_slope = jnp.concatenate([slope, near_slope], axis=0)
        force, turned = force_part(own, inner, own_bf, inner_bf, slope, inner_slope, INNER)
        force, far_slope = lax.optimization_barrier((force, far_slope))
        received = exchange_y(rows_along_y(slope, near_slope, far_slope))
        (part,) = force_part(own, far, own_bf, far_bf, turned, far_slope, MIDDLE)
        part, received = lax.optimization_barrier((part, received))
        outer_slope = jnp.concatenate(below_above(received), axis=0)
        (last,) = force_part(own, outer, own_bf, outer_bf, turned, outer_slope, OUTER)
        force = force + part + last
        return jnp.where(present, force, 0.0)

    pushed = forces_of(positions)
    for _ in range(STEPS):
        velocities = velocities + 0.5 * TIME_STEP * pushed
        positions = positions + TIME_STEP * velocities
        pushed = forces_of(positions)
        velocities = velocities + 0.5 * TIME_STEP * pushed
    return (positions[:, None], velocities[:, None], pushed[:, None])


def solution(mesh):
    in_specs = (
        P(None, "gx", "gy", None, None),
        P(None, "gx", "gy", None, None),
        P("gx", "gy", None),
    )
    out_specs = (P(None, "gx", "gy", None, None),) * 3
    return jax.shard_map(shards, mesh=mesh, in_specs=in_specs, out_specs=out_specs, check_vma=False)
```

time: 193 us -> 153 us (0.79)
  waiting for transfers between devices: 46.2 us -> 5.6 us
  starting transfers between devices: 42 us -> 39.3 us
  other arithmetic: 1.25 us -> 3.38 us
  Pallas kernels: 100 us -> 102 us
    ppermute x24, waiting for transfers between devices: 46.2 us -> 5.6 us  [swap(): return lax.ppermute(value, axis, [(i, partner[i]) for i in range(n)])]
    ppermute x24, starting transfers between devices: 42 us -> 39.3 us  [swap(): return lax.ppermute(value, axis, [(i, partner[i]) for i in range(n)])]
    pallas_call x6 -> x18, Pallas kernels: 100 us -> 102 us  [call(): pl.pallas_call(kernel, out_shape=out_shape, in_specs=[VMEM] * len(operand...]
  transfers between devices with their start and end apart: 24 -> 24, of which waited for: 18 -> 8; matrix products, arithmetic and copies ran while one was open for 0% -> 1% of each run, Pallas kernels for 0% -> 45%
where the time goes in v2:
time: 153 us
  Pallas kernels  102 us (67%)
  starting transfers between devices  39.3 us (26%)
  waiting for transfers between devices  5.6 us (4%)
  other arithmetic  3.38 us (2%)
  local copies, waits for them, and re-layouts  2.02 us (1%)
    pallas_call x18, Pallas kernels, call(): pl.pallas_call(kernel, out_shape=out_shape, in_specs=[VMEM] * len(operand...  102 us
    ppermute x24, starting transfers between devices, swap(): return lax.ppermute(value, axis, [(i, partner[i]) for i in range(n)])  39.3 us
    ppermute x24, waiting for transfers between devices, swap(): return lax.ppermute(value, axis, [(i, partner[i]) for i in range(n)])  5.6 us
  transfers between devices with their start and end apart: 24, of which 8 were waited for; matrix products, arithmetic and copies ran while one was open for 1% of the time, Pallas kernels for 45%

profile of v2, /device:TPU:1, one launch (start us, length us, event | category | flops | bytes accessed | tf_op | source)
XLA Modules:
  0.0 153.3 jit_solution(5457099462908550214)
XLA Ops:
  2.2 3.2 %collective-permute-start = (f32[3,2,12,128]{3,2,1,0:T(8,128)S(1)}, f32[3,2,12,128]{3,2,1,0:T(8,128)S(1)}, u32[]{:S(2)}, u32[]{:S(2)}) collective-permute-start(f32[3,2,12,128]{3,2,1,0:T(8,128)S(1)} %fusion.6.own_ref), channel_id=1, source_target_pairs={{0,8},{8,0},{16,24},{24,16},{32,40},{40,32},{48,56},{56,48},{64,72... | collective-permute-start | bytes 110600 | tf_op jit(solution)/shard_map/ppermute | solution.py:260
  5.5 1.3 collective-permute-start.1
  7.5 4.7 %shard_map.175 = (f32[2,12,128]{2,1,0:T(8,128)S(1)}, bf16[12,48,512]{2,1,0:T(8,128)(2,1)S(1)}, bf16[12,2,3,128,48]{4,3,2,1,0:T(8,128)(2,1)S(1)}) custom-call(f32[3,2,12,128]{3,2,1,0:T(8,128)S(1)} %fusion.6.own_ref, f32[3,4,12,128]{3,2,1,0:T(8,128)S(1)} %pad_maximum_fusion.3.near_ref), custom_call_target="tpu_custom_call" | custom-call | flops 1000000000 | bytes 1000000 | tf_op jit(solution)/shard_map/pallas_call | solution.py:212
  12.4 1.7 %collective-permute-start.2 = (f32[3,3,12,128]{3,2,1,0:T(8,128)S(1)}, f32[3,3,12,128]{3,2,1,0:T(8,128)S(1)}, u32[]{:S(2)}, u32[]{:S(2)}) collective-permute-start(f32[3,3,12,128]{3,2,1,0:T(8,128)S(1)} %get-tuple-element.137), channel_id=1, source_target_pairs={{0,1},{1,0},{2,3},{3,2},{4,5},{5,4},{6,7},{7,6},{8,9},{9,8},{10,11... | collective-permute-start | bytes 165896 | tf_op jit(solution)/shard_map/ppermute | solution.py:260
  14.1 2.6 %collective-permute-start.3 = (f32[3,3,12,128]{3,2,1,0:T(8,128)S(1)}, f32[3,3,12,128]{3,2,1,0:T(8,128)S(1)}, u32[]{:S(2)}, u32[]{:S(2)}) collective-permute-start(f32[3,3,12,128]{3,2,1,0:T(8,128)S(1)} %get-tuple-element.136), channel_id=1, source_target_pairs={{0,7},{1,2},{2,1},{3,4},{4,3},{5,6},{6,5},{7,0},{8,15},{9,10},{10,... | collective-permute-start | bytes 165896 | tf_op jit(solution)/shard_map/ppermute | solution.py:260
  16.6 2.5 %shard_map.176 = (f32[2,12,128]{2,1,0:T(8,128)S(1)}, bf16[12,48,256]{2,1,0:T(8,128)(2,1)S(1)}) custom-call(bf16[12,2,3,128,48]{4,3,2,1,0:T(8,128)(2,1)S(1)} %get-tuple-element.60.own_ref.own_bf, f32[3,2,12,128]{3,2,1,0:T(8,128)S(1)} %broadcast_subtract_fusion.2.near_ref), custom_call_target="tpu_custom_call" | custom-call | flops 1000000000 | bytes 1000000 | tf_op jit(solution)/shard_map/pallas_call | solution.py:212
  19.5 3.1 %shard_map.177 = (f32[2,12,128]{2,1,0:T(8,128)S(1)}, bf16[12,48,768]{2,1,0:T(8,128)(2,1)S(1)}) custom-call(bf16[12,2,3,128,48]{4,3,2,1,0:T(8,128)(2,1)S(1)} %get-tuple-element.60.own_ref.own_bf, f32[3,6,12,128]{3,2,1,0:T(8,128)S(1)} %pad_maximum_fusion.near_ref), custom_call_target="tpu_custom_call" | custom-call | flops 1000000000 | bytes 1000000 | tf_op jit(solution)/shard_map/pallas_call | solution.py:212
  22.6 6.4 %collective-permute-start.4 = (f32[2,12,128]{2,1,0:T(8,128)S(1)}, f32[2,12,128]{2,1,0:T(8,128)S(1)}, u32[]{:S(2)}, u32[]{:S(2)}) collective-permute-start(f32[2,12,128]{2,1,0:T(8,128)S(1)} %rsqrt_multiply_fusion.2.own_slope_ref), channel_id=1, source_target_pairs={{0,8},{8,0},{16,24},{24,16},{32,40},{40,32},{48,56},{56,48},{64,72... | collective-permute-start | bytes 36872 | tf_op jit(solution)/shard_map/ppermute | solution.py:260
  29.9 10.6 %shard_map.178 = (f32[3,2,12,128]{3,2,1,0:T(8,128)S(1)}, f32[12,2,128,128]{3,2,1,0:T(8,128)S(1)}) custom-call(f32[3,2,12,128]{3,2,1,0:T(8,128)S(1)} %fusion.6.own_ref, f32[3,4,12,128]{3,2,1,0:T(8,128)S(1)} %pad_maximum_fusion.3.near_ref, bf16[12,2,3,128,48]{4,3,2,1,0:T(8,128)(2,1)S(1)} %get-tuple-element.60.own_ref.own_bf, ...), custom_call_target="tpu_custom_call" | custom-call | flops 1000000000 | bytes 1000000 | tf_op jit(solution)/shard_map/pallas_call | solution.py:212
  40.6 3.1 %collective-permute-start.7 = (f32[3,12,128]{2,1,0:T(8,128)S(1)}, f32[3,12,128]{2,1,0:T(8,128)S(1)}, u32[]{:S(2)}, u32[]{:S(2)}) collective-permute-start(f32[3,12,128]{2,1,0:T(8,128)S(1)} %get-tuple-element.161), channel_id=1, source_target_pairs={{0,7},{1,2},{2,1},{3,4},{4,3},{5,6},{6,5},{7,0},{8,15},{9,10},{10,... | collective-permute-start | bytes 55304 | tf_op jit(solution)/shard_map/ppermute | solution.py:260
  43.7 5.3 %shard_map.179 = f32[3,2,12,128]{3,2,1,0:T(8,128)S(1)} custom-call(f32[3,2,12,128]{3,2,1,0:T(8,128)S(1)} %fusion.6.own_ref, f32[3,2,12,128]{3,2,1,0:T(8,128)S(1)} %broadcast_subtract_fusion.2.near_ref, bf16[12,2,3,128,48]{4,3,2,1,0:T(8,128)(2,1)S(1)} %get-tuple-element.60.own_ref.own_bf, bf16[12,48,256]{2,1,0:T(8,128)(2,1)S(1)} %get-tuple-element.72.near_bf, ...), custom_call_target="tpu_custom_call" | custom-call | flops 1000000000 | bytes 1000000 | tf_op jit(solution)/shard_map/pallas_call | solution.py:212
  49.1 7.7 %shard_map.180 = f32[3,2,12,128]{3,2,1,0:T(8,128)S(1)} custom-call(f32[3,2,12,128]{3,2,1,0:T(8,128)S(1)} %fusion.6.own_ref, f32[3,6,12,128]{3,2,1,0:T(8,128)S(1)} %pad_maximum_fusion.near_ref, bf16[12,2,3,128,48]{4,3,2,1,0:T(8,128)(2,1)S(1)} %get-tuple-element.60.own_ref.own_bf, bf16[12,48,768]{2,1,0:T(8,128)(2,1)S(1)} %get-tuple-element.76.near_bf, ...), custom_call_target="tpu_custom_call" | custom-call | flops 1000000000 | bytes 1000000 | tf_op jit(solution)/shard_map/pallas_call | solution.py:212
  56.9 1.8 %collective-permute-start.8 = (f32[3,2,12,128]{3,2,1,0:T(8,128)S(1)}, f32[3,2,12,128]{3,2,1,0:T(8,128)S(1)}, u32[]{:S(2)}, u32[]{:S(2)}) collective-permute-start(f32[3,2,12,128]{3,2,1,0:T(8,128)S(1)} %get-tuple-element.124.own_ref), channel_id=1, source_target_pairs={{0,8},{8,0},{16,24},{24,16},{32,40},{40,32},{48,56},{56,48},{64,72... | collective-permute-start | bytes 110600 | tf_op jit(solution)/shard_map/ppermute | solution.py:260
  59.7 4.7 %shard_map.181 = (f32[2,12,128]{2,1,0:T(8,128)S(1)}, bf16[12,48,512]{2,1,0:T(8,128)(2,1)S(1)}, bf16[12,2,3,128,48]{4,3,2,1,0:T(8,128)(2,1)S(1)}) custom-call(f32[3,2,12,128]{3,2,1,0:T(8,128)S(1)} %get-tuple-element.124.own_ref, f32[3,4,12,128]{3,2,1,0:T(8,128)S(1)} %pad_maximum_fusion.4.near_ref), custom_call_target="tpu_custom_call" | custom-call | flops 1000000000 | bytes 1000000 | tf_op jit(solution)/shard_map/pallas_call | solution.py:212
  64.6 1.5 collective-permute-start.11
  66.1 2.5 %shard_map.182 = (f32[2,12,128]{2,1,0:T(8,128)S(1)}, bf16[12,48,256]{2,1,0:T(8,128)(2,1)S(1)}) custom-call(bf16[12,2,3,128,48]{4,3,2,1,0:T(8,128)(2,1)S(1)} %get-tuple-element.79.own_ref.own_bf, f32[3,2,12,128]{3,2,1,0:T(8,128)S(1)} %broadcast_subtract_fusion.1.near_ref), custom_call_target="tpu_custom_call" | custom-call | flops 1000000000 | bytes 1000000 | tf_op jit(solution)/shard_map/pallas_call | solution.py:212
  68.7 1.6 %collective-permute-done.11 = f32[3,3,12,128]{3,2,1,0:T(8,128)S(1)} collective-permute-done((f32[3,3,12,128]{3,2,1,0:T(8,128)S(1)}, f32[3,3,12,128]{3,2,1,0:T(8,128)S(1)}, u32[]{:S(2)}, u32[]{:S(2)}) %collective-permute-start.11) | collective-permute-done | bytes 55328 | tf_op jit(solution)/shard_map/ppermute | solution.py:260
  70.4 3.1 %shard_map.183 = (f32[2,12,128]{2,1,0:T(8,128)S(1)}, bf16[12,48,768]{2,1,0:T(8,128)(2,1)S(1)}) custom-call(bf16[12,2,3,128,48]{4,3,2,1,0:T(8,128)(2,1)S(1)} %get-tuple-element.79.own_ref.own_bf, f32[3,6,12,128]{3,2,1,0:T(8,128)S(1)} %pad_maximum_fusion.1.near_ref), custom_call_target="tpu_custom_call" | custom-call | flops 1000000000 | bytes 1000000 | tf_op jit(solution)/shard_map/pallas_call | solution.py:212
  73.5 3.9 %collective-permute-start.12 = (f32[2,12,128]{2,1,0:T(8,128)S(1)}, f32[2,12,128]{2,1,0:T(8,128)S(1)}, u32[]{:S(2)}, u32[]{:S(2)}) collective-permute-start(f32[2,12,128]{2,1,0:T(8,128)S(1)} %rsqrt_multiply_fusion.1.own_slope_ref), channel_id=1, source_target_pairs={{0,8},{8,0},{16,24},{24,16},{32,40},{40,32},{48,56},{56,48},{64,72... | collective-permute-start | bytes 36872 | tf_op jit(solution)/shard_map/ppermute | solution.py:260
  78.3 10.6 %shard_map.184 = (f32[3,2,12,128]{3,2,1,0:T(8,128)S(1)}, f32[12,2,128,128]{3,2,1,0:T(8,128)S(1)}) custom-call(f32[3,2,12,128]{3,2,1,0:T(8,128)S(1)} %get-tuple-element.124.own_ref, f32[3,4,12,128]{3,2,1,0:T(8,128)S(1)} %pad_maximum_fusion.4.near_ref, bf16[12,2,3,128,48]{4,3,2,1,0:T(8,128)(2,1)S(1)} %get-tuple-element.79.own_ref.own_bf, ...), custom_call_target="tpu_custom_call" | custom-call | flops 1000000000 | bytes 1000000 | tf_op jit(solution)/shard_map/pallas_call | solution.py:212
  90.5 5.3 %shard_map.185 = f32[3,2,12,128]{3,2,1,0:T(8,128)S(1)} custom-call(f32[3,2,12,128]{3,2,1,0:T(8,128)S(1)} %get-tuple-element.124.own_ref, f32[3,2,12,128]{3,2,1,0:T(8,128)S(1)} %broadcast_subtract_fusion.1.near_ref, bf16[12,2,3,128,48]{4,3,2,1,0:T(8,128)(2,1)S(1)} %get-tuple-element.79.own_ref.own_bf, bf16[12,48,256]{2,1,0:T(8,128)(2,1)S(1)} %get-tuple-element.91.near_bf, ...), custom_call_target="tpu_custom_call" | custom-call | flops 1000000000 | bytes 1000000 | tf_op jit(solution)/shard_map/pallas_call | solution.py:212
  95.8 7.7 %shard_map.186 = f32[3,2,12,128]{3,2,1,0:T(8,128)S(1)} custom-call(f32[3,2,12,128]{3,2,1,0:T(8,128)S(1)} %get-tuple-element.124.own_ref, f32[3,6,12,128]{3,2,1,0:T(8,128)S(1)} %pad_maximum_fusion.1.near_ref, bf16[12,2,3,128,48]{4,3,2,1,0:T(8,128)(2,1)S(1)} %get-tuple-element.79.own_ref.own_bf, bf16[12,48,768]{2,1,0:T(8,128)(2,1)S(1)} %get-tuple-element.95.near_bf, ...), custom_call_target="tpu_custom_call" | custom-call | flops 1000000000 | bytes 1000000 | tf_op jit(solution)/shard_map/pallas_call | solution.py:212
  103.6 1.6 %collective-permute-start.16 = (f32[3,2,12,128]{3,2,1,0:T(8,128)S(1)}, f32[3,2,12,128]{3,2,1,0:T(8,128)S(1)}, u32[]{:S(2)}, u32[]{:S(2)}) collective-permute-start(f32[3,2,12,128]{3,2,1,0:T(8,128)S(1)} %get-tuple-element.122.own_ref), channel_id=1, source_target_pairs={{0,8},{8,0},{16,24},{24,16},{32,40},{40,32},{48,56},{56,48},{64,72... | collective-permute-start | bytes 110600 | tf_op jit(solution)/shard_map/ppermute | solution.py:260
  106.2 4.7 %shard_map.187 = (f32[2,12,128]{2,1,0:T(8,128)S(1)}, bf16[12,48,512]{2,1,0:T(8,128)(2,1)S(1)}, bf16[12,2,3,128,48]{4,3,2,1,0:T(8,128)(2,1)S(1)}) custom-call(f32[3,2,12,128]{3,2,1,0:T(8,128)S(1)} %get-tuple-element.122.own_ref, f32[3,4,12,128]{3,2,1,0:T(8,128)S(1)} %pad_maximum_fusion.5.near_ref), custom_call_target="tpu_custom_call" | custom-call | flops 1000000000 | bytes 1000000 | tf_op jit(solution)/shard_map/pallas_call | solution.py:212
  111.6 2.1 %collective-permute-start.19 = (f32[3,3,12,128]{3,2,1,0:T(8,128)S(1)}, f32[3,3,12,128]{3,2,1,0:T(8,128)S(1)}, u32[]{:S(2)}, u32[]{:S(2)}) collective-permute-start(f32[3,3,12,128]{3,2,1,0:T(8,128)S(1)} %get-tuple-element.128), channel_id=1, source_target_pairs={{0,7},{1,2},{2,1},{3,4},{4,3},{5,6},{6,5},{7,0},{8,15},{9,10},{10,... | collective-permute-start | bytes 165896 | tf_op jit(solution)/shard_map/ppermute | solution.py:260
  113.7 2.5 %shard_map.188 = (f32[2,12,128]{2,1,0:T(8,128)S(1)}, bf16[12,48,256]{2,1,0:T(8,128)(2,1)S(1)}) custom-call(bf16[12,2,3,128,48]{4,3,2,1,0:T(8,128)(2,1)S(1)} %get-tuple-element.98.own_ref.own_bf, f32[3,2,12,128]{3,2,1,0:T(8,128)S(1)} %broadcast_subtract_fusion.near_ref), custom_call_target="tpu_custom_call" | custom-call | flops 1000000000 | bytes 1000000 | tf_op jit(solution)/shard_map/pallas_call | solution.py:212
  117.0 3.1 %shard_map.189 = (f32[2,12,128]{2,1,0:T(8,128)S(1)}, bf16[12,48,768]{2,1,0:T(8,128)(2,1)S(1)}) custom-call(bf16[12,2,3,128,48]{4,3,2,1,0:T(8,128)(2,1)S(1)} %get-tuple-element.98.own_ref.own_bf, f32[3,6,12,128]{3,2,1,0:T(8,128)S(1)} %pad_maximum_fusion.2.near_ref), custom_call_target="tpu_custom_call" | custom-call | flops 1000000000 | bytes 1000000 | tf_op jit(solution)/shard_map/pallas_call | solution.py:212
  120.1 4.0 %collective-permute-start.20 = (f32[2,12,128]{2,1,0:T(8,128)S(1)}, f32[2,12,128]{2,1,0:T(8,128)S(1)}, u32[]{:S(2)}, u32[]{:S(2)}) collective-permute-start(f32[2,12,128]{2,1,0:T(8,128)S(1)} %rsqrt_multiply_fusion.own_slope_ref), channel_id=1, source_target_pairs={{0,8},{8,0},{16,24},{24,16},{32,40},{40,32},{48,56},{56,48},{64,72... | collective-permute-start | bytes 36872 | tf_op jit(solution)/shard_map/ppermute | solution.py:260
  125.0 10.6 %shard_map.190 = (f32[3,2,12,128]{3,2,1,0:T(8,128)S(1)}, f32[12,2,128,128]{3,2,1,0:T(8,128)S(1)}) custom-call(f32[3,2,12,128]{3,2,1,0:T(8,128)S(1)} %get-tuple-element.122.own_ref, f32[3,4,12,128]{3,2,1,0:T(8,128)S(1)} %pad_maximum_fusion.5.near_ref, bf16[12,2,3,128,48]{4,3,2,1,0:T(8,128)(2,1)S(1)} %get-tuple-element.98.own_ref.own_bf, ...), custom_call_target="tpu_custom_call" | custom-call | flops 1000000000 | bytes 1000000 | tf_op jit(solution)/shard_map/pallas_call | solution.py:212
  136.0 2.3 %collective-permute-start.23 = (f32[3,12,128]{2,1,0:T(8,128)S(1)}, f32[3,12,128]{2,1,0:T(8,128)S(1)}, u32[]{:S(2)}, u32[]{:S(2)}) collective-permute-start(f32[3,12,128]{2,1,0:T(8,128)S(1)} %get-tuple-element.141), channel_id=1, source_target_pairs={{0,7},{1,2},{2,1},{3,4},{4,3},{5,6},{6,5},{7,0},{8,15},{9,10},{10,... | collective-permute-start | bytes 55304 | tf_op jit(solution)/shard_map/ppermute | solution.py:260
  138.3 5.3 %shard_map.191 = f32[3,2,12,128]{3,2,1,0:T(8,128)S(1)} custom-call(f32[3,2,12,128]{3,2,1,0:T(8,128)S(1)} %get-tuple-element.122.own_ref, f32[3,2,12,128]{3,2,1,0:T(8,128)S(1)} %broadcast_subtract_fusion.near_ref, bf16[12,2,3,128,48]{4,3,2,1,0:T(8,128)(2,1)S(1)} %get-tuple-element.98.own_ref.own_bf, bf16[12,48,256]{2,1,0:T(8,128)(2,1)S(1)} %get-tuple-element.110.near_bf, ...), custom_call_target="tpu_custom_call" | custom-call | flops 1000000000 | bytes 1000000 | tf_op jit(solution)/shard_map/pallas_call | solution.py:212
  143.6 7.7 %shard_map.192 = f32[3,2,12,128]{3,2,1,0:T(8,128)S(1)} custom-call(f32[3,2,12,128]{3,2,1,0:T(8,128)S(1)} %get-tuple-element.122.own_ref, f32[3,6,12,128]{3,2,1,0:T(8,128)S(1)} %pad_maximum_fusion.2.near_ref, bf16[12,2,3,128,48]{4,3,2,1,0:T(8,128)(2,1)S(1)} %get-tuple-element.98.own_ref.own_bf, bf16[12,48,768]{2,1,0:T(8,128)(2,1)S(1)} %get-tuple-element.114.near_bf, ...), custom_call_target="tpu_custom_call" | custom-call | flops 1000000000 | bytes 1000000 | tf_op jit(solution)/shard_map/pallas_call | solution.py:212
  (103 shorter events, 13.2 us)
Async XLA Ops:
  2.2 5.2 %collective-permute-start = (f32[3,2,12,128]{3,2,1,0:T(8,128)S(1)}, f32[3,2,12,128]{3,2,1,0:T(8,128)S(1)}, u32[]{:S(2)}, u32[]{:S(2)}) collective-permute-start(f32[3,2,12,128]{3,2,1,0:T(8,128)S(1)} %fusion.6.own_ref), channel_id=1, source_target_pairs={{0,8},{8,0},{16,24},{24,16},{32,40},{40,32},{48,56},{56,48},{64,72... | collective-permute-start | bytes 110600 | tf_op jit(solution)/shard_map/ppermute | solution.py:260
  5.5 6.8 %collective-permute-start.1 = (f32[3,2,12,128]{3,2,1,0:T(8,128)S(1)}, f32[3,2,12,128]{3,2,1,0:T(8,128)S(1)}, u32[]{:S(2)}, u32[]{:S(2)}) collective-permute-start(f32[3,2,12,128]{3,2,1,0:T(8,128)S(1)} %fusion.6.own_ref), channel_id=1, source_target_pairs={{0,248},{8,16},{16,8},{24,32},{32,24},{40,48},{48,40},{56,64},{64,... | collective-permute-start | bytes 110600 | tf_op jit(solution)/shard_map/ppermute | solution.py:260
  12.2 7.2 %copy-start.3 = (f32[3]{0:T(128)S(1)}, f32[3]{0:T(128)}, u32[]{:S(2)}) copy-start(f32[3]{0:T(128)} %constant.90) | copy-start | bytes 40
  12.2 7.2 %copy-start.4 = (f32[3]{0:T(128)S(1)}, f32[3]{0:T(128)}, u32[]{:S(2)}) copy-start(f32[3]{0:T(128)} %constant.89) | copy-start | bytes 40
  12.4 6.8 %collective-permute-start.2 = (f32[3,3,12,128]{3,2,1,0:T(8,128)S(1)}, f32[3,3,12,128]{3,2,1,0:T(8,128)S(1)}, u32[]{:S(2)}, u32[]{:S(2)}) collective-permute-start(f32[3,3,12,128]{3,2,1,0:T(8,128)S(1)} %get-tuple-element.137), channel_id=1, source_target_pairs={{0,1},{1,0},{2,3},{3,2},{4,5},{5,4},{6,7},{7,6},{8,9},{9,8},{10,11... | collective-permute-start | bytes 165896 | tf_op jit(solution)/shard_map/ppermute | solution.py:260
  14.1 5.3 %collective-permute-start.3 = (f32[3,3,12,128]{3,2,1,0:T(8,128)S(1)}, f32[3,3,12,128]{3,2,1,0:T(8,128)S(1)}, u32[]{:S(2)}, u32[]{:S(2)}) collective-permute-start(f32[3,3,12,128]{3,2,1,0:T(8,128)S(1)} %get-tuple-element.136), channel_id=1, source_target_pairs={{0,7},{1,2},{2,1},{3,4},{4,3},{5,6},{6,5},{7,0},{8,15},{9,10},{10,... | collective-permute-start | bytes 165896 | tf_op jit(solution)/shard_map/ppermute | solution.py:260
  22.6 7.2 %collective-permute-start.4 = (f32[2,12,128]{2,1,0:T(8,128)S(1)}, f32[2,12,128]{2,1,0:T(8,128)S(1)}, u32[]{:S(2)}, u32[]{:S(2)}) collective-permute-start(f32[2,12,128]{2,1,0:T(8,128)S(1)} %rsqrt_multiply_fusion.2.own_slope_ref), channel_id=1, source_target_pairs={{0,8},{8,0},{16,24},{24,16},{32,40},{40,32},{48,56},{56,48},{64,72... | collective-permute-start | bytes 36872 | tf_op jit(solution)/shard_map/ppermute | solution.py:260
  29.0 11.4 %collective-permute-start.5 = (f32[2,12,128]{2,1,0:T(8,128)S(1)}, f32[2,12,128]{2,1,0:T(8,128)S(1)}, u32[]{:S(2)}, u32[]{:S(2)}) collective-permute-start(f32[2,12,128]{2,1,0:T(8,128)S(1)} %rsqrt_multiply_fusion.2.own_slope_ref), channel_id=1, source_target_pairs={{0,248},{8,16},{16,8},{24,32},{32,24},{40,48},{48,40},{56,64},{64,... | collective-permute-start | bytes 36872 | tf_op jit(solution)/shard_map/ppermute | solution.py:260
  40.5 8.5 %collective-permute-start.6 = (f32[3,12,128]{2,1,0:T(8,128)S(1)}, f32[3,12,128]{2,1,0:T(8,128)S(1)}, u32[]{:S(2)}, u32[]{:S(2)}) collective-permute-start(f32[3,12,128]{2,1,0:T(8,128)S(1)} %get-tuple-element.162), channel_id=1, source_target_pairs={{0,1},{1,0},{2,3},{3,2},{4,5},{5,4},{6,7},{7,6},{8,9},{9,8},{10,11... | collective-permute-start | bytes 55304 | tf_op jit(solution)/shard_map/ppermute | solution.py:260
  40.6 8.4 %collective-permute-start.7 = (f32[3,12,128]{2,1,0:T(8,128)S(1)}, f32[3,12,128]{2,1,0:T(8,128)S(1)}, u32[]{:S(2)}, u32[]{:S(2)}) collective-permute-start(f32[3,12,128]{2,1,0:T(8,128)S(1)} %get-tuple-element.161), channel_id=1, source_target_pairs={{0,7},{1,2},{2,1},{3,4},{4,3},{5,6},{6,5},{7,0},{8,15},{9,10},{10,... | collective-permute-start | bytes 55304 | tf_op jit(solution)/shard_map/ppermute | solution.py:260
  49.0 7.8 %copy-start = (f32[3,1,2,12,128]{4,2,3,1,0:T(2,128)S(1)}, f32[3,1,2,12,128]{4,2,3,1,0:T(2,128)}, u32[]{:S(2)}) copy-start(f32[3,1,2,12,128]{4,2,3,1,0:T(2,128)} %param.16) | copy-start | bytes 110596
  49.1 7.8 %copy-start.1 = (f32[3,1,2,12,128]{4,2,3,1,0:T(2,128)S(1)}, f32[3,1,2,12,128]{4,2,3,1,0:T(2,128)}, u32[]{:S(2)}) copy-start(f32[3,1,2,12,128]{4,2,3,1,0:T(2,128)} %param.17) | copy-start | bytes 110596
  49.1 7.8 %copy-start.2 = (f32[3,2]{1,0:T(4,128)S(1)}, f32[3,2]{1,0:T(4,128)}, u32[]{:S(2)}) copy-start(f32[3,2]{1,0:T(4,128)} %constant.88) | copy-start | bytes 76
  56.9 2.7 %collective-permute-start.8 = (f32[3,2,12,128]{3,2,1,0:T(8,128)S(1)}, f32[3,2,12,128]{3,2,1,0:T(8,128)S(1)}, u32[]{:S(2)}, u32[]{:S(2)}) collective-permute-start(f32[3,2,12,128]{3,2,1,0:T(8,128)S(1)} %get-tuple-element.124.own_ref), channel_id=1, source_target_pairs={{0,8},{8,0},{16,24},{24,16},{32,40},{40,32},{48,56},{56,48},{64,72... | collective-permute-start | bytes 110600 | tf_op jit(solution)/shard_map/ppermute | solution.py:260
  58.7 5.7 %collective-permute-start.9 = (f32[3,2,12,128]{3,2,1,0:T(8,128)S(1)}, f32[3,2,12,128]{3,2,1,0:T(8,128)S(1)}, u32[]{:S(2)}, u32[]{:S(2)}) collective-permute-start(f32[3,2,12,128]{3,2,1,0:T(8,128)S(1)} %get-tuple-element.124.own_ref), channel_id=1, source_target_pairs={{0,248},{8,16},{16,8},{24,32},{32,24},{40,48},{48,40},{56,64},{64,... | collective-permute-start | bytes 110600 | tf_op jit(solution)/shard_map/ppermute | solution.py:260
  64.5 4.1 %collective-permute-start.10 = (f32[3,3,12,128]{3,2,1,0:T(8,128)S(1)}, f32[3,3,12,128]{3,2,1,0:T(8,128)S(1)}, u32[]{:S(2)}, u32[]{:S(2)}) collective-permute-start(f32[3,3,12,128]{3,2,1,0:T(8,128)S(1)} %get-tuple-element.133), channel_id=1, source_target_pairs={{0,1},{1,0},{2,3},{3,2},{4,5},{5,4},{6,7},{7,6},{8,9},{9,8},{10,11... | collective-permute-start | bytes 165896 | tf_op jit(solution)/shard_map/ppermute | solution.py:260
  64.6 5.7 %collective-permute-start.11 = (f32[3,3,12,128]{3,2,1,0:T(8,128)S(1)}, f32[3,3,12,128]{3,2,1,0:T(8,128)S(1)}, u32[]{:S(2)}, u32[]{:S(2)}) collective-permute-start(f32[3,3,12,128]{3,2,1,0:T(8,128)S(1)} %get-tuple-element.132), channel_id=1, source_target_pairs={{0,7},{1,2},{2,1},{3,4},{4,3},{5,6},{6,5},{7,0},{8,15},{9,10},{10,... | collective-permute-start | bytes 165896 | tf_op jit(solution)/shard_map/ppermute | solution.py:260
  73.5 4.7 %collective-permute-start.12 = (f32[2,12,128]{2,1,0:T(8,128)S(1)}, f32[2,12,128]{2,1,0:T(8,128)S(1)}, u32[]{:S(2)}, u32[]{:S(2)}) collective-permute-start(f32[2,12,128]{2,1,0:T(8,128)S(1)} %rsqrt_multiply_fusion.1.own_slope_ref), channel_id=1, source_target_pairs={{0,8},{8,0},{16,24},{24,16},{32,40},{40,32},{48,56},{56,48},{64,72... | collective-permute-start | bytes 36872 | tf_op jit(solution)/shard_map/ppermute | solution.py:260
  77.4 11.4 %collective-permute-start.13 = (f32[2,12,128]{2,1,0:T(8,128)S(1)}, f32[2,12,128]{2,1,0:T(8,128)S(1)}, u32[]{:S(2)}, u32[]{:S(2)}) collective-permute-start(f32[2,12,128]{2,1,0:T(8,128)S(1)} %rsqrt_multiply_fusion.1.own_slope_ref), channel_id=1, source_target_pairs={{0,248},{8,16},{16,8},{24,32},{32,24},{40,48},{48,40},{56,64},{64,... | collective-permute-start | bytes 36872 | tf_op jit(solution)/shard_map/ppermute | solution.py:260
  88.9 6.8 %collective-permute-start.14 = (f32[3,12,128]{2,1,0:T(8,128)S(1)}, f32[3,12,128]{2,1,0:T(8,128)S(1)}, u32[]{:S(2)}, u32[]{:S(2)}) collective-permute-start(f32[3,12,128]{2,1,0:T(8,128)S(1)} %get-tuple-element.152), channel_id=1, source_target_pairs={{0,1},{1,0},{2,3},{3,2},{4,5},{5,4},{6,7},{7,6},{8,9},{9,8},{10,11... | collective-permute-start | bytes 55304 | tf_op jit(solution)/shard_map/ppermute | solution.py:260
  89.2 6.5 %collective-permute-start.15 = (f32[3,12,128]{2,1,0:T(8,128)S(1)}, f32[3,12,128]{2,1,0:T(8,128)S(1)}, u32[]{:S(2)}, u32[]{:S(2)}) collective-permute-start(f32[3,12,128]{2,1,0:T(8,128)S(1)} %get-tuple-element.151), channel_id=1, source_target_pairs={{0,7},{1,2},{2,1},{3,4},{4,3},{5,6},{6,5},{7,0},{8,15},{9,10},{10,... | collective-permute-start | bytes 55304 | tf_op jit(solution)/shard_map/ppermute | solution.py:260
  103.6 2.5 %collective-permute-start.16 = (f32[3,2,12,128]{3,2,1,0:T(8,128)S(1)}, f32[3,2,12,128]{3,2,1,0:T(8,128)S(1)}, u32[]{:S(2)}, u32[]{:S(2)}) collective-permute-start(f32[3,2,12,128]{3,2,1,0:T(8,128)S(1)} %get-tuple-element.122.own_ref), channel_id=1, source_target_pairs={{0,8},{8,0},{16,24},{24,16},{32,40},{40,32},{48,56},{56,48},{64,72... | collective-permute-start | bytes 110600 | tf_op jit(solution)/shard_map/ppermute | solution.py:260
  105.2 5.7 %collective-permute-start.17 = (f32[3,2,12,128]{3,2,1,0:T(8,128)S(1)}, f32[3,2,12,128]{3,2,1,0:T(8,128)S(1)}, u32[]{:S(2)}, u32[]{:S(2)}) collective-permute-start(f32[3,2,12,128]{3,2,1,0:T(8,128)S(1)} %get-tuple-element.122.own_ref), channel_id=1, source_target_pairs={{0,248},{8,16},{16,8},{24,32},{32,24},{40,48},{48,40},{56,64},{64,... | collective-permute-start | bytes 110600 | tf_op jit(solution)/shard_map/ppermute | solution.py:260
  111.1 5.2 %collective-permute-start.18 = (f32[3,3,12,128]{3,2,1,0:T(8,128)S(1)}, f32[3,3,12,128]{3,2,1,0:T(8,128)S(1)}, u32[]{:S(2)}, u32[]{:S(2)}) collective-permute-start(f32[3,3,12,128]{3,2,1,0:T(8,128)S(1)} %get-tuple-element.129), channel_id=1, source_target_pairs={{0,1},{1,0},{2,3},{3,2},{4,5},{5,4},{6,7},{7,6},{8,9},{9,8},{10,11... | collective-permute-start | bytes 165896 | tf_op jit(solution)/shard_map/ppermute | solution.py:260
  111.6 5.3 %collective-permute-start.19 = (f32[3,3,12,128]{3,2,1,0:T(8,128)S(1)}, f32[3,3,12,128]{3,2,1,0:T(8,128)S(1)}, u32[]{:S(2)}, u32[]{:S(2)}) collective-permute-start(f32[3,3,12,128]{3,2,1,0:T(8,128)S(1)} %get-tuple-element.128), channel_id=1, source_target_pairs={{0,7},{1,2},{2,1},{3,4},{4,3},{5,6},{6,5},{7,0},{8,15},{9,10},{10,... | collective-permute-start | bytes 165896 | tf_op jit(solution)/shard_map/ppermute | solution.py:260
  120.1 4.8 %collective-permute-start.20 = (f32[2,12,128]{2,1,0:T(8,128)S(1)}, f32[2,12,128]{2,1,0:T(8,128)S(1)}, u32[]{:S(2)}, u32[]{:S(2)}) collective-permute-start(f32[2,12,128]{2,1,0:T(8,128)S(1)} %rsqrt_multiply_fusion.own_slope_ref), channel_id=1, source_target_pairs={{0,8},{8,0},{16,24},{24,16},{32,40},{40,32},{48,56},{56,48},{64,72... | collective-permute-start | bytes 36872 | tf_op jit(solution)/shard_map/ppermute | solution.py:260
  124.1 11.4 %collective-permute-start.21 = (f32[2,12,128]{2,1,0:T(8,128)S(1)}, f32[2,12,128]{2,1,0:T(8,128)S(1)}, u32[]{:S(2)}, u32[]{:S(2)}) collective-permute-start(f32[2,12,128]{2,1,0:T(8,128)S(1)} %rsqrt_multiply_fusion.own_slope_ref), channel_id=1, source_target_pairs={{0,248},{8,16},{16,8},{24,32},{32,24},{40,48},{48,40},{56,64},{64,... | collective-permute-start | bytes 36872 | tf_op jit(solution)/shard_map/ppermute | solution.py:260
  135.6 8.0 %collective-permute-start.22 = (f32[3,12,128]{2,1,0:T(8,128)S(1)}, f32[3,12,128]{2,1,0:T(8,128)S(1)}, u32[]{:S(2)}, u32[]{:S(2)}) collective-permute-start(f32[3,12,128]{2,1,0:T(8,128)S(1)} %get-tuple-element.142), channel_id=1, source_target_pairs={{0,1},{1,0},{2,3},{3,2},{4,5},{5,4},{6,7},{7,6},{8,9},{9,8},{10,11... | collective-permute-start | bytes 55304 | tf_op jit(solution)/shard_map/ppermute | solution.py:260
  136.0 7.6 %collective-permute-start.23 = (f32[3,12,128]{2,1,0:T(8,128)S(1)}, f32[3,12,128]{2,1,0:T(8,128)S(1)}, u32[]{:S(2)}, u32[]{:S(2)}) collective-permute-start(f32[3,12,128]{2,1,0:T(8,128)S(1)} %get-tuple-element.141), channel_id=1, source_target_pairs={{0,7},{1,2},{2,1},{3,4},{4,3},{5,6},{6,5},{7,0},{8,15},{9,10},{10,... | collective-permute-start | bytes 55304 | tf_op jit(solution)/shard_map/ppermute | solution.py:260

commit v3 on v2

--- a/solution.py
+++ b/solution.py
@@ -16,9 +16,9 @@
 SLOTS = 128
 KF = 48
 CHUNK = 16
-UNROLL = 2
-INNER = ((0, 4), (0, 4))
-MIDDLE = ((0, 2), (0, 2))
+UNROLL = 4
+INNER = ((0, 3), (0, 3))
+MIDDLE = ((0, 3), (0, 3))
 OUTER = ((0, 3), (3, 6))
 
 
@@ -73,7 +73,11 @@
 
 
 def slab_of(c, r):
-    return lax.rem(c + (r + NZ - 1), NZ)
+    if isinstance(c, int):
+        return (c + r + NZ - 1) % NZ
+    if r == 1:
+        return c
+    return jnp.where(c == 0, NZ - 1, c - 1) if r == 0 else jnp.where(c == NZ - 1, 0, c + 1)
 
 
 def density_kernel(spans, fresh, own_ref, near_ref, sum_ref, near_bf, *refs):
@@ -162,7 +166,7 @@
                 fold(jnp.maximum(c - 1, 0), 1)
             else:
                 fold(c, 0)
-            ahead = (c, 1) if iy == 0 else (lax.rem(c + 1, NZ), 0)
+            ahead = (c, 1) if iy == 0 else (slab_of(c, 2), 0)
             step = 0
             pending = list(tiles)
             first, last = spans[iy]
@@ -254,6 +258,29 @@
     )
 
 
+def finish_kernel(counts_ref, position_ref, velocity_ref, *refs):
+    *parts, position_out, velocity_out, force_out = refs
+    lane = lax.broadcasted_iota(jnp.int32, (NZ, SLOTS), 1)
+    for iy in range(2):
+        present = lane < counts_ref[iy]
+        for k in range(3):
+            force = jnp.where(present, sum(part[k, iy] for part in parts), 0.0)
+            force_out[k, :, iy, :] = force
+            velocity_out[k, :, iy, :] = velocity_ref[k, iy] + 0.5 * TIME_STEP * force
+            position_out[k, :, iy, :] = position_ref[k, iy]
+
+
+def finish(positions, velocities, counts, parts):
+    counts = jnp.broadcast_to(counts[..., None], (2, NZ, SLOTS))
+    outs = pl.pallas_call(
+        finish_kernel,
+        out_shape=[jax.ShapeDtypeStruct((3, NZ, 2, SLOTS), jnp.float32)] * 3,
+        in_specs=[VMEM] * (3 + len(parts)),
+        compiler_params=pltpu.CompilerParams(vmem_limit_bytes=8 * 2**20),
+    )(counts, positions, velocities, *parts)
+    return tuple(out.transpose(0, 2, 1, 3)[:, None] for out in outs)
+
+
 def swap(value, axis, odd):
     n = lax.axis_size(axis)
     partner = [(i + 1 if i % 2 == odd else i - 1) % n for i in range(n)]
@@ -305,12 +332,13 @@
         own = jnp.where(present, positions + frame, FAR)
         near, far = exchange_x(own)
         near = near + along(0, side)
-        inner = jnp.concatenate([own, near], axis=1)
+        inner = jnp.concatenate([own, near[:, :1]], axis=1)
         square, inner_bf, own_bf = density_part(own, inner, INNER)
         square, far = lax.optimization_barrier((square, far))
         far = far - along(0, side)
         received = exchange_y(rows_along_y(own, near, far))
-        part, far_bf = density_part(own_bf, far, MIDDLE)
+        middle = jnp.concatenate([near[:, 1:], far], axis=1)
+        part, middle_bf = density_part(own_bf, middle, MIDDLE)
         part, received = lax.optimization_barrier((part, received))
         below, above = below_above(received)
         outer = jnp.concatenate([below - along(1, 2.0), above + along(1, 2.0)], axis=1)
@@ -318,24 +346,28 @@
         density = DENSITY_SCALE * jnp.maximum(square + part + last - 1.0, 0.0)
         slope = -0.25 * lax.rsqrt(1.0 + density)
         near_slope, far_slope = exchange_x(slope)
-        inner_slope = jnp.concatenate([slope, near_slope], axis=0)
+        inner_slope = jnp.concatenate([slope, near_slope[:1]], axis=0)
         force, turned = force_part(own, inner, own_bf, inner_bf, slope, inner_slope, INNER)
         force, far_slope = lax.optimization_barrier((force, far_slope))
         received = exchange_y(rows_along_y(slope, near_slope, far_slope))
-        (part,) = force_part(own, far, own_bf, far_bf, turned, far_slope, MIDDLE)
+        middle_slope = jnp.concatenate([near_slope[1:], far_slope], axis=0)
+        (part,) = force_part(own, middle, own_bf, middle_bf, turned, middle_slope, MIDDLE)
         part, received = lax.optimization_barrier((part, received))
         outer_slope = jnp.concatenate(below_above(received), axis=0)
         (last,) = force_part(own, outer, own_bf, outer_bf, turned, outer_slope, OUTER)
-        force = force + part + last
-        return jnp.where(present, force, 0.0)
-
-    pushed = forces_of(positions)
-    for _ in range(STEPS):
+        return force, part, last
+
+    parts = forces_of(positions)
+    for step in range(STEPS):
+        if step:
+            pushed = jnp.where(present, sum(parts), 0.0)
+            velocities = velocities + 0.5 * TIME_STEP * pushed
+        else:
+            pushed = jnp.where(present, sum(parts), 0.0)
         velocities = velocities + 0.5 * TIME_STEP * pushed
         positions = positions + TIME_STEP * velocities
-        pushed = forces_of(positions)
-        velocities = velocities + 0.5 * TIME_STEP * pushed
-    return (positions[:, None], velocities[:, None], pushed[:, None])
+        parts = forces_of(positions)
+    return finish(positions, velocities, counts[0], parts)
 
 
 def solution(mesh):

time: 153 us -> 151 us (0.987)
  Pallas kernels: 102 us -> 99.1 us
  starting transfers between devices: 39.3 us -> 41.3 us
  local copies, waits for them, and re-layouts: 2.02 us -> 0.19 us
    pallas_call x18, Pallas kernels: 102 us -> 98.4 us  [call(): pl.pallas_call(kernel, out_shape=out_shape, in_specs=[VMEM] * len(operand...]
    ppermute x24, starting transfers between devices: 39.3 us -> 41.3 us  [swap(): return lax.ppermute(value, axis, [(i, partner[i]) for i in range(n)])]
    unnamed x13 -> x12, local copies, waits for them, and re-layouts: 1.94 us -> 0.04 us
  transfers between devices with their start and end apart: 24 -> 24, of which waited for: 8 -> 9; matrix products, arithmetic and copies ran while one was open for 1% -> 1% of each run, Pallas kernels for 45% -> 44%
where the time goes in v3:
time: 151 us
  Pallas kernels  99.1 us (66%)
  starting transfers between devices  41.3 us (27%)
  waiting for transfers between devices  5.8 us (4%)
  other arithmetic  3.39 us (2%)
    pallas_call x18, Pallas kernels, call(): pl.pallas_call(kernel, out_shape=out_shape, in_specs=[VMEM] * len(operand...  98.4 us
    ppermute x24, starting transfers between devices, swap(): return lax.ppermute(value, axis, [(i, partner[i]) for i in range(n)])  41.3 us
    ppermute x24, waiting for transfers between devices, swap(): return lax.ppermute(value, axis, [(i, partner[i]) for i in range(n)])  5.8 us
  transfers between devices with their start and end apart: 24, of which 9 were waited for; matrix products, arithmetic and copies ran while one was open for 1% of the time, Pallas kernels for 44%

profile of v3, /device:TPU:1, one launch (start us, length us, event | category | flops | bytes accessed | tf_op | source)
XLA Modules:
  0.0 151.0 jit_solution(1822606095396804356)
XLA Ops:
  2.2 3.2 %collective-permute-start = (f32[3,2,12,128]{3,2,1,0:T(8,128)S(1)}, f32[3,2,12,128]{3,2,1,0:T(8,128)S(1)}, u32[]{:S(2)}, u32[]{:S(2)}) collective-permute-start(f32[3,2,12,128]{3,2,1,0:T(8,128)S(1)} %fusion.6.own_ref), channel_id=1, source_target_pairs={{0,8},{8,0},{16,24},{24,16},{32,40},{40,32},{48,56},{56,48},{64,72... | collective-permute-start | bytes 110600 | tf_op jit(solution)/shard_map/ppermute | solution.py:287
  7.5 3.6 %shard_map.175 = (f32[2,12,128]{2,1,0:T(8,128)S(1)}, bf16[12,48,384]{2,1,0:T(8,128)(2,1)S(1)}, bf16[12,2,3,128,48]{4,3,2,1,0:T(8,128)(2,1)S(1)}) custom-call(f32[3,2,12,128]{3,2,1,0:T(8,128)S(1)} %fusion.6.own_ref, f32[3,3,12,128]{3,2,1,0:T(8,128)S(1)} %pad_maximum_fusion.3.near_ref), custom_call_target="tpu_custom_call" | custom-call | flops 1000000000 | bytes 1000000 | tf_op jit(solution)/shard_map/pallas_call | solution.py:216
  11.3 1.7 %collective-permute-start.2 = (f32[3,3,12,128]{3,2,1,0:T(8,128)S(1)}, f32[3,3,12,128]{3,2,1,0:T(8,128)S(1)}, u32[]{:S(2)}, u32[]{:S(2)}) collective-permute-start(f32[3,3,12,128]{3,2,1,0:T(8,128)S(1)} %get-tuple-element.142), channel_id=1, source_target_pairs={{0,1},{1,0},{2,3},{3,2},{4,5},{5,4},{6,7},{7,6},{8,9},{9,8},{10,11... | collective-permute-start | bytes 165896 | tf_op jit(solution)/shard_map/ppermute | solution.py:287
  13.0 2.6 %collective-permute-start.3 = (f32[3,3,12,128]{3,2,1,0:T(8,128)S(1)}, f32[3,3,12,128]{3,2,1,0:T(8,128)S(1)}, u32[]{:S(2)}, u32[]{:S(2)}) collective-permute-start(f32[3,3,12,128]{3,2,1,0:T(8,128)S(1)} %get-tuple-element.141), channel_id=1, source_target_pairs={{0,7},{1,2},{2,1},{3,4},{4,3},{5,6},{6,5},{7,0},{8,15},{9,10},{10,... | collective-permute-start | bytes 165896 | tf_op jit(solution)/shard_map/ppermute | solution.py:287
  15.5 2.5 %shard_map.176 = (f32[2,12,128]{2,1,0:T(8,128)S(1)}, bf16[12,48,384]{2,1,0:T(8,128)(2,1)S(1)}) custom-call(bf16[12,2,3,128,48]{4,3,2,1,0:T(8,128)(2,1)S(1)} %get-tuple-element.63.own_ref.own_bf, f32[3,3,12,128]{3,2,1,0:T(8,128)S(1)} %get-tuple-element.175.near_ref), custom_call_target="tpu_custom_call" | custom-call | flops 1000000000 | bytes 1000000 | tf_op jit(solution)/shard_map/pallas_call | solution.py:216
  18.6 2.6 %shard_map.177 = (f32[2,12,128]{2,1,0:T(8,128)S(1)}, bf16[12,48,768]{2,1,0:T(8,128)(2,1)S(1)}) custom-call(bf16[12,2,3,128,48]{4,3,2,1,0:T(8,128)(2,1)S(1)} %get-tuple-element.63.own_ref.own_bf, f32[3,6,12,128]{3,2,1,0:T(8,128)S(1)} %pad_maximum_fusion.near_ref), custom_call_target="tpu_custom_call" | custom-call | flops 1000000000 | bytes 1000000 | tf_op jit(solution)/shard_map/pallas_call | solution.py:216
  21.3 6.2 %collective-permute-start.4 = (f32[2,12,128]{2,1,0:T(8,128)S(1)}, f32[2,12,128]{2,1,0:T(8,128)S(1)}, u32[]{:S(2)}, u32[]{:S(2)}) collective-permute-start(f32[2,12,128]{2,1,0:T(8,128)S(1)} %rsqrt_multiply_fusion.2.own_slope_ref), channel_id=1, source_target_pairs={{0,8},{8,0},{16,24},{24,16},{32,40},{40,32},{48,56},{56,48},{64,72... | collective-permute-start | bytes 36872 | tf_op jit(solution)/shard_map/ppermute | solution.py:287
  28.3 8.4 %shard_map.178 = (f32[3,2,12,128]{3,2,1,0:T(8,128)S(1)}, f32[12,2,128,128]{3,2,1,0:T(8,128)S(1)}) custom-call(f32[3,2,12,128]{3,2,1,0:T(8,128)S(1)} %fusion.6.own_ref, f32[3,3,12,128]{3,2,1,0:T(8,128)S(1)} %pad_maximum_fusion.3.near_ref, bf16[12,2,3,128,48]{4,3,2,1,0:T(8,128)(2,1)S(1)} %get-tuple-element.63.own_ref.own_bf, ...), custom_call_target="tpu_custom_call" | custom-call | flops 1000000000 | bytes 1000000 | tf_op jit(solution)/shard_map/pallas_call | solution.py:216
  36.8 3.2 %collective-permute-start.7 = (f32[3,12,128]{2,1,0:T(8,128)S(1)}, f32[3,12,128]{2,1,0:T(8,128)S(1)}, u32[]{:S(2)}, u32[]{:S(2)}) collective-permute-start(f32[3,12,128]{2,1,0:T(8,128)S(1)} %get-tuple-element.165), channel_id=1, source_target_pairs={{0,7},{1,2},{2,1},{3,4},{4,3},{5,6},{6,5},{7,0},{8,15},{9,10},{10,... | collective-permute-start | bytes 55304 | tf_op jit(solution)/shard_map/ppermute | solution.py:287
  40.0 7.8 %shard_map.179 = f32[3,2,12,128]{3,2,1,0:T(8,128)S(1)} custom-call(f32[3,2,12,128]{3,2,1,0:T(8,128)S(1)} %fusion.6.own_ref, f32[3,3,12,128]{3,2,1,0:T(8,128)S(1)} %get-tuple-element.175.near_ref, bf16[12,2,3,128,48]{4,3,2,1,0:T(8,128)(2,1)S(1)} %get-tuple-element.63.own_ref.own_bf, bf16[12,48,384]{2,1,0:T(8,128)(2,1)S(1)} %get-tuple-element.75.near_bf, ...), custom_call_target="tpu_custom_call" | custom-call | flops 1000000000 | bytes 1000000 | tf_op jit(solution)/shard_map/pallas_call | solution.py:216
  47.9 7.9 %shard_map.180 = f32[3,2,12,128]{3,2,1,0:T(8,128)S(1)} custom-call(f32[3,2,12,128]{3,2,1,0:T(8,128)S(1)} %fusion.6.own_ref, f32[3,6,12,128]{3,2,1,0:T(8,128)S(1)} %pad_maximum_fusion.near_ref, bf16[12,2,3,128,48]{4,3,2,1,0:T(8,128)(2,1)S(1)} %get-tuple-element.63.own_ref.own_bf, bf16[12,48,768]{2,1,0:T(8,128)(2,1)S(1)} %get-tuple-element.79.near_bf, ...), custom_call_target="tpu_custom_call" | custom-call | flops 1000000000 | bytes 1000000 | tf_op jit(solution)/shard_map/pallas_call | solution.py:216
  55.9 1.7 %collective-permute-start.8 = (f32[3,2,12,128]{3,2,1,0:T(8,128)S(1)}, f32[3,2,12,128]{3,2,1,0:T(8,128)S(1)}, u32[]{:S(2)}, u32[]{:S(2)}) collective-permute-start(f32[3,2,12,128]{3,2,1,0:T(8,128)S(1)} %get-tuple-element.129.own_ref), channel_id=1, source_target_pairs={{0,8},{8,0},{16,24},{24,16},{32,40},{40,32},{48,56},{56,48},{64,72... | collective-permute-start | bytes 110600 | tf_op jit(solution)/shard_map/ppermute | solution.py:287
  58.6 3.6 %shard_map.181 = (f32[2,12,128]{2,1,0:T(8,128)S(1)}, bf16[12,48,384]{2,1,0:T(8,128)(2,1)S(1)}, bf16[12,2,3,128,48]{4,3,2,1,0:T(8,128)(2,1)S(1)}) custom-call(f32[3,2,12,128]{3,2,1,0:T(8,128)S(1)} %get-tuple-element.129.own_ref, f32[3,3,12,128]{3,2,1,0:T(8,128)S(1)} %pad_maximum_fusion.7.near_ref), custom_call_target="tpu_custom_call" | custom-call | flops 1000000000 | bytes 1000000 | tf_op jit(solution)/shard_map/pallas_call | solution.py:216
  62.6 1.6 %collective-permute-start.11 = (f32[3,3,12,128]{3,2,1,0:T(8,128)S(1)}, f32[3,3,12,128]{3,2,1,0:T(8,128)S(1)}, u32[]{:S(2)}, u32[]{:S(2)}) collective-permute-start(f32[3,3,12,128]{3,2,1,0:T(8,128)S(1)} %get-tuple-element.137), channel_id=1, source_target_pairs={{0,7},{1,2},{2,1},{3,4},{4,3},{5,6},{6,5},{7,0},{8,15},{9,10},{10,... | collective-permute-start | bytes 165896 | tf_op jit(solution)/shard_map/ppermute | solution.py:287
  64.2 2.5 %shard_map.182 = (f32[2,12,128]{2,1,0:T(8,128)S(1)}, bf16[12,48,384]{2,1,0:T(8,128)(2,1)S(1)}) custom-call(bf16[12,2,3,128,48]{4,3,2,1,0:T(8,128)(2,1)S(1)} %get-tuple-element.82.own_ref.own_bf, f32[3,3,12,128]{3,2,1,0:T(8,128)S(1)} %get-tuple-element.174.near_ref), custom_call_target="tpu_custom_call" | custom-call | flops 1000000000 | bytes 1000000 | tf_op jit(solution)/shard_map/pallas_call | solution.py:216
  66.7 1.3 collective-permute-done.11
  68.1 2.6 %shard_map.183 = (f32[2,12,128]{2,1,0:T(8,128)S(1)}, bf16[12,48,768]{2,1,0:T(8,128)(2,1)S(1)}) custom-call(bf16[12,2,3,128,48]{4,3,2,1,0:T(8,128)(2,1)S(1)} %get-tuple-element.82.own_ref.own_bf, f32[3,6,12,128]{3,2,1,0:T(8,128)S(1)} %pad_maximum_fusion.1.near_ref), custom_call_target="tpu_custom_call" | custom-call | flops 1000000000 | bytes 1000000 | tf_op jit(solution)/shard_map/pallas_call | solution.py:216
  70.8 4.4 %collective-permute-start.12 = (f32[2,12,128]{2,1,0:T(8,128)S(1)}, f32[2,12,128]{2,1,0:T(8,128)S(1)}, u32[]{:S(2)}, u32[]{:S(2)}) collective-permute-start(f32[2,12,128]{2,1,0:T(8,128)S(1)} %rsqrt_multiply_fusion.1.own_slope_ref), channel_id=1, source_target_pairs={{0,8},{8,0},{16,24},{24,16},{32,40},{40,32},{48,56},{56,48},{64,72... | collective-permute-start | bytes 36872 | tf_op jit(solution)/shard_map/ppermute | solution.py:287
  76.1 8.4 %shard_map.184 = (f32[3,2,12,128]{3,2,1,0:T(8,128)S(1)}, f32[12,2,128,128]{3,2,1,0:T(8,128)S(1)}) custom-call(f32[3,2,12,128]{3,2,1,0:T(8,128)S(1)} %get-tuple-element.129.own_ref, f32[3,3,12,128]{3,2,1,0:T(8,128)S(1)} %pad_maximum_fusion.7.near_ref, bf16[12,2,3,128,48]{4,3,2,1,0:T(8,128)(2,1)S(1)} %get-tuple-element.82.own_ref.own_bf, ...), custom_call_target="tpu_custom_call" | custom-call | flops 1000000000 | bytes 1000000 | tf_op jit(solution)/shard_map/pallas_call | solution.py:216
  85.0 1.5 collective-permute-start.15
  86.5 7.8 %shard_map.185 = f32[3,2,12,128]{3,2,1,0:T(8,128)S(1)} custom-call(f32[3,2,12,128]{3,2,1,0:T(8,128)S(1)} %get-tuple-element.129.own_ref, f32[3,3,12,128]{3,2,1,0:T(8,128)S(1)} %get-tuple-element.174.near_ref, bf16[12,2,3,128,48]{4,3,2,1,0:T(8,128)(2,1)S(1)} %get-tuple-element.82.own_ref.own_bf, bf16[12,48,384]{2,1,0:T(8,128)(2,1)S(1)} %get-tuple-element.94.near_bf, ...), custom_call_target="tpu_custom_call" | custom-call | flops 1000000000 | bytes 1000000 | tf_op jit(solution)/shard_map/pallas_call | solution.py:216
  94.4 7.9 %shard_map.186 = f32[3,2,12,128]{3,2,1,0:T(8,128)S(1)} custom-call(f32[3,2,12,128]{3,2,1,0:T(8,128)S(1)} %get-tuple-element.129.own_ref, f32[3,6,12,128]{3,2,1,0:T(8,128)S(1)} %pad_maximum_fusion.1.near_ref, bf16[12,2,3,128,48]{4,3,2,1,0:T(8,128)(2,1)S(1)} %get-tuple-element.82.own_ref.own_bf, bf16[12,48,768]{2,1,0:T(8,128)(2,1)S(1)} %get-tuple-element.98.near_bf, ...), custom_call_target="tpu_custom_call" | custom-call | flops 1000000000 | bytes 1000000 | tf_op jit(solution)/shard_map/pallas_call | solution.py:216
  102.3 2.0 %collective-permute-start.16 = (f32[3,2,12,128]{3,2,1,0:T(8,128)S(1)}, f32[3,2,12,128]{3,2,1,0:T(8,128)S(1)}, u32[]{:S(2)}, u32[]{:S(2)}) collective-permute-start(f32[3,2,12,128]{3,2,1,0:T(8,128)S(1)} %get-tuple-element.126.own_ref), channel_id=1, source_target_pairs={{0,8},{8,0},{16,24},{24,16},{32,40},{40,32},{48,56},{56,48},{64,72... | collective-permute-start | bytes 110600 | tf_op jit(solution)/shard_map/ppermute | solution.py:287
  105.3 3.6 %shard_map.187 = (f32[2,12,128]{2,1,0:T(8,128)S(1)}, bf16[12,48,384]{2,1,0:T(8,128)(2,1)S(1)}, bf16[12,2,3,128,48]{4,3,2,1,0:T(8,128)(2,1)S(1)}) custom-call(f32[3,2,12,128]{3,2,1,0:T(8,128)S(1)} %get-tuple-element.126.own_ref, f32[3,3,12,128]{3,2,1,0:T(8,128)S(1)} %pad_maximum_fusion.11.near_ref), custom_call_target="tpu_custom_call" | custom-call | flops 1000000000 | bytes 1000000 | tf_op jit(solution)/shard_map/pallas_call | solution.py:216
  109.3 2.5 %collective-permute-start.19 = (f32[3,3,12,128]{3,2,1,0:T(8,128)S(1)}, f32[3,3,12,128]{3,2,1,0:T(8,128)S(1)}, u32[]{:S(2)}, u32[]{:S(2)}) collective-permute-start(f32[3,3,12,128]{3,2,1,0:T(8,128)S(1)} %get-tuple-element.133), channel_id=1, source_target_pairs={{0,7},{1,2},{2,1},{3,4},{4,3},{5,6},{6,5},{7,0},{8,15},{9,10},{10,... | collective-permute-start | bytes 165896 | tf_op jit(solution)/shard_map/ppermute | solution.py:287
  111.8 2.5 %shard_map.188 = (f32[2,12,128]{2,1,0:T(8,128)S(1)}, bf16[12,48,384]{2,1,0:T(8,128)(2,1)S(1)}) custom-call(bf16[12,2,3,128,48]{4,3,2,1,0:T(8,128)(2,1)S(1)} %get-tuple-element.101.own_ref.own_bf, f32[3,3,12,128]{3,2,1,0:T(8,128)S(1)} %get-tuple-element.173.near_ref), custom_call_target="tpu_custom_call" | custom-call | flops 1000000000 | bytes 1000000 | tf_op jit(solution)/shard_map/pallas_call | solution.py:216
  114.8 2.6 %shard_map.189 = (f32[2,12,128]{2,1,0:T(8,128)S(1)}, bf16[12,48,768]{2,1,0:T(8,128)(2,1)S(1)}) custom-call(bf16[12,2,3,128,48]{4,3,2,1,0:T(8,128)(2,1)S(1)} %get-tuple-element.101.own_ref.own_bf, f32[3,6,12,128]{3,2,1,0:T(8,128)S(1)} %pad_maximum_fusion.2.near_ref), custom_call_target="tpu_custom_call" | custom-call | flops 1000000000 | bytes 1000000 | tf_op jit(solution)/shard_map/pallas_call | solution.py:216
  117.5 4.9 %collective-permute-start.20 = (f32[2,12,128]{2,1,0:T(8,128)S(1)}, f32[2,12,128]{2,1,0:T(8,128)S(1)}, u32[]{:S(2)}, u32[]{:S(2)}) collective-permute-start(f32[2,12,128]{2,1,0:T(8,128)S(1)} %rsqrt_multiply_fusion.own_slope_ref), channel_id=1, source_target_pairs={{0,8},{8,0},{16,24},{24,16},{32,40},{40,32},{48,56},{56,48},{64,72... | collective-permute-start | bytes 36872 | tf_op jit(solution)/shard_map/ppermute | solution.py:287
  123.2 8.4 %shard_map.190 = (f32[3,2,12,128]{3,2,1,0:T(8,128)S(1)}, f32[12,2,128,128]{3,2,1,0:T(8,128)S(1)}) custom-call(f32[3,2,12,128]{3,2,1,0:T(8,128)S(1)} %get-tuple-element.126.own_ref, f32[3,3,12,128]{3,2,1,0:T(8,128)S(1)} %pad_maximum_fusion.11.near_ref, bf16[12,2,3,128,48]{4,3,2,1,0:T(8,128)(2,1)S(1)} %get-tuple-element.101.own_ref.own_bf, ...), custom_call_target="tpu_custom_call" | custom-call | flops 1000000000 | bytes 1000000 | tf_op jit(solution)/shard_map/pallas_call | solution.py:216
  131.7 2.7 %collective-permute-start.23 = (f32[3,12,128]{2,1,0:T(8,128)S(1)}, f32[3,12,128]{2,1,0:T(8,128)S(1)}, u32[]{:S(2)}, u32[]{:S(2)}) collective-permute-start(f32[3,12,128]{2,1,0:T(8,128)S(1)} %get-tuple-element.145), channel_id=1, source_target_pairs={{0,7},{1,2},{2,1},{3,4},{4,3},{5,6},{6,5},{7,0},{8,15},{9,10},{10,... | collective-permute-start | bytes 55304 | tf_op jit(solution)/shard_map/ppermute | solution.py:287
  134.5 7.8 %shard_map.191.refs_1_ = f32[3,2,12,128]{3,2,1,0:T(8,128)S(1)} custom-call(f32[3,2,12,128]{3,2,1,0:T(8,128)S(1)} %get-tuple-element.126.own_ref, f32[3,3,12,128]{3,2,1,0:T(8,128)S(1)} %get-tuple-element.173.near_ref, bf16[12,2,3,128,48]{4,3,2,1,0:T(8,128)(2,1)S(1)} %get-tuple-element.101.own_ref.own_bf, bf16[12,48,384]{2,1,0:T(8,128)(2,1)S(1)} %get-tuple-element.113.near_bf, ...), custom_call_target="tpu_custom_call" | custom-call | flops 1000000000 | bytes 1000000 | tf_op jit(solution)/shard_map/pallas_call | solution.py:216
  142.3 7.9 %shard_map.192.refs_2_ = f32[3,2,12,128]{3,2,1,0:T(8,128)S(1)} custom-call(f32[3,2,12,128]{3,2,1,0:T(8,128)S(1)} %get-tuple-element.126.own_ref, f32[3,6,12,128]{3,2,1,0:T(8,128)S(1)} %pad_maximum_fusion.2.near_ref, bf16[12,2,3,128,48]{4,3,2,1,0:T(8,128)(2,1)S(1)} %get-tuple-element.101.own_ref.own_bf, bf16[12,48,768]{2,1,0:T(8,128)(2,1)S(1)} %get-tuple-element.117.near_bf, ...), custom_call_target="tpu_custom_call" | custom-call | flops 1000000000 | bytes 1000000 | tf_op jit(solution)/shard_map/pallas_call | solution.py:216
  (104 shorter events, 12.0 us)
Async XLA Ops:
  2.2 5.2 %collective-permute-start = (f32[3,2,12,128]{3,2,1,0:T(8,128)S(1)}, f32[3,2,12,128]{3,2,1,0:T(8,128)S(1)}, u32[]{:S(2)}, u32[]{:S(2)}) collective-permute-start(f32[3,2,12,128]{3,2,1,0:T(8,128)S(1)} %fusion.6.own_ref), channel_id=1, source_target_pairs={{0,8},{8,0},{16,24},{24,16},{32,40},{40,32},{48,56},{56,48},{64,72... | collective-permute-start | bytes 110600 | tf_op jit(solution)/shard_map/ppermute | solution.py:287
  5.5 5.7 %collective-permute-start.1 = (f32[3,2,12,128]{3,2,1,0:T(8,128)S(1)}, f32[3,2,12,128]{3,2,1,0:T(8,128)S(1)}, u32[]{:S(2)}, u32[]{:S(2)}) collective-permute-start(f32[3,2,12,128]{3,2,1,0:T(8,128)S(1)} %fusion.6.own_ref), channel_id=1, source_target_pairs={{0,248},{8,16},{16,8},{24,32},{32,24},{40,48},{48,40},{56,64},{64,... | collective-permute-start | bytes 110600 | tf_op jit(solution)/shard_map/ppermute | solution.py:287
  11.1 7.4 %copy-start.3 = (f32[3]{0:T(128)S(1)}, f32[3]{0:T(128)}, u32[]{:S(2)}) copy-start(f32[3]{0:T(128)} %constant.89) | copy-start | bytes 40
  11.1 7.4 %copy-start.4 = (f32[3]{0:T(128)S(1)}, f32[3]{0:T(128)}, u32[]{:S(2)}) copy-start(f32[3]{0:T(128)} %constant.90) | copy-start | bytes 40
  11.3 6.8 %collective-permute-start.2 = (f32[3,3,12,128]{3,2,1,0:T(8,128)S(1)}, f32[3,3,12,128]{3,2,1,0:T(8,128)S(1)}, u32[]{:S(2)}, u32[]{:S(2)}) collective-permute-start(f32[3,3,12,128]{3,2,1,0:T(8,128)S(1)} %get-tuple-element.142), channel_id=1, source_target_pairs={{0,1},{1,0},{2,3},{3,2},{4,5},{5,4},{6,7},{7,6},{8,9},{9,8},{10,11... | collective-permute-start | bytes 165896 | tf_op jit(solution)/shard_map/ppermute | solution.py:287
  13.0 5.5 %collective-permute-start.3 = (f32[3,3,12,128]{3,2,1,0:T(8,128)S(1)}, f32[3,3,12,128]{3,2,1,0:T(8,128)S(1)}, u32[]{:S(2)}, u32[]{:S(2)}) collective-permute-start(f32[3,3,12,128]{3,2,1,0:T(8,128)S(1)} %get-tuple-element.141), channel_id=1, source_target_pairs={{0,7},{1,2},{2,1},{3,4},{4,3},{5,6},{6,5},{7,0},{8,15},{9,10},{10,... | collective-permute-start | bytes 165896 | tf_op jit(solution)/shard_map/ppermute | solution.py:287
  21.3 7.0 %collective-permute-start.4 = (f32[2,12,128]{2,1,0:T(8,128)S(1)}, f32[2,12,128]{2,1,0:T(8,128)S(1)}, u32[]{:S(2)}, u32[]{:S(2)}) collective-permute-start(f32[2,12,128]{2,1,0:T(8,128)S(1)} %rsqrt_multiply_fusion.2.own_slope_ref), channel_id=1, source_target_pairs={{0,8},{8,0},{16,24},{24,16},{32,40},{40,32},{48,56},{56,48},{64,72... | collective-permute-start | bytes 36872 | tf_op jit(solution)/shard_map/ppermute | solution.py:287
  27.4 9.3 %collective-permute-start.5 = (f32[2,12,128]{2,1,0:T(8,128)S(1)}, f32[2,12,128]{2,1,0:T(8,128)S(1)}, u32[]{:S(2)}, u32[]{:S(2)}) collective-permute-start(f32[2,12,128]{2,1,0:T(8,128)S(1)} %rsqrt_multiply_fusion.2.own_slope_ref), channel_id=1, source_target_pairs={{0,248},{8,16},{16,8},{24,32},{32,24},{40,48},{48,40},{56,64},{64,... | collective-permute-start | bytes 36872 | tf_op jit(solution)/shard_map/ppermute | solution.py:287
  36.7 11.1 %collective-permute-start.6 = (f32[3,12,128]{2,1,0:T(8,128)S(1)}, f32[3,12,128]{2,1,0:T(8,128)S(1)}, u32[]{:S(2)}, u32[]{:S(2)}) collective-permute-start(f32[3,12,128]{2,1,0:T(8,128)S(1)} %get-tuple-element.166), channel_id=1, source_target_pairs={{0,1},{1,0},{2,3},{3,2},{4,5},{5,4},{6,7},{7,6},{8,9},{9,8},{10,11... | collective-permute-start | bytes 55304 | tf_op jit(solution)/shard_map/ppermute | solution.py:287
  36.8 11.0 %collective-permute-start.7 = (f32[3,12,128]{2,1,0:T(8,128)S(1)}, f32[3,12,128]{2,1,0:T(8,128)S(1)}, u32[]{:S(2)}, u32[]{:S(2)}) collective-permute-start(f32[3,12,128]{2,1,0:T(8,128)S(1)} %get-tuple-element.165), channel_id=1, source_target_pairs={{0,7},{1,2},{2,1},{3,4},{4,3},{5,6},{6,5},{7,0},{8,15},{9,10},{10,... | collective-permute-start | bytes 55304 | tf_op jit(solution)/shard_map/ppermute | solution.py:287
  47.9 7.9 %copy-start = (f32[3,1,2,12,128]{4,2,3,1,0:T(2,128)S(1)}, f32[3,1,2,12,128]{4,2,3,1,0:T(2,128)}, u32[]{:S(2)}) copy-start(f32[3,1,2,12,128]{4,2,3,1,0:T(2,128)} %param.16) | copy-start | bytes 110596
  47.9 7.9 %copy-start.1 = (f32[3,1,2,12,128]{4,2,3,1,0:T(2,128)S(1)}, f32[3,1,2,12,128]{4,2,3,1,0:T(2,128)}, u32[]{:S(2)}) copy-start(f32[3,1,2,12,128]{4,2,3,1,0:T(2,128)} %param.17) | copy-start | bytes 110596
  47.9 7.9 %copy-start.2 = (f32[3,2]{1,0:T(4,128)S(1)}, f32[3,2]{1,0:T(4,128)}, u32[]{:S(2)}) copy-start(f32[3,2]{1,0:T(4,128)} %constant.88) | copy-start | bytes 76
  55.9 2.6 %collective-permute-start.8 = (f32[3,2,12,128]{3,2,1,0:T(8,128)S(1)}, f32[3,2,12,128]{3,2,1,0:T(8,128)S(1)}, u32[]{:S(2)}, u32[]{:S(2)}) collective-permute-start(f32[3,2,12,128]{3,2,1,0:T(8,128)S(1)} %get-tuple-element.129.own_ref), channel_id=1, source_target_pairs={{0,8},{8,0},{16,24},{24,16},{32,40},{40,32},{48,56},{56,48},{64,72... | collective-permute-start | bytes 110600 | tf_op jit(solution)/shard_map/ppermute | solution.py:287
  57.6 4.6 %collective-permute-start.9 = (f32[3,2,12,128]{3,2,1,0:T(8,128)S(1)}, f32[3,2,12,128]{3,2,1,0:T(8,128)S(1)}, u32[]{:S(2)}, u32[]{:S(2)}) collective-permute-start(f32[3,2,12,128]{3,2,1,0:T(8,128)S(1)} %get-tuple-element.129.own_ref), channel_id=1, source_target_pairs={{0,248},{8,16},{16,8},{24,32},{32,24},{40,48},{48,40},{56,64},{64,... | collective-permute-start | bytes 110600 | tf_op jit(solution)/shard_map/ppermute | solution.py:287
  62.3 4.4 %collective-permute-start.10 = (f32[3,3,12,128]{3,2,1,0:T(8,128)S(1)}, f32[3,3,12,128]{3,2,1,0:T(8,128)S(1)}, u32[]{:S(2)}, u32[]{:S(2)}) collective-permute-start(f32[3,3,12,128]{3,2,1,0:T(8,128)S(1)} %get-tuple-element.138), channel_id=1, source_target_pairs={{0,1},{1,0},{2,3},{3,2},{4,5},{5,4},{6,7},{7,6},{8,9},{9,8},{10,11... | collective-permute-start | bytes 165896 | tf_op jit(solution)/shard_map/ppermute | solution.py:287
  62.6 5.4 %collective-permute-start.11 = (f32[3,3,12,128]{3,2,1,0:T(8,128)S(1)}, f32[3,3,12,128]{3,2,1,0:T(8,128)S(1)}, u32[]{:S(2)}, u32[]{:S(2)}) collective-permute-start(f32[3,3,12,128]{3,2,1,0:T(8,128)S(1)} %get-tuple-element.137), channel_id=1, source_target_pairs={{0,7},{1,2},{2,1},{3,4},{4,3},{5,6},{6,5},{7,0},{8,15},{9,10},{10,... | collective-permute-start | bytes 165896 | tf_op jit(solution)/shard_map/ppermute | solution.py:287
  70.8 5.3 %collective-permute-start.12 = (f32[2,12,128]{2,1,0:T(8,128)S(1)}, f32[2,12,128]{2,1,0:T(8,128)S(1)}, u32[]{:S(2)}, u32[]{:S(2)}) collective-permute-start(f32[2,12,128]{2,1,0:T(8,128)S(1)} %rsqrt_multiply_fusion.1.own_slope_ref), channel_id=1, source_target_pairs={{0,8},{8,0},{16,24},{24,16},{32,40},{40,32},{48,56},{56,48},{64,72... | collective-permute-start | bytes 36872 | tf_op jit(solution)/shard_map/ppermute | solution.py:287
  75.2 9.3 %collective-permute-start.13 = (f32[2,12,128]{2,1,0:T(8,128)S(1)}, f32[2,12,128]{2,1,0:T(8,128)S(1)}, u32[]{:S(2)}, u32[]{:S(2)}) collective-permute-start(f32[2,12,128]{2,1,0:T(8,128)S(1)} %rsqrt_multiply_fusion.1.own_slope_ref), channel_id=1, source_target_pairs={{0,248},{8,16},{16,8},{24,32},{32,24},{40,48},{48,40},{56,64},{64,... | collective-permute-start | bytes 36872 | tf_op jit(solution)/shard_map/ppermute | solution.py:287
  84.5 9.8 %collective-permute-start.14 = (f32[3,12,128]{2,1,0:T(8,128)S(1)}, f32[3,12,128]{2,1,0:T(8,128)S(1)}, u32[]{:S(2)}, u32[]{:S(2)}) collective-permute-start(f32[3,12,128]{2,1,0:T(8,128)S(1)} %get-tuple-element.156), channel_id=1, source_target_pairs={{0,1},{1,0},{2,3},{3,2},{4,5},{5,4},{6,7},{7,6},{8,9},{9,8},{10,11... | collective-permute-start | bytes 55304 | tf_op jit(solution)/shard_map/ppermute | solution.py:287
  85.0 9.3 %collective-permute-start.15 = (f32[3,12,128]{2,1,0:T(8,128)S(1)}, f32[3,12,128]{2,1,0:T(8,128)S(1)}, u32[]{:S(2)}, u32[]{:S(2)}) collective-permute-start(f32[3,12,128]{2,1,0:T(8,128)S(1)} %get-tuple-element.155), channel_id=1, source_target_pairs={{0,7},{1,2},{2,1},{3,4},{4,3},{5,6},{6,5},{7,0},{8,15},{9,10},{10,... | collective-permute-start | bytes 55304 | tf_op jit(solution)/shard_map/ppermute | solution.py:287
  102.3 2.9 %collective-permute-start.16 = (f32[3,2,12,128]{3,2,1,0:T(8,128)S(1)}, f32[3,2,12,128]{3,2,1,0:T(8,128)S(1)}, u32[]{:S(2)}, u32[]{:S(2)}) collective-permute-start(f32[3,2,12,128]{3,2,1,0:T(8,128)S(1)} %get-tuple-element.126.own_ref), channel_id=1, source_target_pairs={{0,8},{8,0},{16,24},{24,16},{32,40},{40,32},{48,56},{56,48},{64,72... | collective-permute-start | bytes 110600 | tf_op jit(solution)/shard_map/ppermute | solution.py:287
  104.3 4.8 %collective-permute-start.17 = (f32[3,2,12,128]{3,2,1,0:T(8,128)S(1)}, f32[3,2,12,128]{3,2,1,0:T(8,128)S(1)}, u32[]{:S(2)}, u32[]{:S(2)}) collective-permute-start(f32[3,2,12,128]{3,2,1,0:T(8,128)S(1)} %get-tuple-element.126.own_ref), channel_id=1, source_target_pairs={{0,248},{8,16},{16,8},{24,32},{32,24},{40,48},{48,40},{56,64},{64,... | collective-permute-start | bytes 110600 | tf_op jit(solution)/shard_map/ppermute | solution.py:287
  109.2 5.1 %collective-permute-start.18 = (f32[3,3,12,128]{3,2,1,0:T(8,128)S(1)}, f32[3,3,12,128]{3,2,1,0:T(8,128)S(1)}, u32[]{:S(2)}, u32[]{:S(2)}) collective-permute-start(f32[3,3,12,128]{3,2,1,0:T(8,128)S(1)} %get-tuple-element.134), channel_id=1, source_target_pairs={{0,1},{1,0},{2,3},{3,2},{4,5},{5,4},{6,7},{7,6},{8,9},{9,8},{10,11... | collective-permute-start | bytes 165896 | tf_op jit(solution)/shard_map/ppermute | solution.py:287
  109.3 5.4 %collective-permute-start.19 = (f32[3,3,12,128]{3,2,1,0:T(8,128)S(1)}, f32[3,3,12,128]{3,2,1,0:T(8,128)S(1)}, u32[]{:S(2)}, u32[]{:S(2)}) collective-permute-start(f32[3,3,12,128]{3,2,1,0:T(8,128)S(1)} %get-tuple-element.133), channel_id=1, source_target_pairs={{0,7},{1,2},{2,1},{3,4},{4,3},{5,6},{6,5},{7,0},{8,15},{9,10},{10,... | collective-permute-start | bytes 165896 | tf_op jit(solution)/shard_map/ppermute | solution.py:287
  117.5 5.7 %collective-permute-start.20 = (f32[2,12,128]{2,1,0:T(8,128)S(1)}, f32[2,12,128]{2,1,0:T(8,128)S(1)}, u32[]{:S(2)}, u32[]{:S(2)}) collective-permute-start(f32[2,12,128]{2,1,0:T(8,128)S(1)} %rsqrt_multiply_fusion.own_slope_ref), channel_id=1, source_target_pairs={{0,8},{8,0},{16,24},{24,16},{32,40},{40,32},{48,56},{56,48},{64,72... | collective-permute-start | bytes 36872 | tf_op jit(solution)/shard_map/ppermute | solution.py:287
  122.4 9.2 %collective-permute-start.21 = (f32[2,12,128]{2,1,0:T(8,128)S(1)}, f32[2,12,128]{2,1,0:T(8,128)S(1)}, u32[]{:S(2)}, u32[]{:S(2)}) collective-permute-start(f32[2,12,128]{2,1,0:T(8,128)S(1)} %rsqrt_multiply_fusion.own_slope_ref), channel_id=1, source_target_pairs={{0,248},{8,16},{16,8},{24,32},{32,24},{40,48},{48,40},{56,64},{64,... | collective-permute-start | bytes 36872 | tf_op jit(solution)/shard_map/ppermute | solution.py:287
  131.6 10.6 %collective-permute-start.22 = (f32[3,12,128]{2,1,0:T(8,128)S(1)}, f32[3,12,128]{2,1,0:T(8,128)S(1)}, u32[]{:S(2)}, u32[]{:S(2)}) collective-permute-start(f32[3,12,128]{2,1,0:T(8,128)S(1)} %get-tuple-element.146), channel_id=1, source_target_pairs={{0,1},{1,0},{2,3},{3,2},{4,5},{5,4},{6,7},{7,6},{8,9},{9,8},{10,11... | collective-permute-start | bytes 55304 | tf_op jit(solution)/shard_map/ppermute | solution.py:287
  131.7 10.5 %collective-permute-start.23 = (f32[3,12,128]{2,1,0:T(8,128)S(1)}, f32[3,12,128]{2,1,0:T(8,128)S(1)}, u32[]{:S(2)}, u32[]{:S(2)}) collective-permute-start(f32[3,12,128]{2,1,0:T(8,128)S(1)} %get-tuple-element.145), channel_id=1, source_target_pairs={{0,7},{1,2},{2,1},{3,4},{4,3},{5,6},{6,5},{7,0},{8,15},{9,10},{10,... | collective-permute-start | bytes 55304 | tf_op jit(solution)/shard_map/ppermute | solution.py:287
  142.3 7.9 %copy-start.5 = (s32[1,2,12]{2,1,0:T(2,128)S(1)}, s32[1,2,12]{2,1,0:T(2,128)}, u32[]{:S(2)}) copy-start(s32[1,2,12]{2,1,0:T(2,128)} %param.18) | copy-start | bytes 292

commit v4 on v3

--- a/solution.py
+++ b/solution.py
@@ -69,7 +69,7 @@
                 own_bf[c, iy, r] = features.T.astype(jnp.bfloat16)
         return carry
 
-    lax.fori_loop(0, NZ, per_cell, 0, unroll=2)
+    lax.fori_loop(0, NZ, per_cell, 0, unroll=4)
 
 
 def slab_of(c, r):
@@ -202,7 +202,7 @@
         return carry
 
     sums_b[...] = jnp.zeros((4, SLOTS, SLOTS), jnp.float32)
-    lax.fori_loop(0, NZ, per_cell, 0)
+    lax.fori_loop(0, NZ, per_cell, 0, unroll=2)
     fold(NZ - 1, 1)
 
 
@@ -258,11 +258,10 @@
     )
 
 
-def finish_kernel(counts_ref, position_ref, velocity_ref, *refs):
+def finish_kernel(mark_ref, position_ref, velocity_ref, *refs):
     *parts, position_out, velocity_out, force_out = refs
-    lane = lax.broadcasted_iota(jnp.int32, (NZ, SLOTS), 1)
     for iy in range(2):
-        present = lane < counts_ref[iy]
+        present = mark_ref[iy] < 0.5 * FAR
         for k in range(3):
             force = jnp.where(present, sum(part[k, iy] for part in parts), 0.0)
             force_out[k, :, iy, :] = force
@@ -270,14 +269,13 @@
             position_out[k, :, iy, :] = position_ref[k, iy]
 
 
-def finish(positions, velocities, counts, parts):
-    counts = jnp.broadcast_to(counts[..., None], (2, NZ, SLOTS))
+def finish(positions, velocities, mark, parts):
     outs = pl.pallas_call(
         finish_kernel,
         out_shape=[jax.ShapeDtypeStruct((3, NZ, 2, SLOTS), jnp.float32)] * 3,
         in_specs=[VMEM] * (3 + len(parts)),
         compiler_params=pltpu.CompilerParams(vmem_limit_bytes=8 * 2**20),
-    )(counts, positions, velocities, *parts)
+    )(mark, positions, velocities, *parts)
     return tuple(out.transpose(0, 2, 1, 3)[:, None] for out in outs)
 
 
@@ -300,8 +298,8 @@
 def exchange_y(value):
     even = lax.axis_index("gy") % 2 == 0
     first, last = value
+    far = swap(jnp.where(even, first, last), "gy", 1)
     near = swap(jnp.where(even, last, first), "gy", 0)
-    far = swap(jnp.where(even, first, last), "gy", 1)
     return near, far
 
 
@@ -318,7 +316,6 @@
 def shards(positions, velocities, counts):
     positions, velocities = positions[:, 0], velocities[:, 0]
     places = lax.broadcasted_iota(jnp.int32, (2, NZ, SLOTS), 2)
-    present = (places < counts[0][..., None])[None]
     frame = jnp.stack(
         [
             jnp.full((2, 1, 1), -0.5, jnp.float32),
@@ -328,8 +325,7 @@
     )
     side = jnp.where(lax.axis_index("gx") % 2 == 0, 1.0, -1.0)
 
-    def forces_of(positions):
-        own = jnp.where(present, positions + frame, FAR)
+    def forces_of(own):
         near, far = exchange_x(own)
         near = near + along(0, side)
         inner = jnp.concatenate([own, near[:, :1]], axis=1)
@@ -357,17 +353,18 @@
         (last,) = force_part(own, outer, own_bf, outer_bf, turned, outer_slope, OUTER)
         return force, part, last
 
-    parts = forces_of(positions)
+    own = jnp.where((places < counts[0][..., None])[None], positions + frame, FAR)
+    mark = own[0]
+    present = (mark < 0.5 * FAR)[None]
+    parts = forces_of(own)
     for step in range(STEPS):
+        pushed = jnp.where(present, sum(parts), 0.0)
         if step:
-            pushed = jnp.where(present, sum(parts), 0.0)
             velocities = velocities + 0.5 * TIME_STEP * pushed
-        else:
-            pushed = jnp.where(present, sum(parts), 0.0)
         velocities = velocities + 0.5 * TIME_STEP * pushed
         positions = positions + TIME_STEP * velocities
-        parts = forces_of(positions)
-    return finish(positions, velocities, counts[0], parts)
+        parts = forces_of(jnp.where(present, positions + frame, FAR))
+    return finish(positions, velocities, mark, parts)
 
 
 def solution(mesh):

time: 151 us -> 149 us (0.987)
  Pallas kernels: 99.1 us -> 97.2 us
    pallas_call x18, Pallas kernels: 98.4 us -> 96.4 us  [call(): pl.pallas_call(kernel, out_shape=out_shape, in_specs=[VMEM] * len(operand...]
  transfers between devices with their start and end apart: 24 -> 24, of which waited for: 9 -> 10; matrix products, arithmetic and copies ran while one was open for 1% -> 1% of each run, Pallas kernels for 44% -> 44%
where the time goes in v4:
time: 149 us
  Pallas kernels  97.2 us (65%)
  starting transfers between devices  41.4 us (28%)
  waiting for transfers between devices  6.06 us (4%)
  other arithmetic  3.4 us (2%)
    pallas_call x18, Pallas kernels, call(): pl.pallas_call(kernel, out_shape=out_shape, in_specs=[VMEM] * len(operand...  96.4 us
    ppermute x24, starting transfers between devices, swap(): return lax.ppermute(value, axis, [(i, partner[i]) for i in range(n)])  41.4 us
    ppermute x24, waiting for transfers between devices, swap(): return lax.ppermute(value, axis, [(i, partner[i]) for i in range(n)])  6.06 us
  transfers between devices with their start and end apart: 24, of which 10 were waited for; matrix products, arithmetic and copies ran while one was open for 1% of the time, Pallas kernels for 44%

profile of v4, /device:TPU:1, one launch (start us, length us, event | category | flops | bytes accessed | tf_op | source)
XLA Modules:
  0.0 149.3 jit_solution(10533014407790365456)
XLA Ops:
  2.2 3.2 %collective-permute-start = (f32[3,2,12,128]{3,2,1,0:T(8,128)S(1)}, f32[3,2,12,128]{3,2,1,0:T(8,128)S(1)}, u32[]{:S(2)}, u32[]{:S(2)}) collective-permute-start(f32[3,2,12,128]{3,2,1,0:T(8,128)S(1)} %fusion.6.own_ref), channel_id=1, source_target_pairs={{0,8},{8,0},{16,24},{24,16},{32,40},{40,32},{48,56},{56,48},{64,72... | collective-permute-start | bytes 110600 | tf_op jit(solution)/shard_map/ppermute | solution.py:285
  5.5 1.3 collective-permute-start.1
  7.5 3.4 %shard_map.175 = (f32[2,12,128]{2,1,0:T(8,128)S(1)}, bf16[12,48,384]{2,1,0:T(8,128)(2,1)S(1)}, bf16[12,2,3,128,48]{4,3,2,1,0:T(8,128)(2,1)S(1)}) custom-call(f32[3,2,12,128]{3,2,1,0:T(8,128)S(1)} %fusion.6.own_ref, f32[3,3,12,128]{3,2,1,0:T(8,128)S(1)} %pad_maximum_fusion.3.near_ref), custom_call_target="tpu_custom_call" | custom-call | flops 1000000000 | bytes 1000000 | tf_op jit(solution)/shard_map/pallas_call | solution.py:216
  11.1 1.7 %collective-permute-start.2 = (f32[3,3,12,128]{3,2,1,0:T(8,128)S(1)}, f32[3,3,12,128]{3,2,1,0:T(8,128)S(1)}, u32[]{:S(2)}, u32[]{:S(2)}) collective-permute-start(f32[3,3,12,128]{3,2,1,0:T(8,128)S(1)} %get-tuple-element.142), channel_id=1, source_target_pairs={{0,1},{1,0},{2,3},{3,2},{4,5},{5,4},{6,7},{7,6},{8,9},{9,8},{10,11... | collective-permute-start | bytes 165896 | tf_op jit(solution)/shard_map/ppermute | solution.py:285
  12.8 2.5 %collective-permute-start.3 = (f32[3,3,12,128]{3,2,1,0:T(8,128)S(1)}, f32[3,3,12,128]{3,2,1,0:T(8,128)S(1)}, u32[]{:S(2)}, u32[]{:S(2)}) collective-permute-start(f32[3,3,12,128]{3,2,1,0:T(8,128)S(1)} %get-tuple-element.141), channel_id=1, source_target_pairs={{0,7},{1,2},{2,1},{3,4},{4,3},{5,6},{6,5},{7,0},{8,15},{9,10},{10,... | collective-permute-start | bytes 165896 | tf_op jit(solution)/shard_map/ppermute | solution.py:285
  15.3 2.5 %shard_map.176 = (f32[2,12,128]{2,1,0:T(8,128)S(1)}, bf16[12,48,384]{2,1,0:T(8,128)(2,1)S(1)}) custom-call(bf16[12,2,3,128,48]{4,3,2,1,0:T(8,128)(2,1)S(1)} %get-tuple-element.63.own_ref.own_bf, f32[3,3,12,128]{3,2,1,0:T(8,128)S(1)} %get-tuple-element.175.near_ref), custom_call_target="tpu_custom_call" | custom-call | flops 1000000000 | bytes 1000000 | tf_op jit(solution)/shard_map/pallas_call | solution.py:216
  18.4 2.6 %shard_map.177 = (f32[2,12,128]{2,1,0:T(8,128)S(1)}, bf16[12,48,768]{2,1,0:T(8,128)(2,1)S(1)}) custom-call(bf16[12,2,3,128,48]{4,3,2,1,0:T(8,128)(2,1)S(1)} %get-tuple-element.63.own_ref.own_bf, f32[3,6,12,128]{3,2,1,0:T(8,128)S(1)} %pad_maximum_fusion.near_ref), custom_call_target="tpu_custom_call" | custom-call | flops 1000000000 | bytes 1000000 | tf_op jit(solution)/shard_map/pallas_call | solution.py:216
  21.1 6.2 %collective-permute-start.4 = (f32[2,12,128]{2,1,0:T(8,128)S(1)}, f32[2,12,128]{2,1,0:T(8,128)S(1)}, u32[]{:S(2)}, u32[]{:S(2)}) collective-permute-start(f32[2,12,128]{2,1,0:T(8,128)S(1)} %rsqrt_multiply_fusion.2.own_slope_ref), channel_id=1, source_target_pairs={{0,8},{8,0},{16,24},{24,16},{32,40},{40,32},{48,56},{56,48},{64,72... | collective-permute-start | bytes 36872 | tf_op jit(solution)/shard_map/ppermute | solution.py:285
  28.1 8.3 %shard_map.178 = (f32[3,2,12,128]{3,2,1,0:T(8,128)S(1)}, f32[12,2,128,128]{3,2,1,0:T(8,128)S(1)}) custom-call(f32[3,2,12,128]{3,2,1,0:T(8,128)S(1)} %fusion.6.own_ref, f32[3,3,12,128]{3,2,1,0:T(8,128)S(1)} %pad_maximum_fusion.3.near_ref, bf16[12,2,3,128,48]{4,3,2,1,0:T(8,128)(2,1)S(1)} %get-tuple-element.63.own_ref.own_bf, ...), custom_call_target="tpu_custom_call" | custom-call | flops 1000000000 | bytes 1000000 | tf_op jit(solution)/shard_map/pallas_call | solution.py:216
  36.5 3.1 %collective-permute-start.7 = (f32[3,12,128]{2,1,0:T(8,128)S(1)}, f32[3,12,128]{2,1,0:T(8,128)S(1)}, u32[]{:S(2)}, u32[]{:S(2)}) collective-permute-start(f32[3,12,128]{2,1,0:T(8,128)S(1)} %get-tuple-element.165), channel_id=1, source_target_pairs={{0,7},{1,2},{2,1},{3,4},{4,3},{5,6},{6,5},{7,0},{8,15},{9,10},{10,... | collective-permute-start | bytes 55304 | tf_op jit(solution)/shard_map/ppermute | solution.py:285
  39.6 7.6 %shard_map.179 = f32[3,2,12,128]{3,2,1,0:T(8,128)S(1)} custom-call(f32[3,2,12,128]{3,2,1,0:T(8,128)S(1)} %fusion.6.own_ref, f32[3,3,12,128]{3,2,1,0:T(8,128)S(1)} %get-tuple-element.175.near_ref, bf16[12,2,3,128,48]{4,3,2,1,0:T(8,128)(2,1)S(1)} %get-tuple-element.63.own_ref.own_bf, bf16[12,48,384]{2,1,0:T(8,128)(2,1)S(1)} %get-tuple-element.75.near_bf, ...), custom_call_target="tpu_custom_call" | custom-call | flops 1000000000 | bytes 1000000 | tf_op jit(solution)/shard_map/pallas_call | solution.py:216
  47.3 7.8 %shard_map.180 = f32[3,2,12,128]{3,2,1,0:T(8,128)S(1)} custom-call(f32[3,2,12,128]{3,2,1,0:T(8,128)S(1)} %fusion.6.own_ref, f32[3,6,12,128]{3,2,1,0:T(8,128)S(1)} %pad_maximum_fusion.near_ref, bf16[12,2,3,128,48]{4,3,2,1,0:T(8,128)(2,1)S(1)} %get-tuple-element.63.own_ref.own_bf, bf16[12,48,768]{2,1,0:T(8,128)(2,1)S(1)} %get-tuple-element.79.near_bf, ...), custom_call_target="tpu_custom_call" | custom-call | flops 1000000000 | bytes 1000000 | tf_op jit(solution)/shard_map/pallas_call | solution.py:216
  55.2 2.1 %collective-permute-start.8 = (f32[3,2,12,128]{3,2,1,0:T(8,128)S(1)}, f32[3,2,12,128]{3,2,1,0:T(8,128)S(1)}, u32[]{:S(2)}, u32[]{:S(2)}) collective-permute-start(f32[3,2,12,128]{3,2,1,0:T(8,128)S(1)} %get-tuple-element.129.own_ref), channel_id=1, source_target_pairs={{0,8},{8,0},{16,24},{24,16},{32,40},{40,32},{48,56},{56,48},{64,72... | collective-permute-start | bytes 110600 | tf_op jit(solution)/shard_map/ppermute | solution.py:285
  58.3 3.4 %shard_map.181 = (f32[2,12,128]{2,1,0:T(8,128)S(1)}, bf16[12,48,384]{2,1,0:T(8,128)(2,1)S(1)}, bf16[12,2,3,128,48]{4,3,2,1,0:T(8,128)(2,1)S(1)}) custom-call(f32[3,2,12,128]{3,2,1,0:T(8,128)S(1)} %get-tuple-element.129.own_ref, f32[3,3,12,128]{3,2,1,0:T(8,128)S(1)} %pad_maximum_fusion.7.near_ref), custom_call_target="tpu_custom_call" | custom-call | flops 1000000000 | bytes 1000000 | tf_op jit(solution)/shard_map/pallas_call | solution.py:216
  61.9 2.0 %collective-permute-start.11 = (f32[3,3,12,128]{3,2,1,0:T(8,128)S(1)}, f32[3,3,12,128]{3,2,1,0:T(8,128)S(1)}, u32[]{:S(2)}, u32[]{:S(2)}) collective-permute-start(f32[3,3,12,128]{3,2,1,0:T(8,128)S(1)} %get-tuple-element.137), channel_id=1, source_target_pairs={{0,7},{1,2},{2,1},{3,4},{4,3},{5,6},{6,5},{7,0},{8,15},{9,10},{10,... | collective-permute-start | bytes 165896 | tf_op jit(solution)/shard_map/ppermute | solution.py:285
  63.9 2.5 %shard_map.182 = (f32[2,12,128]{2,1,0:T(8,128)S(1)}, bf16[12,48,384]{2,1,0:T(8,128)(2,1)S(1)}) custom-call(bf16[12,2,3,128,48]{4,3,2,1,0:T(8,128)(2,1)S(1)} %get-tuple-element.82.own_ref.own_bf, f32[3,3,12,128]{3,2,1,0:T(8,128)S(1)} %get-tuple-element.174.near_ref), custom_call_target="tpu_custom_call" | custom-call | flops 1000000000 | bytes 1000000 | tf_op jit(solution)/shard_map/pallas_call | solution.py:216
  67.4 2.6 %shard_map.183 = (f32[2,12,128]{2,1,0:T(8,128)S(1)}, bf16[12,48,768]{2,1,0:T(8,128)(2,1)S(1)}) custom-call(bf16[12,2,3,128,48]{4,3,2,1,0:T(8,128)(2,1)S(1)} %get-tuple-element.82.own_ref.own_bf, f32[3,6,12,128]{3,2,1,0:T(8,128)S(1)} %pad_maximum_fusion.1.near_ref), custom_call_target="tpu_custom_call" | custom-call | flops 1000000000 | bytes 1000000 | tf_op jit(solution)/shard_map/pallas_call | solution.py:216
  70.1 4.7 %collective-permute-start.12 = (f32[2,12,128]{2,1,0:T(8,128)S(1)}, f32[2,12,128]{2,1,0:T(8,128)S(1)}, u32[]{:S(2)}, u32[]{:S(2)}) collective-permute-start(f32[2,12,128]{2,1,0:T(8,128)S(1)} %rsqrt_multiply_fusion.1.own_slope_ref), channel_id=1, source_target_pairs={{0,8},{8,0},{16,24},{24,16},{32,40},{40,32},{48,56},{56,48},{64,72... | collective-permute-start | bytes 36872 | tf_op jit(solution)/shard_map/ppermute | solution.py:285
  75.6 8.2 %shard_map.184 = (f32[3,2,12,128]{3,2,1,0:T(8,128)S(1)}, f32[12,2,128,128]{3,2,1,0:T(8,128)S(1)}) custom-call(f32[3,2,12,128]{3,2,1,0:T(8,128)S(1)} %get-tuple-element.129.own_ref, f32[3,3,12,128]{3,2,1,0:T(8,128)S(1)} %pad_maximum_fusion.7.near_ref, bf16[12,2,3,128,48]{4,3,2,1,0:T(8,128)(2,1)S(1)} %get-tuple-element.82.own_ref.own_bf, ...), custom_call_target="tpu_custom_call" | custom-call | flops 1000000000 | bytes 1000000 | tf_op jit(solution)/shard_map/pallas_call | solution.py:216
  84.4 1.3 collective-permute-start.15
  85.7 7.6 %shard_map.185 = f32[3,2,12,128]{3,2,1,0:T(8,128)S(1)} custom-call(f32[3,2,12,128]{3,2,1,0:T(8,128)S(1)} %get-tuple-element.129.own_ref, f32[3,3,12,128]{3,2,1,0:T(8,128)S(1)} %get-tuple-element.174.near_ref, bf16[12,2,3,128,48]{4,3,2,1,0:T(8,128)(2,1)S(1)} %get-tuple-element.82.own_ref.own_bf, bf16[12,48,384]{2,1,0:T(8,128)(2,1)S(1)} %get-tuple-element.94.near_bf, ...), custom_call_target="tpu_custom_call" | custom-call | flops 1000000000 | bytes 1000000 | tf_op jit(solution)/shard_map/pallas_call | solution.py:216
  93.4 7.8 %shard_map.186 = f32[3,2,12,128]{3,2,1,0:T(8,128)S(1)} custom-call(f32[3,2,12,128]{3,2,1,0:T(8,128)S(1)} %get-tuple-element.129.own_ref, f32[3,6,12,128]{3,2,1,0:T(8,128)S(1)} %pad_maximum_fusion.1.near_ref, bf16[12,2,3,128,48]{4,3,2,1,0:T(8,128)(2,1)S(1)} %get-tuple-element.82.own_ref.own_bf, bf16[12,48,768]{2,1,0:T(8,128)(2,1)S(1)} %get-tuple-element.98.near_bf, ...), custom_call_target="tpu_custom_call" | custom-call | flops 1000000000 | bytes 1000000 | tf_op jit(solution)/shard_map/pallas_call | solution.py:216
  101.3 2.0 %collective-permute-start.16 = (f32[3,2,12,128]{3,2,1,0:T(8,128)S(1)}, f32[3,2,12,128]{3,2,1,0:T(8,128)S(1)}, u32[]{:S(2)}, u32[]{:S(2)}) collective-permute-start(f32[3,2,12,128]{3,2,1,0:T(8,128)S(1)} %get-tuple-element.126.own_ref), channel_id=1, source_target_pairs={{0,8},{8,0},{16,24},{24,16},{32,40},{40,32},{48,56},{56,48},{64,72... | collective-permute-start | bytes 110600 | tf_op jit(solution)/shard_map/ppermute | solution.py:285
  104.3 3.4 %shard_map.187 = (f32[2,12,128]{2,1,0:T(8,128)S(1)}, bf16[12,48,384]{2,1,0:T(8,128)(2,1)S(1)}, bf16[12,2,3,128,48]{4,3,2,1,0:T(8,128)(2,1)S(1)}) custom-call(f32[3,2,12,128]{3,2,1,0:T(8,128)S(1)} %get-tuple-element.126.own_ref, f32[3,3,12,128]{3,2,1,0:T(8,128)S(1)} %pad_maximum_fusion.11.near_ref), custom_call_target="tpu_custom_call" | custom-call | flops 1000000000 | bytes 1000000 | tf_op jit(solution)/shard_map/pallas_call | solution.py:216
  108.3 2.0 %collective-permute-start.19 = (f32[3,3,12,128]{3,2,1,0:T(8,128)S(1)}, f32[3,3,12,128]{3,2,1,0:T(8,128)S(1)}, u32[]{:S(2)}, u32[]{:S(2)}) collective-permute-start(f32[3,3,12,128]{3,2,1,0:T(8,128)S(1)} %get-tuple-element.133), channel_id=1, source_target_pairs={{0,7},{1,2},{2,1},{3,4},{4,3},{5,6},{6,5},{7,0},{8,15},{9,10},{10,... | collective-permute-start | bytes 165896 | tf_op jit(solution)/shard_map/ppermute | solution.py:285
  110.3 2.5 %shard_map.188 = (f32[2,12,128]{2,1,0:T(8,128)S(1)}, bf16[12,48,384]{2,1,0:T(8,128)(2,1)S(1)}) custom-call(bf16[12,2,3,128,48]{4,3,2,1,0:T(8,128)(2,1)S(1)} %get-tuple-element.101.own_ref.own_bf, f32[3,3,12,128]{3,2,1,0:T(8,128)S(1)} %get-tuple-element.173.near_ref), custom_call_target="tpu_custom_call" | custom-call | flops 1000000000 | bytes 1000000 | tf_op jit(solution)/shard_map/pallas_call | solution.py:216
  113.8 2.6 %shard_map.189 = (f32[2,12,128]{2,1,0:T(8,128)S(1)}, bf16[12,48,768]{2,1,0:T(8,128)(2,1)S(1)}) custom-call(bf16[12,2,3,128,48]{4,3,2,1,0:T(8,128)(2,1)S(1)} %get-tuple-element.101.own_ref.own_bf, f32[3,6,12,128]{3,2,1,0:T(8,128)S(1)} %pad_maximum_fusion.2.near_ref), custom_call_target="tpu_custom_call" | custom-call | flops 1000000000 | bytes 1000000 | tf_op jit(solution)/shard_map/pallas_call | solution.py:216
  116.4 4.8 %collective-permute-start.20 = (f32[2,12,128]{2,1,0:T(8,128)S(1)}, f32[2,12,128]{2,1,0:T(8,128)S(1)}, u32[]{:S(2)}, u32[]{:S(2)}) collective-permute-start(f32[2,12,128]{2,1,0:T(8,128)S(1)} %rsqrt_multiply_fusion.own_slope_ref), channel_id=1, source_target_pairs={{0,8},{8,0},{16,24},{24,16},{32,40},{40,32},{48,56},{56,48},{64,72... | collective-permute-start | bytes 36872 | tf_op jit(solution)/shard_map/ppermute | solution.py:285
  122.1 8.1 %shard_map.190 = (f32[3,2,12,128]{3,2,1,0:T(8,128)S(1)}, f32[12,2,128,128]{3,2,1,0:T(8,128)S(1)}) custom-call(f32[3,2,12,128]{3,2,1,0:T(8,128)S(1)} %get-tuple-element.126.own_ref, f32[3,3,12,128]{3,2,1,0:T(8,128)S(1)} %pad_maximum_fusion.11.near_ref, bf16[12,2,3,128,48]{4,3,2,1,0:T(8,128)(2,1)S(1)} %get-tuple-element.101.own_ref.own_bf, ...), custom_call_target="tpu_custom_call" | custom-call | flops 1000000000 | bytes 1000000 | tf_op jit(solution)/shard_map/pallas_call | solution.py:216
  130.5 2.5 %collective-permute-start.23 = (f32[3,12,128]{2,1,0:T(8,128)S(1)}, f32[3,12,128]{2,1,0:T(8,128)S(1)}, u32[]{:S(2)}, u32[]{:S(2)}) collective-permute-start(f32[3,12,128]{2,1,0:T(8,128)S(1)} %get-tuple-element.145), channel_id=1, source_target_pairs={{0,7},{1,2},{2,1},{3,4},{4,3},{5,6},{6,5},{7,0},{8,15},{9,10},{10,... | collective-permute-start | bytes 55304 | tf_op jit(solution)/shard_map/ppermute | solution.py:285
  133.0 7.7 %shard_map.191.refs_1_ = f32[3,2,12,128]{3,2,1,0:T(8,128)S(1)} custom-call(f32[3,2,12,128]{3,2,1,0:T(8,128)S(1)} %get-tuple-element.126.own_ref, f32[3,3,12,128]{3,2,1,0:T(8,128)S(1)} %get-tuple-element.173.near_ref, bf16[12,2,3,128,48]{4,3,2,1,0:T(8,128)(2,1)S(1)} %get-tuple-element.101.own_ref.own_bf, bf16[12,48,384]{2,1,0:T(8,128)(2,1)S(1)} %get-tuple-element.113.near_bf, ...), custom_call_target="tpu_custom_call" | custom-call | flops 1000000000 | bytes 1000000 | tf_op jit(solution)/shard_map/pallas_call | solution.py:216
  140.8 7.8 %shard_map.192.refs_2_ = f32[3,2,12,128]{3,2,1,0:T(8,128)S(1)} custom-call(f32[3,2,12,128]{3,2,1,0:T(8,128)S(1)} %get-tuple-element.126.own_ref, f32[3,6,12,128]{3,2,1,0:T(8,128)S(1)} %pad_maximum_fusion.2.near_ref, bf16[12,2,3,128,48]{4,3,2,1,0:T(8,128)(2,1)S(1)} %get-tuple-element.101.own_ref.own_bf, bf16[12,48,768]{2,1,0:T(8,128)(2,1)S(1)} %get-tuple-element.117.near_bf, ...), custom_call_target="tpu_custom_call" | custom-call | flops 1000000000 | bytes 1000000 | tf_op jit(solution)/shard_map/pallas_call | solution.py:216
  (103 shorter events, 12.2 us)
Async XLA Ops:
  2.2 5.2 %collective-permute-start = (f32[3,2,12,128]{3,2,1,0:T(8,128)S(1)}, f32[3,2,12,128]{3,2,1,0:T(8,128)S(1)}, u32[]{:S(2)}, u32[]{:S(2)}) collective-permute-start(f32[3,2,12,128]{3,2,1,0:T(8,128)S(1)} %fusion.6.own_ref), channel_id=1, source_target_pairs={{0,8},{8,0},{16,24},{24,16},{32,40},{40,32},{48,56},{56,48},{64,72... | collective-permute-start | bytes 110600 | tf_op jit(solution)/shard_map/ppermute | solution.py:285
  5.5 5.5 %collective-permute-start.1 = (f32[3,2,12,128]{3,2,1,0:T(8,128)S(1)}, f32[3,2,12,128]{3,2,1,0:T(8,128)S(1)}, u32[]{:S(2)}, u32[]{:S(2)}) collective-permute-start(f32[3,2,12,128]{3,2,1,0:T(8,128)S(1)} %fusion.6.own_ref), channel_id=1, source_target_pairs={{0,248},{8,16},{16,8},{24,32},{32,24},{40,48},{48,40},{56,64},{64,... | collective-permute-start | bytes 110600 | tf_op jit(solution)/shard_map/ppermute | solution.py:285
  10.9 7.4 %copy-start.3 = (f32[3]{0:T(128)S(1)}, f32[3]{0:T(128)}, u32[]{:S(2)}) copy-start(f32[3]{0:T(128)} %constant.92) | copy-start | bytes 40
  10.9 7.4 %copy-start.4 = (f32[3]{0:T(128)S(1)}, f32[3]{0:T(128)}, u32[]{:S(2)}) copy-start(f32[3]{0:T(128)} %constant.91) | copy-start | bytes 40
  11.1 6.8 %collective-permute-start.2 = (f32[3,3,12,128]{3,2,1,0:T(8,128)S(1)}, f32[3,3,12,128]{3,2,1,0:T(8,128)S(1)}, u32[]{:S(2)}, u32[]{:S(2)}) collective-permute-start(f32[3,3,12,128]{3,2,1,0:T(8,128)S(1)} %get-tuple-element.142), channel_id=1, source_target_pairs={{0,1},{1,0},{2,3},{3,2},{4,5},{5,4},{6,7},{7,6},{8,9},{9,8},{10,11... | collective-permute-start | bytes 165896 | tf_op jit(solution)/shard_map/ppermute | solution.py:285
  12.8 5.5 %collective-permute-start.3 = (f32[3,3,12,128]{3,2,1,0:T(8,128)S(1)}, f32[3,3,12,128]{3,2,1,0:T(8,128)S(1)}, u32[]{:S(2)}, u32[]{:S(2)}) collective-permute-start(f32[3,3,12,128]{3,2,1,0:T(8,128)S(1)} %get-tuple-element.141), channel_id=1, source_target_pairs={{0,7},{1,2},{2,1},{3,4},{4,3},{5,6},{6,5},{7,0},{8,15},{9,10},{10,... | collective-permute-start | bytes 165896 | tf_op jit(solution)/shard_map/ppermute | solution.py:285
  21.1 7.0 %collective-permute-start.4 = (f32[2,12,128]{2,1,0:T(8,128)S(1)}, f32[2,12,128]{2,1,0:T(8,128)S(1)}, u32[]{:S(2)}, u32[]{:S(2)}) collective-permute-start(f32[2,12,128]{2,1,0:T(8,128)S(1)} %rsqrt_multiply_fusion.2.own_slope_ref), channel_id=1, source_target_pairs={{0,8},{8,0},{16,24},{24,16},{32,40},{40,32},{48,56},{56,48},{64,72... | collective-permute-start | bytes 36872 | tf_op jit(solution)/shard_map/ppermute | solution.py:285
  27.2 9.1 %collective-permute-start.5 = (f32[2,12,128]{2,1,0:T(8,128)S(1)}, f32[2,12,128]{2,1,0:T(8,128)S(1)}, u32[]{:S(2)}, u32[]{:S(2)}) collective-permute-start(f32[2,12,128]{2,1,0:T(8,128)S(1)} %rsqrt_multiply_fusion.2.own_slope_ref), channel_id=1, source_target_pairs={{0,248},{8,16},{16,8},{24,32},{32,24},{40,48},{48,40},{56,64},{64,... | collective-permute-start | bytes 36872 | tf_op jit(solution)/shard_map/ppermute | solution.py:285
  36.4 10.9 %collective-permute-start.6 = (f32[3,12,128]{2,1,0:T(8,128)S(1)}, f32[3,12,128]{2,1,0:T(8,128)S(1)}, u32[]{:S(2)}, u32[]{:S(2)}) collective-permute-start(f32[3,12,128]{2,1,0:T(8,128)S(1)} %get-tuple-element.166), channel_id=1, source_target_pairs={{0,1},{1,0},{2,3},{3,2},{4,5},{5,4},{6,7},{7,6},{8,9},{9,8},{10,11... | collective-permute-start | bytes 55304 | tf_op jit(solution)/shard_map/ppermute | solution.py:285
  36.5 10.8 %collective-permute-start.7 = (f32[3,12,128]{2,1,0:T(8,128)S(1)}, f32[3,12,128]{2,1,0:T(8,128)S(1)}, u32[]{:S(2)}, u32[]{:S(2)}) collective-permute-start(f32[3,12,128]{2,1,0:T(8,128)S(1)} %get-tuple-element.165), channel_id=1, source_target_pairs={{0,7},{1,2},{2,1},{3,4},{4,3},{5,6},{6,5},{7,0},{8,15},{9,10},{10,... | collective-permute-start | bytes 55304 | tf_op jit(solution)/shard_map/ppermute | solution.py:285
  47.3 7.8 %copy-start = (f32[3,1,2,12,128]{4,2,3,1,0:T(2,128)S(1)}, f32[3,1,2,12,128]{4,2,3,1,0:T(2,128)}, u32[]{:S(2)}) copy-start(f32[3,1,2,12,128]{4,2,3,1,0:T(2,128)} %param.16) | copy-start | bytes 110596
  47.3 7.8 %copy-start.1 = (f32[3,1,2,12,128]{4,2,3,1,0:T(2,128)S(1)}, f32[3,1,2,12,128]{4,2,3,1,0:T(2,128)}, u32[]{:S(2)}) copy-start(f32[3,1,2,12,128]{4,2,3,1,0:T(2,128)} %param.17) | copy-start | bytes 110596
  47.3 7.8 %copy-start.2 = (f32[3,2]{1,0:T(4,128)S(1)}, f32[3,2]{1,0:T(4,128)}, u32[]{:S(2)}) copy-start(f32[3,2]{1,0:T(4,128)} %constant.90) | copy-start | bytes 76
  55.2 3.0 %collective-permute-start.8 = (f32[3,2,12,128]{3,2,1,0:T(8,128)S(1)}, f32[3,2,12,128]{3,2,1,0:T(8,128)S(1)}, u32[]{:S(2)}, u32[]{:S(2)}) collective-permute-start(f32[3,2,12,128]{3,2,1,0:T(8,128)S(1)} %get-tuple-element.129.own_ref), channel_id=1, source_target_pairs={{0,8},{8,0},{16,24},{24,16},{32,40},{40,32},{48,56},{56,48},{64,72... | collective-permute-start | bytes 110600 | tf_op jit(solution)/shard_map/ppermute | solution.py:285
  57.3 4.4 %collective-permute-start.9 = (f32[3,2,12,128]{3,2,1,0:T(8,128)S(1)}, f32[3,2,12,128]{3,2,1,0:T(8,128)S(1)}, u32[]{:S(2)}, u32[]{:S(2)}) collective-permute-start(f32[3,2,12,128]{3,2,1,0:T(8,128)S(1)} %get-tuple-element.129.own_ref), channel_id=1, source_target_pairs={{0,248},{8,16},{16,8},{24,32},{32,24},{40,48},{48,40},{56,64},{64,... | collective-permute-start | bytes 110600 | tf_op jit(solution)/shard_map/ppermute | solution.py:285
  61.8 4.6 %collective-permute-start.10 = (f32[3,3,12,128]{3,2,1,0:T(8,128)S(1)}, f32[3,3,12,128]{3,2,1,0:T(8,128)S(1)}, u32[]{:S(2)}, u32[]{:S(2)}) collective-permute-start(f32[3,3,12,128]{3,2,1,0:T(8,128)S(1)} %get-tuple-element.138), channel_id=1, source_target_pairs={{0,1},{1,0},{2,3},{3,2},{4,5},{5,4},{6,7},{7,6},{8,9},{9,8},{10,11... | collective-permute-start | bytes 165896 | tf_op jit(solution)/shard_map/ppermute | solution.py:285
  61.9 5.4 %collective-permute-start.11 = (f32[3,3,12,128]{3,2,1,0:T(8,128)S(1)}, f32[3,3,12,128]{3,2,1,0:T(8,128)S(1)}, u32[]{:S(2)}, u32[]{:S(2)}) collective-permute-start(f32[3,3,12,128]{3,2,1,0:T(8,128)S(1)} %get-tuple-element.137), channel_id=1, source_target_pairs={{0,7},{1,2},{2,1},{3,4},{4,3},{5,6},{6,5},{7,0},{8,15},{9,10},{10,... | collective-permute-start | bytes 165896 | tf_op jit(solution)/shard_map/ppermute | solution.py:285
  70.1 5.5 %collective-permute-start.12 = (f32[2,12,128]{2,1,0:T(8,128)S(1)}, f32[2,12,128]{2,1,0:T(8,128)S(1)}, u32[]{:S(2)}, u32[]{:S(2)}) collective-permute-start(f32[2,12,128]{2,1,0:T(8,128)S(1)} %rsqrt_multiply_fusion.1.own_slope_ref), channel_id=1, source_target_pairs={{0,8},{8,0},{16,24},{24,16},{32,40},{40,32},{48,56},{56,48},{64,72... | collective-permute-start | bytes 36872 | tf_op jit(solution)/shard_map/ppermute | solution.py:285
  74.8 9.1 %collective-permute-start.13 = (f32[2,12,128]{2,1,0:T(8,128)S(1)}, f32[2,12,128]{2,1,0:T(8,128)S(1)}, u32[]{:S(2)}, u32[]{:S(2)}) collective-permute-start(f32[2,12,128]{2,1,0:T(8,128)S(1)} %rsqrt_multiply_fusion.1.own_slope_ref), channel_id=1, source_target_pairs={{0,248},{8,16},{16,8},{24,32},{32,24},{40,48},{48,40},{56,64},{64,... | collective-permute-start | bytes 36872 | tf_op jit(solution)/shard_map/ppermute | solution.py:285
  83.9 9.5 %collective-permute-start.14 = (f32[3,12,128]{2,1,0:T(8,128)S(1)}, f32[3,12,128]{2,1,0:T(8,128)S(1)}, u32[]{:S(2)}, u32[]{:S(2)}) collective-permute-start(f32[3,12,128]{2,1,0:T(8,128)S(1)} %get-tuple-element.156), channel_id=1, source_target_pairs={{0,1},{1,0},{2,3},{3,2},{4,5},{5,4},{6,7},{7,6},{8,9},{9,8},{10,11... | collective-permute-start | bytes 55304 | tf_op jit(solution)/shard_map/ppermute | solution.py:285
  84.4 9.0 %collective-permute-start.15 = (f32[3,12,128]{2,1,0:T(8,128)S(1)}, f32[3,12,128]{2,1,0:T(8,128)S(1)}, u32[]{:S(2)}, u32[]{:S(2)}) collective-permute-start(f32[3,12,128]{2,1,0:T(8,128)S(1)} %get-tuple-element.155), channel_id=1, source_target_pairs={{0,7},{1,2},{2,1},{3,4},{4,3},{5,6},{6,5},{7,0},{8,15},{9,10},{10,... | collective-permute-start | bytes 55304 | tf_op jit(solution)/shard_map/ppermute | solution.py:285
  101.3 2.9 %collective-permute-start.16 = (f32[3,2,12,128]{3,2,1,0:T(8,128)S(1)}, f32[3,2,12,128]{3,2,1,0:T(8,128)S(1)}, u32[]{:S(2)}, u32[]{:S(2)}) collective-permute-start(f32[3,2,12,128]{3,2,1,0:T(8,128)S(1)} %get-tuple-element.126.own_ref), channel_id=1, source_target_pairs={{0,8},{8,0},{16,24},{24,16},{32,40},{40,32},{48,56},{56,48},{64,72... | collective-permute-start | bytes 110600 | tf_op jit(solution)/shard_map/ppermute | solution.py:285
  103.3 4.8 %collective-permute-start.17 = (f32[3,2,12,128]{3,2,1,0:T(8,128)S(1)}, f32[3,2,12,128]{3,2,1,0:T(8,128)S(1)}, u32[]{:S(2)}, u32[]{:S(2)}) collective-permute-start(f32[3,2,12,128]{3,2,1,0:T(8,128)S(1)} %get-tuple-element.126.own_ref), channel_id=1, source_target_pairs={{0,248},{8,16},{16,8},{24,32},{32,24},{40,48},{48,40},{56,64},{64,... | collective-permute-start | bytes 110600 | tf_op jit(solution)/shard_map/ppermute | solution.py:285
  108.2 4.7 %collective-permute-start.18 = (f32[3,3,12,128]{3,2,1,0:T(8,128)S(1)}, f32[3,3,12,128]{3,2,1,0:T(8,128)S(1)}, u32[]{:S(2)}, u32[]{:S(2)}) collective-permute-start(f32[3,3,12,128]{3,2,1,0:T(8,128)S(1)} %get-tuple-element.134), channel_id=1, source_target_pairs={{0,1},{1,0},{2,3},{3,2},{4,5},{5,4},{6,7},{7,6},{8,9},{9,8},{10,11... | collective-permute-start | bytes 165896 | tf_op jit(solution)/shard_map/ppermute | solution.py:285
  108.3 5.4 %collective-permute-start.19 = (f32[3,3,12,128]{3,2,1,0:T(8,128)S(1)}, f32[3,3,12,128]{3,2,1,0:T(8,128)S(1)}, u32[]{:S(2)}, u32[]{:S(2)}) collective-permute-start(f32[3,3,12,128]{3,2,1,0:T(8,128)S(1)} %get-tuple-element.133), channel_id=1, source_target_pairs={{0,7},{1,2},{2,1},{3,4},{4,3},{5,6},{6,5},{7,0},{8,15},{9,10},{10,... | collective-permute-start | bytes 165896 | tf_op jit(solution)/shard_map/ppermute | solution.py:285
  116.4 5.7 %collective-permute-start.20 = (f32[2,12,128]{2,1,0:T(8,128)S(1)}, f32[2,12,128]{2,1,0:T(8,128)S(1)}, u32[]{:S(2)}, u32[]{:S(2)}) collective-permute-start(f32[2,12,128]{2,1,0:T(8,128)S(1)} %rsqrt_multiply_fusion.own_slope_ref), channel_id=1, source_target_pairs={{0,8},{8,0},{16,24},{24,16},{32,40},{40,32},{48,56},{56,48},{64,72... | collective-permute-start | bytes 36872 | tf_op jit(solution)/shard_map/ppermute | solution.py:285
  121.2 9.0 %collective-permute-start.21 = (f32[2,12,128]{2,1,0:T(8,128)S(1)}, f32[2,12,128]{2,1,0:T(8,128)S(1)}, u32[]{:S(2)}, u32[]{:S(2)}) collective-permute-start(f32[2,12,128]{2,1,0:T(8,128)S(1)} %rsqrt_multiply_fusion.own_slope_ref), channel_id=1, source_target_pairs={{0,248},{8,16},{16,8},{24,32},{32,24},{40,48},{48,40},{56,64},{64,... | collective-permute-start | bytes 36872 | tf_op jit(solution)/shard_map/ppermute | solution.py:285
  130.3 10.4 %collective-permute-start.22 = (f32[3,12,128]{2,1,0:T(8,128)S(1)}, f32[3,12,128]{2,1,0:T(8,128)S(1)}, u32[]{:S(2)}, u32[]{:S(2)}) collective-permute-start(f32[3,12,128]{2,1,0:T(8,128)S(1)} %get-tuple-element.146), channel_id=1, source_target_pairs={{0,1},{1,0},{2,3},{3,2},{4,5},{5,4},{6,7},{7,6},{8,9},{9,8},{10,11... | collective-permute-start | bytes 55304 | tf_op jit(solution)/shard_map/ppermute | solution.py:285
  130.5 10.2 %collective-permute-start.23 = (f32[3,12,128]{2,1,0:T(8,128)S(1)}, f32[3,12,128]{2,1,0:T(8,128)S(1)}, u32[]{:S(2)}, u32[]{:S(2)}) collective-permute-start(f32[3,12,128]{2,1,0:T(8,128)S(1)} %get-tuple-element.145), channel_id=1, source_target_pairs={{0,7},{1,2},{2,1},{3,4},{4,3},{5,6},{6,5},{7,0},{8,15},{9,10},{10,... | collective-permute-start | bytes 55304 | tf_op jit(solution)/shard_map/ppermute | solution.py:285

commit v5 on v4

--- a/solution.py
+++ b/solution.py
@@ -300,12 +300,12 @@
     first, last = value
     far = swap(jnp.where(even, first, last), "gy", 1)
     near = swap(jnp.where(even, last, first), "gy", 0)
-    return near, far
+    return far, near
 
 
 def below_above(received):
     even = lax.axis_index("gy") % 2 == 0
-    near, far = received
+    far, near = received
     return jnp.where(even, far, near), jnp.where(even, near, far)
 
 

time: 149 us -> 149 us (level); the launches traced: 149 us -> 148 us
  starting transfers between devices: 41.4 us -> 39.8 us
    ppermute x24, starting transfers between devices: 41.4 us -> 39.8 us  [swap(): return lax.ppermute(value, axis, [(i, partner[i]) for i in range(n)])]
  transfers between devices with their start and end apart: 24 -> 24, of which waited for: 10 -> 8; matrix products, arithmetic and copies ran while one was open for 1% -> 1% of each run, Pallas kernels for 44% -> 44%
where the time goes in v5:
time: 149 us; the launch traced here: 148 us
  Pallas kernels  97.2 us (65%)
  starting transfers between devices  39.8 us (27%)
  waiting for transfers between devices  6.09 us (4%)
  other arithmetic  3.4 us (2%)
    pallas_call x18, Pallas kernels, call(): pl.pallas_call(kernel, out_shape=out_shape, in_specs=[VMEM] * len(operand...  96.5 us
    ppermute x24, starting transfers between devices, swap(): return lax.ppermute(value, axis, [(i, partner[i]) for i in range(n)])  39.8 us
    ppermute x24, waiting for transfers between devices, swap(): return lax.ppermute(value, axis, [(i, partner[i]) for i in range(n)])  6.09 us
  transfers between devices with their start and end apart: 24, of which 8 were waited for; matrix products, arithmetic and copies ran while one was open for 1% of the time, Pallas kernels for 44%

profile of v5, /device:TPU:1, one launch (start us, length us, event | category | flops | bytes accessed | tf_op | source)
XLA Modules:
  0.0 147.7 jit_solution(5506539002958173263)
XLA Ops:
  2.2 3.2 %collective-permute-start = (f32[3,2,12,128]{3,2,1,0:T(8,128)S(1)}, f32[3,2,12,128]{3,2,1,0:T(8,128)S(1)}, u32[]{:S(2)}, u32[]{:S(2)}) collective-permute-start(f32[3,2,12,128]{3,2,1,0:T(8,128)S(1)} %fusion.6.own_ref), channel_id=1, source_target_pairs={{0,8},{8,0},{16,24},{24,16},{32,40},{40,32},{48,56},{56,48},{64,72... | collective-permute-start | bytes 110600 | tf_op jit(solution)/shard_map/ppermute | solution.py:285
  5.5 1.3 collective-permute-start.1
  7.5 3.4 %shard_map.175 = (f32[2,12,128]{2,1,0:T(8,128)S(1)}, bf16[12,48,384]{2,1,0:T(8,128)(2,1)S(1)}, bf16[12,2,3,128,48]{4,3,2,1,0:T(8,128)(2,1)S(1)}) custom-call(f32[3,2,12,128]{3,2,1,0:T(8,128)S(1)} %fusion.6.own_ref, f32[3,3,12,128]{3,2,1,0:T(8,128)S(1)} %pad_maximum_fusion.3.near_ref), custom_call_target="tpu_custom_call" | custom-call | flops 1000000000 | bytes 1000000 | tf_op jit(solution)/shard_map/pallas_call | solution.py:216
  11.1 4.2 %collective-permute-start.2 = (f32[3,3,12,128]{3,2,1,0:T(8,128)S(1)}, f32[3,3,12,128]{3,2,1,0:T(8,128)S(1)}, u32[]{:S(2)}, u32[]{:S(2)}) collective-permute-start(f32[3,3,12,128]{3,2,1,0:T(8,128)S(1)} %get-tuple-element.142), channel_id=1, source_target_pairs={{0,7},{1,2},{2,1},{3,4},{4,3},{5,6},{6,5},{7,0},{8,15},{9,10},{10,... | collective-permute-start | bytes 165896 | tf_op jit(solution)/shard_map/ppermute | solution.py:285
  15.2 2.5 %shard_map.176 = (f32[2,12,128]{2,1,0:T(8,128)S(1)}, bf16[12,48,384]{2,1,0:T(8,128)(2,1)S(1)}) custom-call(bf16[12,2,3,128,48]{4,3,2,1,0:T(8,128)(2,1)S(1)} %get-tuple-element.63.own_ref.own_bf, f32[3,3,12,128]{3,2,1,0:T(8,128)S(1)} %get-tuple-element.175.near_ref), custom_call_target="tpu_custom_call" | custom-call | flops 1000000000 | bytes 1000000 | tf_op jit(solution)/shard_map/pallas_call | solution.py:216
  18.6 2.6 %shard_map.177 = (f32[2,12,128]{2,1,0:T(8,128)S(1)}, bf16[12,48,768]{2,1,0:T(8,128)(2,1)S(1)}) custom-call(bf16[12,2,3,128,48]{4,3,2,1,0:T(8,128)(2,1)S(1)} %get-tuple-element.63.own_ref.own_bf, f32[3,6,12,128]{3,2,1,0:T(8,128)S(1)} %pad_maximum_fusion.near_ref), custom_call_target="tpu_custom_call" | custom-call | flops 1000000000 | bytes 1000000 | tf_op jit(solution)/shard_map/pallas_call | solution.py:216
  21.2 6.3 %collective-permute-start.4 = (f32[2,12,128]{2,1,0:T(8,128)S(1)}, f32[2,12,128]{2,1,0:T(8,128)S(1)}, u32[]{:S(2)}, u32[]{:S(2)}) collective-permute-start(f32[2,12,128]{2,1,0:T(8,128)S(1)} %rsqrt_multiply_fusion.2.own_slope_ref), channel_id=1, source_target_pairs={{0,8},{8,0},{16,24},{24,16},{32,40},{40,32},{48,56},{56,48},{64,72... | collective-permute-start | bytes 36872 | tf_op jit(solution)/shard_map/ppermute | solution.py:285
  28.3 8.3 %shard_map.178 = (f32[3,2,12,128]{3,2,1,0:T(8,128)S(1)}, f32[12,2,128,128]{3,2,1,0:T(8,128)S(1)}) custom-call(f32[3,2,12,128]{3,2,1,0:T(8,128)S(1)} %fusion.6.own_ref, f32[3,3,12,128]{3,2,1,0:T(8,128)S(1)} %pad_maximum_fusion.3.near_ref, bf16[12,2,3,128,48]{4,3,2,1,0:T(8,128)(2,1)S(1)} %get-tuple-element.63.own_ref.own_bf, ...), custom_call_target="tpu_custom_call" | custom-call | flops 1000000000 | bytes 1000000 | tf_op jit(solution)/shard_map/pallas_call | solution.py:216
  36.6 1.9 %collective-permute-start.6 = (f32[3,12,128]{2,1,0:T(8,128)S(1)}, f32[3,12,128]{2,1,0:T(8,128)S(1)}, u32[]{:S(2)}, u32[]{:S(2)}) collective-permute-start(f32[3,12,128]{2,1,0:T(8,128)S(1)} %get-tuple-element.166), channel_id=1, source_target_pairs={{0,7},{1,2},{2,1},{3,4},{4,3},{5,6},{6,5},{7,0},{8,15},{9,10},{10,... | collective-permute-start | bytes 55304 | tf_op jit(solution)/shard_map/ppermute | solution.py:285
  38.6 7.6 %shard_map.179 = f32[3,2,12,128]{3,2,1,0:T(8,128)S(1)} custom-call(f32[3,2,12,128]{3,2,1,0:T(8,128)S(1)} %fusion.6.own_ref, f32[3,3,12,128]{3,2,1,0:T(8,128)S(1)} %get-tuple-element.175.near_ref, bf16[12,2,3,128,48]{4,3,2,1,0:T(8,128)(2,1)S(1)} %get-tuple-element.63.own_ref.own_bf, bf16[12,48,384]{2,1,0:T(8,128)(2,1)S(1)} %get-tuple-element.75.near_bf, ...), custom_call_target="tpu_custom_call" | custom-call | flops 1000000000 | bytes 1000000 | tf_op jit(solution)/shard_map/pallas_call | solution.py:216
  46.2 7.8 %shard_map.180 = f32[3,2,12,128]{3,2,1,0:T(8,128)S(1)} custom-call(f32[3,2,12,128]{3,2,1,0:T(8,128)S(1)} %fusion.6.own_ref, f32[3,6,12,128]{3,2,1,0:T(8,128)S(1)} %pad_maximum_fusion.near_ref, bf16[12,2,3,128,48]{4,3,2,1,0:T(8,128)(2,1)S(1)} %get-tuple-element.63.own_ref.own_bf, bf16[12,48,768]{2,1,0:T(8,128)(2,1)S(1)} %get-tuple-element.79.near_bf, ...), custom_call_target="tpu_custom_call" | custom-call | flops 1000000000 | bytes 1000000 | tf_op jit(solution)/shard_map/pallas_call | solution.py:216
  54.1 2.4 %collective-permute-start.8 = (f32[3,2,12,128]{3,2,1,0:T(8,128)S(1)}, f32[3,2,12,128]{3,2,1,0:T(8,128)S(1)}, u32[]{:S(2)}, u32[]{:S(2)}) collective-permute-start(f32[3,2,12,128]{3,2,1,0:T(8,128)S(1)} %get-tuple-element.129.own_ref), channel_id=1, source_target_pairs={{0,8},{8,0},{16,24},{24,16},{32,40},{40,32},{48,56},{56,48},{64,72... | collective-permute-start | bytes 110600 | tf_op jit(solution)/shard_map/ppermute | solution.py:285
  57.6 3.4 %shard_map.181 = (f32[2,12,128]{2,1,0:T(8,128)S(1)}, bf16[12,48,384]{2,1,0:T(8,128)(2,1)S(1)}, bf16[12,2,3,128,48]{4,3,2,1,0:T(8,128)(2,1)S(1)}) custom-call(f32[3,2,12,128]{3,2,1,0:T(8,128)S(1)} %get-tuple-element.129.own_ref, f32[3,3,12,128]{3,2,1,0:T(8,128)S(1)} %pad_maximum_fusion.7.near_ref), custom_call_target="tpu_custom_call" | custom-call | flops 1000000000 | bytes 1000000 | tf_op jit(solution)/shard_map/pallas_call | solution.py:216
  61.1 1.5 %collective-permute-start.10 = (f32[3,3,12,128]{3,2,1,0:T(8,128)S(1)}, f32[3,3,12,128]{3,2,1,0:T(8,128)S(1)}, u32[]{:S(2)}, u32[]{:S(2)}) collective-permute-start(f32[3,3,12,128]{3,2,1,0:T(8,128)S(1)} %get-tuple-element.138), channel_id=1, source_target_pairs={{0,7},{1,2},{2,1},{3,4},{4,3},{5,6},{6,5},{7,0},{8,15},{9,10},{10,... | collective-permute-start | bytes 165896 | tf_op jit(solution)/shard_map/ppermute | solution.py:285
  63.0 2.5 %shard_map.182 = (f32[2,12,128]{2,1,0:T(8,128)S(1)}, bf16[12,48,384]{2,1,0:T(8,128)(2,1)S(1)}) custom-call(bf16[12,2,3,128,48]{4,3,2,1,0:T(8,128)(2,1)S(1)} %get-tuple-element.82.own_ref.own_bf, f32[3,3,12,128]{3,2,1,0:T(8,128)S(1)} %get-tuple-element.174.near_ref), custom_call_target="tpu_custom_call" | custom-call | flops 1000000000 | bytes 1000000 | tf_op jit(solution)/shard_map/pallas_call | solution.py:216
  66.6 2.6 %shard_map.183 = (f32[2,12,128]{2,1,0:T(8,128)S(1)}, bf16[12,48,768]{2,1,0:T(8,128)(2,1)S(1)}) custom-call(bf16[12,2,3,128,48]{4,3,2,1,0:T(8,128)(2,1)S(1)} %get-tuple-element.82.own_ref.own_bf, f32[3,6,12,128]{3,2,1,0:T(8,128)S(1)} %pad_maximum_fusion.1.near_ref), custom_call_target="tpu_custom_call" | custom-call | flops 1000000000 | bytes 1000000 | tf_op jit(solution)/shard_map/pallas_call | solution.py:216
  69.3 5.2 %collective-permute-start.12 = (f32[2,12,128]{2,1,0:T(8,128)S(1)}, f32[2,12,128]{2,1,0:T(8,128)S(1)}, u32[]{:S(2)}, u32[]{:S(2)}) collective-permute-start(f32[2,12,128]{2,1,0:T(8,128)S(1)} %rsqrt_multiply_fusion.1.own_slope_ref), channel_id=1, source_target_pairs={{0,8},{8,0},{16,24},{24,16},{32,40},{40,32},{48,56},{56,48},{64,72... | collective-permute-start | bytes 36872 | tf_op jit(solution)/shard_map/ppermute | solution.py:285
  75.3 8.2 %shard_map.184 = (f32[3,2,12,128]{3,2,1,0:T(8,128)S(1)}, f32[12,2,128,128]{3,2,1,0:T(8,128)S(1)}) custom-call(f32[3,2,12,128]{3,2,1,0:T(8,128)S(1)} %get-tuple-element.129.own_ref, f32[3,3,12,128]{3,2,1,0:T(8,128)S(1)} %pad_maximum_fusion.7.near_ref, bf16[12,2,3,128,48]{4,3,2,1,0:T(8,128)(2,1)S(1)} %get-tuple-element.82.own_ref.own_bf, ...), custom_call_target="tpu_custom_call" | custom-call | flops 1000000000 | bytes 1000000 | tf_op jit(solution)/shard_map/pallas_call | solution.py:216
  83.6 1.8 %collective-permute-start.14 = (f32[3,12,128]{2,1,0:T(8,128)S(1)}, f32[3,12,128]{2,1,0:T(8,128)S(1)}, u32[]{:S(2)}, u32[]{:S(2)}) collective-permute-start(f32[3,12,128]{2,1,0:T(8,128)S(1)} %get-tuple-element.156), channel_id=1, source_target_pairs={{0,7},{1,2},{2,1},{3,4},{4,3},{5,6},{6,5},{7,0},{8,15},{9,10},{10,... | collective-permute-start | bytes 55304 | tf_op jit(solution)/shard_map/ppermute | solution.py:285
  86.0 7.7 %shard_map.185 = f32[3,2,12,128]{3,2,1,0:T(8,128)S(1)} custom-call(f32[3,2,12,128]{3,2,1,0:T(8,128)S(1)} %get-tuple-element.129.own_ref, f32[3,3,12,128]{3,2,1,0:T(8,128)S(1)} %get-tuple-element.174.near_ref, bf16[12,2,3,128,48]{4,3,2,1,0:T(8,128)(2,1)S(1)} %get-tuple-element.82.own_ref.own_bf, bf16[12,48,384]{2,1,0:T(8,128)(2,1)S(1)} %get-tuple-element.94.near_bf, ...), custom_call_target="tpu_custom_call" | custom-call | flops 1000000000 | bytes 1000000 | tf_op jit(solution)/shard_map/pallas_call | solution.py:216
  93.7 7.8 %shard_map.186 = f32[3,2,12,128]{3,2,1,0:T(8,128)S(1)} custom-call(f32[3,2,12,128]{3,2,1,0:T(8,128)S(1)} %get-tuple-element.129.own_ref, f32[3,6,12,128]{3,2,1,0:T(8,128)S(1)} %pad_maximum_fusion.1.near_ref, bf16[12,2,3,128,48]{4,3,2,1,0:T(8,128)(2,1)S(1)} %get-tuple-element.82.own_ref.own_bf, bf16[12,48,768]{2,1,0:T(8,128)(2,1)S(1)} %get-tuple-element.98.near_bf, ...), custom_call_target="tpu_custom_call" | custom-call | flops 1000000000 | bytes 1000000 | tf_op jit(solution)/shard_map/pallas_call | solution.py:216
  102.5 1.8 %collective-permute-start.17 = (f32[3,2,12,128]{3,2,1,0:T(8,128)S(1)}, f32[3,2,12,128]{3,2,1,0:T(8,128)S(1)}, u32[]{:S(2)}, u32[]{:S(2)}) collective-permute-start(f32[3,2,12,128]{3,2,1,0:T(8,128)S(1)} %get-tuple-element.126.own_ref), channel_id=1, source_target_pairs={{0,248},{8,16},{16,8},{24,32},{32,24},{40,48},{48,40},{56,64},{64,... | collective-permute-start | bytes 110600 | tf_op jit(solution)/shard_map/ppermute | solution.py:285
  104.4 3.4 %shard_map.187 = (f32[2,12,128]{2,1,0:T(8,128)S(1)}, bf16[12,48,384]{2,1,0:T(8,128)(2,1)S(1)}, bf16[12,2,3,128,48]{4,3,2,1,0:T(8,128)(2,1)S(1)}) custom-call(f32[3,2,12,128]{3,2,1,0:T(8,128)S(1)} %get-tuple-element.126.own_ref, f32[3,3,12,128]{3,2,1,0:T(8,128)S(1)} %pad_maximum_fusion.11.near_ref), custom_call_target="tpu_custom_call" | custom-call | flops 1000000000 | bytes 1000000 | tf_op jit(solution)/shard_map/pallas_call | solution.py:216
  107.9 1.2 collective-permute-start.18
  109.8 2.5 %shard_map.188 = (f32[2,12,128]{2,1,0:T(8,128)S(1)}, bf16[12,48,384]{2,1,0:T(8,128)(2,1)S(1)}) custom-call(bf16[12,2,3,128,48]{4,3,2,1,0:T(8,128)(2,1)S(1)} %get-tuple-element.101.own_ref.own_bf, f32[3,3,12,128]{3,2,1,0:T(8,128)S(1)} %get-tuple-element.173.near_ref), custom_call_target="tpu_custom_call" | custom-call | flops 1000000000 | bytes 1000000 | tf_op jit(solution)/shard_map/pallas_call | solution.py:216
  112.3 1.0 collective-permute-done.18
  113.4 2.6 %shard_map.189 = (f32[2,12,128]{2,1,0:T(8,128)S(1)}, bf16[12,48,768]{2,1,0:T(8,128)(2,1)S(1)}) custom-call(bf16[12,2,3,128,48]{4,3,2,1,0:T(8,128)(2,1)S(1)} %get-tuple-element.101.own_ref.own_bf, f32[3,6,12,128]{3,2,1,0:T(8,128)S(1)} %pad_maximum_fusion.2.near_ref), custom_call_target="tpu_custom_call" | custom-call | flops 1000000000 | bytes 1000000 | tf_op jit(solution)/shard_map/pallas_call | solution.py:216
  116.1 4.4 %collective-permute-start.20 = (f32[2,12,128]{2,1,0:T(8,128)S(1)}, f32[2,12,128]{2,1,0:T(8,128)S(1)}, u32[]{:S(2)}, u32[]{:S(2)}) collective-permute-start(f32[2,12,128]{2,1,0:T(8,128)S(1)} %rsqrt_multiply_fusion.own_slope_ref), channel_id=1, source_target_pairs={{0,8},{8,0},{16,24},{24,16},{32,40},{40,32},{48,56},{56,48},{64,72... | collective-permute-start | bytes 36872 | tf_op jit(solution)/shard_map/ppermute | solution.py:285
  121.3 8.2 %shard_map.190 = (f32[3,2,12,128]{3,2,1,0:T(8,128)S(1)}, f32[12,2,128,128]{3,2,1,0:T(8,128)S(1)}) custom-call(f32[3,2,12,128]{3,2,1,0:T(8,128)S(1)} %get-tuple-element.126.own_ref, f32[3,3,12,128]{3,2,1,0:T(8,128)S(1)} %pad_maximum_fusion.11.near_ref, bf16[12,2,3,128,48]{4,3,2,1,0:T(8,128)(2,1)S(1)} %get-tuple-element.101.own_ref.own_bf, ...), custom_call_target="tpu_custom_call" | custom-call | flops 1000000000 | bytes 1000000 | tf_op jit(solution)/shard_map/pallas_call | solution.py:216
  129.5 1.8 %collective-permute-start.22 = (f32[3,12,128]{2,1,0:T(8,128)S(1)}, f32[3,12,128]{2,1,0:T(8,128)S(1)}, u32[]{:S(2)}, u32[]{:S(2)}) collective-permute-start(f32[3,12,128]{2,1,0:T(8,128)S(1)} %get-tuple-element.146), channel_id=1, source_target_pairs={{0,7},{1,2},{2,1},{3,4},{4,3},{5,6},{6,5},{7,0},{8,15},{9,10},{10,... | collective-permute-start | bytes 55304 | tf_op jit(solution)/shard_map/ppermute | solution.py:285
  131.5 7.6 %shard_map.191.refs_1_ = f32[3,2,12,128]{3,2,1,0:T(8,128)S(1)} custom-call(f32[3,2,12,128]{3,2,1,0:T(8,128)S(1)} %get-tuple-element.126.own_ref, f32[3,3,12,128]{3,2,1,0:T(8,128)S(1)} %get-tuple-element.173.near_ref, bf16[12,2,3,128,48]{4,3,2,1,0:T(8,128)(2,1)S(1)} %get-tuple-element.101.own_ref.own_bf, bf16[12,48,384]{2,1,0:T(8,128)(2,1)S(1)} %get-tuple-element.113.near_bf, ...), custom_call_target="tpu_custom_call" | custom-call | flops 1000000000 | bytes 1000000 | tf_op jit(solution)/shard_map/pallas_call | solution.py:216
  139.2 7.8 %shard_map.192.refs_2_ = f32[3,2,12,128]{3,2,1,0:T(8,128)S(1)} custom-call(f32[3,2,12,128]{3,2,1,0:T(8,128)S(1)} %get-tuple-element.126.own_ref, f32[3,6,12,128]{3,2,1,0:T(8,128)S(1)} %pad_maximum_fusion.2.near_ref, bf16[12,2,3,128,48]{4,3,2,1,0:T(8,128)(2,1)S(1)} %get-tuple-element.101.own_ref.own_bf, bf16[12,48,768]{2,1,0:T(8,128)(2,1)S(1)} %get-tuple-element.117.near_bf, ...), custom_call_target="tpu_custom_call" | custom-call | flops 1000000000 | bytes 1000000 | tf_op jit(solution)/shard_map/pallas_call | solution.py:216
  (103 shorter events, 12.0 us)
Async XLA Ops:
  2.2 5.2 %collective-permute-start = (f32[3,2,12,128]{3,2,1,0:T(8,128)S(1)}, f32[3,2,12,128]{3,2,1,0:T(8,128)S(1)}, u32[]{:S(2)}, u32[]{:S(2)}) collective-permute-start(f32[3,2,12,128]{3,2,1,0:T(8,128)S(1)} %fusion.6.own_ref), channel_id=1, source_target_pairs={{0,8},{8,0},{16,24},{24,16},{32,40},{40,32},{48,56},{56,48},{64,72... | collective-permute-start | bytes 110600 | tf_op jit(solution)/shard_map/ppermute | solution.py:285
  5.5 5.5 %collective-permute-start.1 = (f32[3,2,12,128]{3,2,1,0:T(8,128)S(1)}, f32[3,2,12,128]{3,2,1,0:T(8,128)S(1)}, u32[]{:S(2)}, u32[]{:S(2)}) collective-permute-start(f32[3,2,12,128]{3,2,1,0:T(8,128)S(1)} %fusion.6.own_ref), channel_id=1, source_target_pairs={{0,248},{8,16},{16,8},{24,32},{32,24},{40,48},{48,40},{56,64},{64,... | collective-permute-start | bytes 110600 | tf_op jit(solution)/shard_map/ppermute | solution.py:285
  10.9 7.5 %copy-start.3 = (f32[3]{0:T(128)S(1)}, f32[3]{0:T(128)}, u32[]{:S(2)}) copy-start(f32[3]{0:T(128)} %constant.92) | copy-start | bytes 40
  10.9 7.5 %copy-start.4 = (f32[3]{0:T(128)S(1)}, f32[3]{0:T(128)}, u32[]{:S(2)}) copy-start(f32[3]{0:T(128)} %constant.91) | copy-start | bytes 40
  11.1 6.7 %collective-permute-start.2 = (f32[3,3,12,128]{3,2,1,0:T(8,128)S(1)}, f32[3,3,12,128]{3,2,1,0:T(8,128)S(1)}, u32[]{:S(2)}, u32[]{:S(2)}) collective-permute-start(f32[3,3,12,128]{3,2,1,0:T(8,128)S(1)} %get-tuple-element.142), channel_id=1, source_target_pairs={{0,7},{1,2},{2,1},{3,4},{4,3},{5,6},{6,5},{7,0},{8,15},{9,10},{10,... | collective-permute-start | bytes 165896 | tf_op jit(solution)/shard_map/ppermute | solution.py:285
  15.2 3.2 %collective-permute-start.3 = (f32[3,3,12,128]{3,2,1,0:T(8,128)S(1)}, f32[3,3,12,128]{3,2,1,0:T(8,128)S(1)}, u32[]{:S(2)}, u32[]{:S(2)}) collective-permute-start(f32[3,3,12,128]{3,2,1,0:T(8,128)S(1)} %get-tuple-element.141), channel_id=1, source_target_pairs={{0,1},{1,0},{2,3},{3,2},{4,5},{5,4},{6,7},{7,6},{8,9},{9,8},{10,11... | collective-permute-start | bytes 165896 | tf_op jit(solution)/shard_map/ppermute | solution.py:285
  21.2 7.1 %collective-permute-start.4 = (f32[2,12,128]{2,1,0:T(8,128)S(1)}, f32[2,12,128]{2,1,0:T(8,128)S(1)}, u32[]{:S(2)}, u32[]{:S(2)}) collective-permute-start(f32[2,12,128]{2,1,0:T(8,128)S(1)} %rsqrt_multiply_fusion.2.own_slope_ref), channel_id=1, source_target_pairs={{0,8},{8,0},{16,24},{24,16},{32,40},{40,32},{48,56},{56,48},{64,72... | collective-permute-start | bytes 36872 | tf_op jit(solution)/shard_map/ppermute | solution.py:285
  27.5 9.1 %collective-permute-start.5 = (f32[2,12,128]{2,1,0:T(8,128)S(1)}, f32[2,12,128]{2,1,0:T(8,128)S(1)}, u32[]{:S(2)}, u32[]{:S(2)}) collective-permute-start(f32[2,12,128]{2,1,0:T(8,128)S(1)} %rsqrt_multiply_fusion.2.own_slope_ref), channel_id=1, source_target_pairs={{0,248},{8,16},{16,8},{24,32},{32,24},{40,48},{48,40},{56,64},{64,... | collective-permute-start | bytes 36872 | tf_op jit(solution)/shard_map/ppermute | solution.py:285
  36.6 9.5 %collective-permute-start.6 = (f32[3,12,128]{2,1,0:T(8,128)S(1)}, f32[3,12,128]{2,1,0:T(8,128)S(1)}, u32[]{:S(2)}, u32[]{:S(2)}) collective-permute-start(f32[3,12,128]{2,1,0:T(8,128)S(1)} %get-tuple-element.166), channel_id=1, source_target_pairs={{0,7},{1,2},{2,1},{3,4},{4,3},{5,6},{6,5},{7,0},{8,15},{9,10},{10,... | collective-permute-start | bytes 55304 | tf_op jit(solution)/shard_map/ppermute | solution.py:285
  38.6 7.6 %collective-permute-start.7 = (f32[3,12,128]{2,1,0:T(8,128)S(1)}, f32[3,12,128]{2,1,0:T(8,128)S(1)}, u32[]{:S(2)}, u32[]{:S(2)}) collective-permute-start(f32[3,12,128]{2,1,0:T(8,128)S(1)} %get-tuple-element.165), channel_id=1, source_target_pairs={{0,1},{1,0},{2,3},{3,2},{4,5},{5,4},{6,7},{7,6},{8,9},{9,8},{10,11... | collective-permute-start | bytes 55304 | tf_op jit(solution)/shard_map/ppermute | solution.py:285
  46.2 7.8 %copy-start = (f32[3,1,2,12,128]{4,2,3,1,0:T(2,128)S(1)}, f32[3,1,2,12,128]{4,2,3,1,0:T(2,128)}, u32[]{:S(2)}) copy-start(f32[3,1,2,12,128]{4,2,3,1,0:T(2,128)} %param.16) | copy-start | bytes 110596
  46.2 7.8 %copy-start.1 = (f32[3,1,2,12,128]{4,2,3,1,0:T(2,128)S(1)}, f32[3,1,2,12,128]{4,2,3,1,0:T(2,128)}, u32[]{:S(2)}) copy-start(f32[3,1,2,12,128]{4,2,3,1,0:T(2,128)} %param.17) | copy-start | bytes 110596
  46.2 7.8 %copy-start.2 = (f32[3,2]{1,0:T(4,128)S(1)}, f32[3,2]{1,0:T(4,128)}, u32[]{:S(2)}) copy-start(f32[3,2]{1,0:T(4,128)} %constant.90) | copy-start | bytes 76
  54.1 3.3 %collective-permute-start.8 = (f32[3,2,12,128]{3,2,1,0:T(8,128)S(1)}, f32[3,2,12,128]{3,2,1,0:T(8,128)S(1)}, u32[]{:S(2)}, u32[]{:S(2)}) collective-permute-start(f32[3,2,12,128]{3,2,1,0:T(8,128)S(1)} %get-tuple-element.129.own_ref), channel_id=1, source_target_pairs={{0,8},{8,0},{16,24},{24,16},{32,40},{40,32},{48,56},{56,48},{64,72... | collective-permute-start | bytes 110600 | tf_op jit(solution)/shard_map/ppermute | solution.py:285
  56.6 4.4 %collective-permute-start.9 = (f32[3,2,12,128]{3,2,1,0:T(8,128)S(1)}, f32[3,2,12,128]{3,2,1,0:T(8,128)S(1)}, u32[]{:S(2)}, u32[]{:S(2)}) collective-permute-start(f32[3,2,12,128]{3,2,1,0:T(8,128)S(1)} %get-tuple-element.129.own_ref), channel_id=1, source_target_pairs={{0,248},{8,16},{16,8},{24,32},{32,24},{40,48},{48,40},{56,64},{64,... | collective-permute-start | bytes 110600 | tf_op jit(solution)/shard_map/ppermute | solution.py:285
  61.1 5.4 %collective-permute-start.10 = (f32[3,3,12,128]{3,2,1,0:T(8,128)S(1)}, f32[3,3,12,128]{3,2,1,0:T(8,128)S(1)}, u32[]{:S(2)}, u32[]{:S(2)}) collective-permute-start(f32[3,3,12,128]{3,2,1,0:T(8,128)S(1)} %get-tuple-element.138), channel_id=1, source_target_pairs={{0,7},{1,2},{2,1},{3,4},{4,3},{5,6},{6,5},{7,0},{8,15},{9,10},{10,... | collective-permute-start | bytes 165896 | tf_op jit(solution)/shard_map/ppermute | solution.py:285
  62.7 3.9 %collective-permute-start.11 = (f32[3,3,12,128]{3,2,1,0:T(8,128)S(1)}, f32[3,3,12,128]{3,2,1,0:T(8,128)S(1)}, u32[]{:S(2)}, u32[]{:S(2)}) collective-permute-start(f32[3,3,12,128]{3,2,1,0:T(8,128)S(1)} %get-tuple-element.137), channel_id=1, source_target_pairs={{0,1},{1,0},{2,3},{3,2},{4,5},{5,4},{6,7},{7,6},{8,9},{9,8},{10,11... | collective-permute-start | bytes 165896 | tf_op jit(solution)/shard_map/ppermute | solution.py:285
  69.3 6.1 %collective-permute-start.12 = (f32[2,12,128]{2,1,0:T(8,128)S(1)}, f32[2,12,128]{2,1,0:T(8,128)S(1)}, u32[]{:S(2)}, u32[]{:S(2)}) collective-permute-start(f32[2,12,128]{2,1,0:T(8,128)S(1)} %rsqrt_multiply_fusion.1.own_slope_ref), channel_id=1, source_target_pairs={{0,8},{8,0},{16,24},{24,16},{32,40},{40,32},{48,56},{56,48},{64,72... | collective-permute-start | bytes 36872 | tf_op jit(solution)/shard_map/ppermute | solution.py:285
  74.5 9.1 %collective-permute-start.13 = (f32[2,12,128]{2,1,0:T(8,128)S(1)}, f32[2,12,128]{2,1,0:T(8,128)S(1)}, u32[]{:S(2)}, u32[]{:S(2)}) collective-permute-start(f32[2,12,128]{2,1,0:T(8,128)S(1)} %rsqrt_multiply_fusion.1.own_slope_ref), channel_id=1, source_target_pairs={{0,248},{8,16},{16,8},{24,32},{32,24},{40,48},{48,40},{56,64},{64,... | collective-permute-start | bytes 36872 | tf_op jit(solution)/shard_map/ppermute | solution.py:285
  83.6 10.0 %collective-permute-start.14 = (f32[3,12,128]{2,1,0:T(8,128)S(1)}, f32[3,12,128]{2,1,0:T(8,128)S(1)}, u32[]{:S(2)}, u32[]{:S(2)}) collective-permute-start(f32[3,12,128]{2,1,0:T(8,128)S(1)} %get-tuple-element.156), channel_id=1, source_target_pairs={{0,7},{1,2},{2,1},{3,4},{4,3},{5,6},{6,5},{7,0},{8,15},{9,10},{10,... | collective-permute-start | bytes 55304 | tf_op jit(solution)/shard_map/ppermute | solution.py:285
  85.4 8.2 %collective-permute-start.15 = (f32[3,12,128]{2,1,0:T(8,128)S(1)}, f32[3,12,128]{2,1,0:T(8,128)S(1)}, u32[]{:S(2)}, u32[]{:S(2)}) collective-permute-start(f32[3,12,128]{2,1,0:T(8,128)S(1)} %get-tuple-element.155), channel_id=1, source_target_pairs={{0,1},{1,0},{2,3},{3,2},{4,5},{5,4},{6,7},{7,6},{8,9},{9,8},{10,11... | collective-permute-start | bytes 55304 | tf_op jit(solution)/shard_map/ppermute | solution.py:285
  101.6 2.8 %collective-permute-start.16 = (f32[3,2,12,128]{3,2,1,0:T(8,128)S(1)}, f32[3,2,12,128]{3,2,1,0:T(8,128)S(1)}, u32[]{:S(2)}, u32[]{:S(2)}) collective-permute-start(f32[3,2,12,128]{3,2,1,0:T(8,128)S(1)} %get-tuple-element.126.own_ref), channel_id=1, source_target_pairs={{0,8},{8,0},{16,24},{24,16},{32,40},{40,32},{48,56},{56,48},{64,72... | collective-permute-start | bytes 110600 | tf_op jit(solution)/shard_map/ppermute | solution.py:285
  102.5 5.3 %collective-permute-start.17 = (f32[3,2,12,128]{3,2,1,0:T(8,128)S(1)}, f32[3,2,12,128]{3,2,1,0:T(8,128)S(1)}, u32[]{:S(2)}, u32[]{:S(2)}) collective-permute-start(f32[3,2,12,128]{3,2,1,0:T(8,128)S(1)} %get-tuple-element.126.own_ref), channel_id=1, source_target_pairs={{0,248},{8,16},{16,8},{24,32},{32,24},{40,48},{48,40},{56,64},{64,... | collective-permute-start | bytes 110600 | tf_op jit(solution)/shard_map/ppermute | solution.py:285
  107.9 5.4 %collective-permute-start.18 = (f32[3,3,12,128]{3,2,1,0:T(8,128)S(1)}, f32[3,3,12,128]{3,2,1,0:T(8,128)S(1)}, u32[]{:S(2)}, u32[]{:S(2)}) collective-permute-start(f32[3,3,12,128]{3,2,1,0:T(8,128)S(1)} %get-tuple-element.134), channel_id=1, source_target_pairs={{0,7},{1,2},{2,1},{3,4},{4,3},{5,6},{6,5},{7,0},{8,15},{9,10},{10,... | collective-permute-start | bytes 165896 | tf_op jit(solution)/shard_map/ppermute | solution.py:285
  109.1 4.2 %collective-permute-start.19 = (f32[3,3,12,128]{3,2,1,0:T(8,128)S(1)}, f32[3,3,12,128]{3,2,1,0:T(8,128)S(1)}, u32[]{:S(2)}, u32[]{:S(2)}) collective-permute-start(f32[3,3,12,128]{3,2,1,0:T(8,128)S(1)} %get-tuple-element.133), channel_id=1, source_target_pairs={{0,1},{1,0},{2,3},{3,2},{4,5},{5,4},{6,7},{7,6},{8,9},{9,8},{10,11... | collective-permute-start | bytes 165896 | tf_op jit(solution)/shard_map/ppermute | solution.py:285
  116.1 5.2 %collective-permute-start.20 = (f32[2,12,128]{2,1,0:T(8,128)S(1)}, f32[2,12,128]{2,1,0:T(8,128)S(1)}, u32[]{:S(2)}, u32[]{:S(2)}) collective-permute-start(f32[2,12,128]{2,1,0:T(8,128)S(1)} %rsqrt_multiply_fusion.own_slope_ref), channel_id=1, source_target_pairs={{0,8},{8,0},{16,24},{24,16},{32,40},{40,32},{48,56},{56,48},{64,72... | collective-permute-start | bytes 36872 | tf_op jit(solution)/shard_map/ppermute | solution.py:285
  120.5 9.0 %collective-permute-start.21 = (f32[2,12,128]{2,1,0:T(8,128)S(1)}, f32[2,12,128]{2,1,0:T(8,128)S(1)}, u32[]{:S(2)}, u32[]{:S(2)}) collective-permute-start(f32[2,12,128]{2,1,0:T(8,128)S(1)} %rsqrt_multiply_fusion.own_slope_ref), channel_id=1, source_target_pairs={{0,248},{8,16},{16,8},{24,32},{32,24},{40,48},{48,40},{56,64},{64,... | collective-permute-start | bytes 36872 | tf_op jit(solution)/shard_map/ppermute | solution.py:285
  129.5 9.6 %collective-permute-start.22 = (f32[3,12,128]{2,1,0:T(8,128)S(1)}, f32[3,12,128]{2,1,0:T(8,128)S(1)}, u32[]{:S(2)}, u32[]{:S(2)}) collective-permute-start(f32[3,12,128]{2,1,0:T(8,128)S(1)} %get-tuple-element.146), channel_id=1, source_target_pairs={{0,7},{1,2},{2,1},{3,4},{4,3},{5,6},{6,5},{7,0},{8,15},{9,10},{10,... | collective-permute-start | bytes 55304 | tf_op jit(solution)/shard_map/ppermute | solution.py:285
  131.4 7.8 %collective-permute-start.23 = (f32[3,12,128]{2,1,0:T(8,128)S(1)}, f32[3,12,128]{2,1,0:T(8,128)S(1)}, u32[]{:S(2)}, u32[]{:S(2)}) collective-permute-start(f32[3,12,128]{2,1,0:T(8,128)S(1)} %get-tuple-element.145), channel_id=1, source_target_pairs={{0,1},{1,0},{2,3},{3,2},{4,5},{5,4},{6,7},{7,6},{8,9},{9,8},{10,11... | collective-permute-start | bytes 55304 | tf_op jit(solution)/shard_map/ppermute | solution.py:285

commit v6 on v5

--- a/solution.py
+++ b/solution.py
@@ -17,8 +17,8 @@
 KF = 48
 CHUNK = 16
 UNROLL = 4
-INNER = ((0, 3), (0, 3))
-MIDDLE = ((0, 3), (0, 3))
+INNER = ((0, 2), (0, 2))
+MIDDLE = ((0, 4), (0, 4))
 OUTER = ((0, 3), (3, 6))
 
 
@@ -292,7 +292,8 @@
 
 
 def exchange_x(value):
-    return swap(value, "gx", 0), swap(value, "gx", 1)
+    far = swap(value, "gx", 1)
+    return swap(value, "gx", 0), far
 
 
 def exchange_y(value):
@@ -327,13 +328,11 @@
 
     def forces_of(own):
         near, far = exchange_x(own)
-        near = near + along(0, side)
-        inner = jnp.concatenate([own, near[:, :1]], axis=1)
-        square, inner_bf, own_bf = density_part(own, inner, INNER)
-        square, far = lax.optimization_barrier((square, far))
-        far = far - along(0, side)
+        square, inner_bf, own_bf = density_part(own, own, INNER)
+        square, far, near = lax.optimization_barrier((square, far, near))
+        near, far = near + along(0, side), far - along(0, side)
         received = exchange_y(rows_along_y(own, near, far))
-        middle = jnp.concatenate([near[:, 1:], far], axis=1)
+        middle = jnp.concatenate([near, far], axis=1)
         part, middle_bf = density_part(own_bf, middle, MIDDLE)
         part, received = lax.optimization_barrier((part, received))
         below, above = below_above(received)
@@ -342,11 +341,10 @@
         density = DENSITY_SCALE * jnp.maximum(square + part + last - 1.0, 0.0)
         slope = -0.25 * lax.rsqrt(1.0 + density)
         near_slope, far_slope = exchange_x(slope)
-        inner_slope = jnp.concatenate([slope, near_slope[:1]], axis=0)
-        force, turned = force_part(own, inner, own_bf, inner_bf, slope, inner_slope, INNER)
-        force, far_slope = lax.optimization_barrier((force, far_slope))
+        force, turned = force_part(own, own, own_bf, inner_bf, slope, slope, INNER)
+        force, far_slope, near_slope = lax.optimization_barrier((force, far_slope, near_slope))
         received = exchange_y(rows_along_y(slope, near_slope, far_slope))
-        middle_slope = jnp.concatenate([near_slope[1:], far_slope], axis=0)
+        middle_slope = jnp.concatenate([near_slope, far_slope], axis=0)
         (part,) = force_part(own, middle, own_bf, middle_bf, turned, middle_slope, MIDDLE)
         part, received = lax.optimization_barrier((part, received))
         outer_slope = jnp.concatenate(below_above(received), axis=0)

time: 149 us -> 145 us (0.973)
  starting transfers between devices: 39.8 us -> 44.8 us
  waiting for transfers between devices: 6.09 us -> 1.14 us
  Pallas kernels: 97.2 us -> 94.4 us
    ppermute x24, starting transfers between devices: 39.8 us -> 44.8 us  [swap(): return lax.ppermute(value, axis, [(i, partner[i]) for i in range(n)])]
    ppermute x24, waiting for transfers between devices: 6.09 us -> 1.14 us  [swap(): return lax.ppermute(value, axis, [(i, partner[i]) for i in range(n)])]
    pallas_call x18, Pallas kernels: 96.5 us -> 93.7 us  [call(): pl.pallas_call(kernel, out_shape=out_shape, in_specs=[VMEM] * len(operand...]
  transfers between devices with their start and end apart: 24 -> 24, of which waited for: 8 -> 3; matrix products, arithmetic and copies ran while one was open for 1% -> 0% of each run, Pallas kernels for 44% -> 44%
where the time goes in v6:
time: 145 us
  Pallas kernels  94.4 us (65%)
  starting transfers between devices  44.8 us (31%)
  other arithmetic  3.16 us (2%)
    pallas_call x18, Pallas kernels, call(): pl.pallas_call(kernel, out_shape=out_shape, in_specs=[VMEM] * len(operand...  93.7 us
    ppermute x24, starting transfers between devices, swap(): return lax.ppermute(value, axis, [(i, partner[i]) for i in range(n)])  44.8 us
  transfers between devices with their start and end apart: 24, of which 3 were waited for; matrix products, arithmetic and copies ran while one was open for 0% of the time, Pallas kernels for 44%

profile of v6, /device:TPU:1, one launch (start us, length us, event | category | flops | bytes accessed | tf_op | source)
XLA Modules:
  0.0 144.9 jit_solution(14979920242112091114)
XLA Ops:
  2.2 4.4 %collective-permute-start = (f32[3,2,12,128]{3,2,1,0:T(8,128)S(1)}, f32[3,2,12,128]{3,2,1,0:T(8,128)S(1)}, u32[]{:S(2)}, u32[]{:S(2)}) collective-permute-start(f32[3,2,12,128]{3,2,1,0:T(8,128)S(1)} %fusion.6.own_ref.near_ref), channel_id=1, source_target_pairs={{0,248},{8,16},{16,8},{24,32},{32,24},{40,48},{48,40},{56,64},{64,... | collective-permute-start | bytes 110600 | tf_op jit(solution)/shard_map/ppermute | solution.py:285
  6.6 5.1 %collective-permute-start.1 = (f32[3,2,12,128]{3,2,1,0:T(8,128)S(1)}, f32[3,2,12,128]{3,2,1,0:T(8,128)S(1)}, u32[]{:S(2)}, u32[]{:S(2)}) collective-permute-start(f32[3,2,12,128]{3,2,1,0:T(8,128)S(1)} %fusion.6.own_ref.near_ref), channel_id=1, source_target_pairs={{0,8},{8,0},{16,24},{24,16},{32,40},{40,32},{48,56},{56,48},{64,72... | collective-permute-start | bytes 110600 | tf_op jit(solution)/shard_map/ppermute | solution.py:285
  12.4 2.8 %shard_map.175 = (f32[2,12,128]{2,1,0:T(8,128)S(1)}, bf16[12,48,256]{2,1,0:T(8,128)(2,1)S(1)}, bf16[12,2,3,128,48]{4,3,2,1,0:T(8,128)(2,1)S(1)}) custom-call(f32[3,2,12,128]{3,2,1,0:T(8,128)S(1)} %fusion.6.own_ref.near_ref, f32[3,2,12,128]{3,2,1,0:T(8,128)S(1)} %fusion.6.own_ref.near_ref), custom_call_target="tpu_custom_call" | custom-call | flops 1000000000 | bytes 1000000 | tf_op jit(solution)/shard_map/pallas_call | solution.py:216
  15.4 3.3 %collective-permute-start.2 = (f32[3,3,12,128]{3,2,1,0:T(8,128)S(1)}, f32[3,3,12,128]{3,2,1,0:T(8,128)S(1)}, u32[]{:S(2)}, u32[]{:S(2)}) collective-permute-start(f32[3,3,12,128]{3,2,1,0:T(8,128)S(1)} %get-tuple-element.154), channel_id=1, source_target_pairs={{0,7},{1,2},{2,1},{3,4},{4,3},{5,6},{6,5},{7,0},{8,15},{9,10},{10,... | collective-permute-start | bytes 165896 | tf_op jit(solution)/shard_map/ppermute | solution.py:285
  18.7 3.2 %shard_map.176 = (f32[2,12,128]{2,1,0:T(8,128)S(1)}, bf16[12,48,512]{2,1,0:T(8,128)(2,1)S(1)}) custom-call(bf16[12,2,3,128,48]{4,3,2,1,0:T(8,128)(2,1)S(1)} %get-tuple-element.69.own_ref.own_bf, f32[3,4,12,128]{3,2,1,0:T(8,128)S(1)} %pad_maximum_fusion.3.near_ref), custom_call_target="tpu_custom_call" | custom-call | flops 1000000000 | bytes 1000000 | tf_op jit(solution)/shard_map/pallas_call | solution.py:216
  22.3 2.6 %shard_map.177 = (f32[2,12,128]{2,1,0:T(8,128)S(1)}, bf16[12,48,768]{2,1,0:T(8,128)(2,1)S(1)}) custom-call(bf16[12,2,3,128,48]{4,3,2,1,0:T(8,128)(2,1)S(1)} %get-tuple-element.69.own_ref.own_bf, f32[3,6,12,128]{3,2,1,0:T(8,128)S(1)} %pad_maximum_fusion.near_ref), custom_call_target="tpu_custom_call" | custom-call | flops 1000000000 | bytes 1000000 | tf_op jit(solution)/shard_map/pallas_call | solution.py:216
  25.7 3.3 %collective-permute-start.5 = (f32[2,12,128]{2,1,0:T(8,128)S(1)}, f32[2,12,128]{2,1,0:T(8,128)S(1)}, u32[]{:S(2)}, u32[]{:S(2)}) collective-permute-start(f32[2,12,128]{2,1,0:T(8,128)S(1)} %rsqrt_multiply_fusion.2.own_slope_ref.refs_0_), channel_id=1, source_target_pairs={{0,8},{8,0},{16,24},{24,16},{32,40},{40,32},{48,56},{56,48},{64,72... | collective-permute-start | bytes 36872 | tf_op jit(solution)/shard_map/ppermute | solution.py:285
  29.0 5.6 %shard_map.178 = (f32[3,2,12,128]{3,2,1,0:T(8,128)S(1)}, f32[12,2,128,128]{3,2,1,0:T(8,128)S(1)}) custom-call(f32[3,2,12,128]{3,2,1,0:T(8,128)S(1)} %fusion.6.own_ref.near_ref, f32[3,2,12,128]{3,2,1,0:T(8,128)S(1)} %fusion.6.own_ref.near_ref, bf16[12,2,3,128,48]{4,3,2,1,0:T(8,128)(2,1)S(1)} %get-tuple-element.69.own_ref.own_bf, ...), custom_call_target="tpu_custom_call" | custom-call | flops 1000000000 | bytes 1000000 | tf_op jit(solution)/shard_map/pallas_call | solution.py:216
  34.7 2.2 %collective-permute-start.6 = (f32[3,12,128]{2,1,0:T(8,128)S(1)}, f32[3,12,128]{2,1,0:T(8,128)S(1)}, u32[]{:S(2)}, u32[]{:S(2)}) collective-permute-start(f32[3,12,128]{2,1,0:T(8,128)S(1)} %get-tuple-element.178), channel_id=1, source_target_pairs={{0,7},{1,2},{2,1},{3,4},{4,3},{5,6},{6,5},{7,0},{8,15},{9,10},{10,... | collective-permute-start | bytes 55304 | tf_op jit(solution)/shard_map/ppermute | solution.py:285
  36.9 9.5 %shard_map.179 = f32[3,2,12,128]{3,2,1,0:T(8,128)S(1)} custom-call(f32[3,2,12,128]{3,2,1,0:T(8,128)S(1)} %fusion.6.own_ref.near_ref, f32[3,4,12,128]{3,2,1,0:T(8,128)S(1)} %pad_maximum_fusion.3.near_ref, bf16[12,2,3,128,48]{4,3,2,1,0:T(8,128)(2,1)S(1)} %get-tuple-element.69.own_ref.own_bf, bf16[12,48,512]{2,1,0:T(8,128)(2,1)S(1)} %get-tuple-element.82.near_bf, ...), custom_call_target="tpu_custom_call" | custom-call | flops 1000000000 | bytes 1000000 | tf_op jit(solution)/shard_map/pallas_call | solution.py:216
  46.5 7.5 %shard_map.180 = f32[3,2,12,128]{3,2,1,0:T(8,128)S(1)} custom-call(f32[3,2,12,128]{3,2,1,0:T(8,128)S(1)} %fusion.6.own_ref.near_ref, f32[3,6,12,128]{3,2,1,0:T(8,128)S(1)} %pad_maximum_fusion.near_ref, bf16[12,2,3,128,48]{4,3,2,1,0:T(8,128)(2,1)S(1)} %get-tuple-element.69.own_ref.own_bf, bf16[12,48,768]{2,1,0:T(8,128)(2,1)S(1)} %get-tuple-element.87.near_bf, ...), custom_call_target="tpu_custom_call" | custom-call | flops 1000000000 | bytes 1000000 | tf_op jit(solution)/shard_map/pallas_call | solution.py:216
  54.4 3.7 %collective-permute-start.9 = (f32[3,2,12,128]{3,2,1,0:T(8,128)S(1)}, f32[3,2,12,128]{3,2,1,0:T(8,128)S(1)}, u32[]{:S(2)}, u32[]{:S(2)}) collective-permute-start(f32[3,2,12,128]{3,2,1,0:T(8,128)S(1)} %get-tuple-element.141.own_ref.near_ref), channel_id=1, source_target_pairs={{0,8},{8,0},{16,24},{24,16},{32,40},{40,32},{48,56},{56,48},{64,72... | collective-permute-start | bytes 110600 | tf_op jit(solution)/shard_map/ppermute | solution.py:285
  58.0 2.8 %shard_map.181 = (f32[2,12,128]{2,1,0:T(8,128)S(1)}, bf16[12,48,256]{2,1,0:T(8,128)(2,1)S(1)}, bf16[12,2,3,128,48]{4,3,2,1,0:T(8,128)(2,1)S(1)}) custom-call(f32[3,2,12,128]{3,2,1,0:T(8,128)S(1)} %get-tuple-element.141.own_ref.near_ref, f32[3,2,12,128]{3,2,1,0:T(8,128)S(1)} %get-tuple-element.141.own_ref.near_ref), custom_call_target="tpu_custom_call" | custom-call | flops 1000000000 | bytes 1000000 | tf_op jit(solution)/shard_map/pallas_call | solution.py:216
  61.0 1.1 collective-permute-start.10
  62.6 3.2 %shard_map.182 = (f32[2,12,128]{2,1,0:T(8,128)S(1)}, bf16[12,48,512]{2,1,0:T(8,128)(2,1)S(1)}) custom-call(bf16[12,2,3,128,48]{4,3,2,1,0:T(8,128)(2,1)S(1)} %get-tuple-element.90.own_ref.own_bf, f32[3,4,12,128]{3,2,1,0:T(8,128)S(1)} %pad_maximum_fusion.4.near_ref), custom_call_target="tpu_custom_call" | custom-call | flops 1000000000 | bytes 1000000 | tf_op jit(solution)/shard_map/pallas_call | solution.py:216
  66.5 2.6 %shard_map.183 = (f32[2,12,128]{2,1,0:T(8,128)S(1)}, bf16[12,48,768]{2,1,0:T(8,128)(2,1)S(1)}) custom-call(bf16[12,2,3,128,48]{4,3,2,1,0:T(8,128)(2,1)S(1)} %get-tuple-element.90.own_ref.own_bf, f32[3,6,12,128]{3,2,1,0:T(8,128)S(1)} %pad_maximum_fusion.1.near_ref), custom_call_target="tpu_custom_call" | custom-call | flops 1000000000 | bytes 1000000 | tf_op jit(solution)/shard_map/pallas_call | solution.py:216
  69.2 1.0 collective-permute-start.12
  70.2 4.2 %collective-permute-start.13 = (f32[2,12,128]{2,1,0:T(8,128)S(1)}, f32[2,12,128]{2,1,0:T(8,128)S(1)}, u32[]{:S(2)}, u32[]{:S(2)}) collective-permute-start(f32[2,12,128]{2,1,0:T(8,128)S(1)} %rsqrt_multiply_fusion.1.own_slope_ref.refs_0_), channel_id=1, source_target_pairs={{0,8},{8,0},{16,24},{24,16},{32,40},{40,32},{48,56},{56,48},{64,72... | collective-permute-start | bytes 36872 | tf_op jit(solution)/shard_map/ppermute | solution.py:285
  74.4 5.6 %shard_map.184 = (f32[3,2,12,128]{3,2,1,0:T(8,128)S(1)}, f32[12,2,128,128]{3,2,1,0:T(8,128)S(1)}) custom-call(f32[3,2,12,128]{3,2,1,0:T(8,128)S(1)} %get-tuple-element.141.own_ref.near_ref, f32[3,2,12,128]{3,2,1,0:T(8,128)S(1)} %get-tuple-element.141.own_ref.near_ref, bf16[12,2,3,128,48]{4,3,2,1,0:T(8,128)(2,1)S(1)} %get-tuple-element.90.own_ref.own_bf, ...), custom_call_target="tpu_custom_call" | custom-call | flops 1000000000 | bytes 1000000 | tf_op jit(solution)/shard_map/pallas_call | solution.py:216
  80.1 1.6 %collective-permute-start.14 = (f32[3,12,128]{2,1,0:T(8,128)S(1)}, f32[3,12,128]{2,1,0:T(8,128)S(1)}, u32[]{:S(2)}, u32[]{:S(2)}) collective-permute-start(f32[3,12,128]{2,1,0:T(8,128)S(1)} %get-tuple-element.168), channel_id=1, source_target_pairs={{0,7},{1,2},{2,1},{3,4},{4,3},{5,6},{6,5},{7,0},{8,15},{9,10},{10,... | collective-permute-start | bytes 55304 | tf_op jit(solution)/shard_map/ppermute | solution.py:285
  81.7 9.5 %shard_map.185 = f32[3,2,12,128]{3,2,1,0:T(8,128)S(1)} custom-call(f32[3,2,12,128]{3,2,1,0:T(8,128)S(1)} %get-tuple-element.141.own_ref.near_ref, f32[3,4,12,128]{3,2,1,0:T(8,128)S(1)} %pad_maximum_fusion.4.near_ref, bf16[12,2,3,128,48]{4,3,2,1,0:T(8,128)(2,1)S(1)} %get-tuple-element.90.own_ref.own_bf, bf16[12,48,512]{2,1,0:T(8,128)(2,1)S(1)} %get-tuple-element.103.near_bf, ...), custom_call_target="tpu_custom_call" | custom-call | flops 1000000000 | bytes 1000000 | tf_op jit(solution)/shard_map/pallas_call | solution.py:216
  91.3 7.5 %shard_map.186 = f32[3,2,12,128]{3,2,1,0:T(8,128)S(1)} custom-call(f32[3,2,12,128]{3,2,1,0:T(8,128)S(1)} %get-tuple-element.141.own_ref.near_ref, f32[3,6,12,128]{3,2,1,0:T(8,128)S(1)} %pad_maximum_fusion.1.near_ref, bf16[12,2,3,128,48]{4,3,2,1,0:T(8,128)(2,1)S(1)} %get-tuple-element.90.own_ref.own_bf, bf16[12,48,768]{2,1,0:T(8,128)(2,1)S(1)} %get-tuple-element.108.near_bf, ...), custom_call_target="tpu_custom_call" | custom-call | flops 1000000000 | bytes 1000000 | tf_op jit(solution)/shard_map/pallas_call | solution.py:216
  98.9 4.2 %collective-permute-start.17 = (f32[3,2,12,128]{3,2,1,0:T(8,128)S(1)}, f32[3,2,12,128]{3,2,1,0:T(8,128)S(1)}, u32[]{:S(2)}, u32[]{:S(2)}) collective-permute-start(f32[3,2,12,128]{3,2,1,0:T(8,128)S(1)} %get-tuple-element.138.own_ref.near_ref), channel_id=1, source_target_pairs={{0,8},{8,0},{16,24},{24,16},{32,40},{40,32},{48,56},{56,48},{64,72... | collective-permute-start | bytes 110600 | tf_op jit(solution)/shard_map/ppermute | solution.py:285
  103.2 2.8 %shard_map.187 = (f32[2,12,128]{2,1,0:T(8,128)S(1)}, bf16[12,48,256]{2,1,0:T(8,128)(2,1)S(1)}, bf16[12,2,3,128,48]{4,3,2,1,0:T(8,128)(2,1)S(1)}) custom-call(f32[3,2,12,128]{3,2,1,0:T(8,128)S(1)} %get-tuple-element.138.own_ref.near_ref, f32[3,2,12,128]{3,2,1,0:T(8,128)S(1)} %get-tuple-element.138.own_ref.near_ref), custom_call_target="tpu_custom_call" | custom-call | flops 1000000000 | bytes 1000000 | tf_op jit(solution)/shard_map/pallas_call | solution.py:216
  106.1 1.8 %collective-permute-start.18 = (f32[3,3,12,128]{3,2,1,0:T(8,128)S(1)}, f32[3,3,12,128]{3,2,1,0:T(8,128)S(1)}, u32[]{:S(2)}, u32[]{:S(2)}) collective-permute-start(f32[3,3,12,128]{3,2,1,0:T(8,128)S(1)} %get-tuple-element.146), channel_id=1, source_target_pairs={{0,7},{1,2},{2,1},{3,4},{4,3},{5,6},{6,5},{7,0},{8,15},{9,10},{10,... | collective-permute-start | bytes 165896 | tf_op jit(solution)/shard_map/ppermute | solution.py:285
  108.3 3.2 %shard_map.188 = (f32[2,12,128]{2,1,0:T(8,128)S(1)}, bf16[12,48,512]{2,1,0:T(8,128)(2,1)S(1)}) custom-call(bf16[12,2,3,128,48]{4,3,2,1,0:T(8,128)(2,1)S(1)} %get-tuple-element.111.own_ref.own_bf, f32[3,4,12,128]{3,2,1,0:T(8,128)S(1)} %pad_maximum_fusion.5.near_ref), custom_call_target="tpu_custom_call" | custom-call | flops 1000000000 | bytes 1000000 | tf_op jit(solution)/shard_map/pallas_call | solution.py:216
  111.7 2.6 %shard_map.189 = (f32[2,12,128]{2,1,0:T(8,128)S(1)}, bf16[12,48,768]{2,1,0:T(8,128)(2,1)S(1)}) custom-call(bf16[12,2,3,128,48]{4,3,2,1,0:T(8,128)(2,1)S(1)} %get-tuple-element.111.own_ref.own_bf, f32[3,6,12,128]{3,2,1,0:T(8,128)S(1)} %pad_maximum_fusion.2.near_ref), custom_call_target="tpu_custom_call" | custom-call | flops 1000000000 | bytes 1000000 | tf_op jit(solution)/shard_map/pallas_call | solution.py:216
  114.8 4.8 %collective-permute-start.21 = (f32[2,12,128]{2,1,0:T(8,128)S(1)}, f32[2,12,128]{2,1,0:T(8,128)S(1)}, u32[]{:S(2)}, u32[]{:S(2)}) collective-permute-start(f32[2,12,128]{2,1,0:T(8,128)S(1)} %rsqrt_multiply_fusion.own_slope_ref.refs_0_), channel_id=1, source_target_pairs={{0,8},{8,0},{16,24},{24,16},{32,40},{40,32},{48,56},{56,48},{64,72... | collective-permute-start | bytes 36872 | tf_op jit(solution)/shard_map/ppermute | solution.py:285
  119.6 5.6 %shard_map.190 = (f32[3,2,12,128]{3,2,1,0:T(8,128)S(1)}, f32[12,2,128,128]{3,2,1,0:T(8,128)S(1)}) custom-call(f32[3,2,12,128]{3,2,1,0:T(8,128)S(1)} %get-tuple-element.138.own_ref.near_ref, f32[3,2,12,128]{3,2,1,0:T(8,128)S(1)} %get-tuple-element.138.own_ref.near_ref, bf16[12,2,3,128,48]{4,3,2,1,0:T(8,128)(2,1)S(1)} %get-tuple-element.111.own_ref.own_bf, ...), custom_call_target="tpu_custom_call" | custom-call | flops 1000000000 | bytes 1000000 | tf_op jit(solution)/shard_map/pallas_call | solution.py:216
  125.3 1.8 %collective-permute-start.22 = (f32[3,12,128]{2,1,0:T(8,128)S(1)}, f32[3,12,128]{2,1,0:T(8,128)S(1)}, u32[]{:S(2)}, u32[]{:S(2)}) collective-permute-start(f32[3,12,128]{2,1,0:T(8,128)S(1)} %get-tuple-element.158), channel_id=1, source_target_pairs={{0,7},{1,2},{2,1},{3,4},{4,3},{5,6},{6,5},{7,0},{8,15},{9,10},{10,... | collective-permute-start | bytes 55304 | tf_op jit(solution)/shard_map/ppermute | solution.py:285
  127.1 9.5 %shard_map.191.refs_1_ = f32[3,2,12,128]{3,2,1,0:T(8,128)S(1)} custom-call(f32[3,2,12,128]{3,2,1,0:T(8,128)S(1)} %get-tuple-element.138.own_ref.near_ref, f32[3,4,12,128]{3,2,1,0:T(8,128)S(1)} %pad_maximum_fusion.5.near_ref, bf16[12,2,3,128,48]{4,3,2,1,0:T(8,128)(2,1)S(1)} %get-tuple-element.111.own_ref.own_bf, ...), custom_call_target="tpu_custom_call" | custom-call | flops 1000000000 | bytes 1000000 | tf_op jit(solution)/shard_map/pallas_call | solution.py:216
  136.7 7.5 %shard_map.192.refs_2_ = f32[3,2,12,128]{3,2,1,0:T(8,128)S(1)} custom-call(f32[3,2,12,128]{3,2,1,0:T(8,128)S(1)} %get-tuple-element.138.own_ref.near_ref, f32[3,6,12,128]{3,2,1,0:T(8,128)S(1)} %pad_maximum_fusion.2.near_ref, bf16[12,2,3,128,48]{4,3,2,1,0:T(8,128)(2,1)S(1)} %get-tuple-element.111.own_ref.own_bf, ...), custom_call_target="tpu_custom_call" | custom-call | flops 1000000000 | bytes 1000000 | tf_op jit(solution)/shard_map/pallas_call | solution.py:216
  (99 shorter events, 7.4 us)
Async XLA Ops:
  2.2 13.0 %collective-permute-start = (f32[3,2,12,128]{3,2,1,0:T(8,128)S(1)}, f32[3,2,12,128]{3,2,1,0:T(8,128)S(1)}, u32[]{:S(2)}, u32[]{:S(2)}) collective-permute-start(f32[3,2,12,128]{3,2,1,0:T(8,128)S(1)} %fusion.6.own_ref.near_ref), channel_id=1, source_target_pairs={{0,248},{8,16},{16,8},{24,32},{32,24},{40,48},{48,40},{56,64},{64,... | collective-permute-start | bytes 110600 | tf_op jit(solution)/shard_map/ppermute | solution.py:285
  6.6 8.6 %collective-permute-start.1 = (f32[3,2,12,128]{3,2,1,0:T(8,128)S(1)}, f32[3,2,12,128]{3,2,1,0:T(8,128)S(1)}, u32[]{:S(2)}, u32[]{:S(2)}) collective-permute-start(f32[3,2,12,128]{3,2,1,0:T(8,128)S(1)} %fusion.6.own_ref.near_ref), channel_id=1, source_target_pairs={{0,8},{8,0},{16,24},{24,16},{32,40},{40,32},{48,56},{56,48},{64,72... | collective-permute-start | bytes 110600 | tf_op jit(solution)/shard_map/ppermute | solution.py:285
  15.2 7.0 %copy-start.3 = (f32[3]{0:T(128)S(1)}, f32[3]{0:T(128)}, u32[]{:S(2)}) copy-start(f32[3]{0:T(128)} %constant.92) | copy-start | bytes 40
  15.2 7.0 %copy-start.4 = (f32[3]{0:T(128)S(1)}, f32[3]{0:T(128)}, u32[]{:S(2)}) copy-start(f32[3]{0:T(128)} %constant.91) | copy-start | bytes 40
  15.4 6.4 %collective-permute-start.2 = (f32[3,3,12,128]{3,2,1,0:T(8,128)S(1)}, f32[3,3,12,128]{3,2,1,0:T(8,128)S(1)}, u32[]{:S(2)}, u32[]{:S(2)}) collective-permute-start(f32[3,3,12,128]{3,2,1,0:T(8,128)S(1)} %get-tuple-element.154), channel_id=1, source_target_pairs={{0,7},{1,2},{2,1},{3,4},{4,3},{5,6},{6,5},{7,0},{8,15},{9,10},{10,... | collective-permute-start | bytes 165896 | tf_op jit(solution)/shard_map/ppermute | solution.py:285
  18.7 3.5 %collective-permute-start.3 = (f32[3,3,12,128]{3,2,1,0:T(8,128)S(1)}, f32[3,3,12,128]{3,2,1,0:T(8,128)S(1)}, u32[]{:S(2)}, u32[]{:S(2)}) collective-permute-start(f32[3,3,12,128]{3,2,1,0:T(8,128)S(1)} %get-tuple-element.153), channel_id=1, source_target_pairs={{0,1},{1,0},{2,3},{3,2},{4,5},{5,4},{6,7},{7,6},{8,9},{9,8},{10,11... | collective-permute-start | bytes 165896 | tf_op jit(solution)/shard_map/ppermute | solution.py:285
  25.0 9.6 %collective-permute-start.4 = (f32[2,12,128]{2,1,0:T(8,128)S(1)}, f32[2,12,128]{2,1,0:T(8,128)S(1)}, u32[]{:S(2)}, u32[]{:S(2)}) collective-permute-start(f32[2,12,128]{2,1,0:T(8,128)S(1)} %rsqrt_multiply_fusion.2.own_slope_ref.refs_0_), channel_id=1, source_target_pairs={{0,248},{8,16},{16,8},{24,32},{32,24},{40,48},{48,40},{56,64},{64,... | collective-permute-start | bytes 36872 | tf_op jit(solution)/shard_map/ppermute | solution.py:285
  25.7 8.9 %collective-permute-start.5 = (f32[2,12,128]{2,1,0:T(8,128)S(1)}, f32[2,12,128]{2,1,0:T(8,128)S(1)}, u32[]{:S(2)}, u32[]{:S(2)}) collective-permute-start(f32[2,12,128]{2,1,0:T(8,128)S(1)} %rsqrt_multiply_fusion.2.own_slope_ref.refs_0_), channel_id=1, source_target_pairs={{0,8},{8,0},{16,24},{24,16},{32,40},{40,32},{48,56},{56,48},{64,72... | collective-permute-start | bytes 36872 | tf_op jit(solution)/shard_map/ppermute | solution.py:285
  34.7 11.7 %collective-permute-start.6 = (f32[3,12,128]{2,1,0:T(8,128)S(1)}, f32[3,12,128]{2,1,0:T(8,128)S(1)}, u32[]{:S(2)}, u32[]{:S(2)}) collective-permute-start(f32[3,12,128]{2,1,0:T(8,128)S(1)} %get-tuple-element.178), channel_id=1, source_target_pairs={{0,7},{1,2},{2,1},{3,4},{4,3},{5,6},{6,5},{7,0},{8,15},{9,10},{10,... | collective-permute-start | bytes 55304 | tf_op jit(solution)/shard_map/ppermute | solution.py:285
  36.9 9.5 %collective-permute-start.7 = (f32[3,12,128]{2,1,0:T(8,128)S(1)}, f32[3,12,128]{2,1,0:T(8,128)S(1)}, u32[]{:S(2)}, u32[]{:S(2)}) collective-permute-start(f32[3,12,128]{2,1,0:T(8,128)S(1)} %get-tuple-element.177), channel_id=1, source_target_pairs={{0,1},{1,0},{2,3},{3,2},{4,5},{5,4},{6,7},{7,6},{8,9},{9,8},{10,11... | collective-permute-start | bytes 55304 | tf_op jit(solution)/shard_map/ppermute | solution.py:285
  46.4 7.6 %copy-start = (f32[3,1,2,12,128]{4,2,3,1,0:T(2,128)S(1)}, f32[3,1,2,12,128]{4,2,3,1,0:T(2,128)}, u32[]{:S(2)}) copy-start(f32[3,1,2,12,128]{4,2,3,1,0:T(2,128)} %param.16) | copy-start | bytes 110596
  46.5 7.6 %copy-start.1 = (f32[3,1,2,12,128]{4,2,3,1,0:T(2,128)S(1)}, f32[3,1,2,12,128]{4,2,3,1,0:T(2,128)}, u32[]{:S(2)}) copy-start(f32[3,1,2,12,128]{4,2,3,1,0:T(2,128)} %param.17) | copy-start | bytes 110596
  46.5 7.6 %copy-start.2 = (f32[3,2]{1,0:T(4,128)S(1)}, f32[3,2]{1,0:T(4,128)}, u32[]{:S(2)}) copy-start(f32[3,2]{1,0:T(4,128)} %constant.90) | copy-start | bytes 76
  54.1 6.7 %collective-permute-start.8 = (f32[3,2,12,128]{3,2,1,0:T(8,128)S(1)}, f32[3,2,12,128]{3,2,1,0:T(8,128)S(1)}, u32[]{:S(2)}, u32[]{:S(2)}) collective-permute-start(f32[3,2,12,128]{3,2,1,0:T(8,128)S(1)} %get-tuple-element.141.own_ref.near_ref), channel_id=1, source_target_pairs={{0,248},{8,16},{16,8},{24,32},{32,24},{40,48},{48,40},{56,64},{64,... | collective-permute-start | bytes 110600 | tf_op jit(solution)/shard_map/ppermute | solution.py:285
  54.4 6.5 %collective-permute-start.9 = (f32[3,2,12,128]{3,2,1,0:T(8,128)S(1)}, f32[3,2,12,128]{3,2,1,0:T(8,128)S(1)}, u32[]{:S(2)}, u32[]{:S(2)}) collective-permute-start(f32[3,2,12,128]{3,2,1,0:T(8,128)S(1)} %get-tuple-element.141.own_ref.near_ref), channel_id=1, source_target_pairs={{0,8},{8,0},{16,24},{24,16},{32,40},{40,32},{48,56},{56,48},{64,72... | collective-permute-start | bytes 110600 | tf_op jit(solution)/shard_map/ppermute | solution.py:285
  61.0 5.4 %collective-permute-start.10 = (f32[3,3,12,128]{3,2,1,0:T(8,128)S(1)}, f32[3,3,12,128]{3,2,1,0:T(8,128)S(1)}, u32[]{:S(2)}, u32[]{:S(2)}) collective-permute-start(f32[3,3,12,128]{3,2,1,0:T(8,128)S(1)} %get-tuple-element.150), channel_id=1, source_target_pairs={{0,7},{1,2},{2,1},{3,4},{4,3},{5,6},{6,5},{7,0},{8,15},{9,10},{10,... | collective-permute-start | bytes 165896 | tf_op jit(solution)/shard_map/ppermute | solution.py:285
  62.1 4.3 %collective-permute-start.11 = (f32[3,3,12,128]{3,2,1,0:T(8,128)S(1)}, f32[3,3,12,128]{3,2,1,0:T(8,128)S(1)}, u32[]{:S(2)}, u32[]{:S(2)}) collective-permute-start(f32[3,3,12,128]{3,2,1,0:T(8,128)S(1)} %get-tuple-element.149), channel_id=1, source_target_pairs={{0,1},{1,0},{2,3},{3,2},{4,5},{5,4},{6,7},{7,6},{8,9},{9,8},{10,11... | collective-permute-start | bytes 165896 | tf_op jit(solution)/shard_map/ppermute | solution.py:285
  69.2 10.8 %collective-permute-start.12 = (f32[2,12,128]{2,1,0:T(8,128)S(1)}, f32[2,12,128]{2,1,0:T(8,128)S(1)}, u32[]{:S(2)}, u32[]{:S(2)}) collective-permute-start(f32[2,12,128]{2,1,0:T(8,128)S(1)} %rsqrt_multiply_fusion.1.own_slope_ref.refs_0_), channel_id=1, source_target_pairs={{0,248},{8,16},{16,8},{24,32},{32,24},{40,48},{48,40},{56,64},{64,... | collective-permute-start | bytes 36872 | tf_op jit(solution)/shard_map/ppermute | solution.py:285
  70.2 9.9 %collective-permute-start.13 = (f32[2,12,128]{2,1,0:T(8,128)S(1)}, f32[2,12,128]{2,1,0:T(8,128)S(1)}, u32[]{:S(2)}, u32[]{:S(2)}) collective-permute-start(f32[2,12,128]{2,1,0:T(8,128)S(1)} %rsqrt_multiply_fusion.1.own_slope_ref.refs_0_), channel_id=1, source_target_pairs={{0,8},{8,0},{16,24},{24,16},{32,40},{40,32},{48,56},{56,48},{64,72... | collective-permute-start | bytes 36872 | tf_op jit(solution)/shard_map/ppermute | solution.py:285
  80.1 11.1 %collective-permute-start.14 = (f32[3,12,128]{2,1,0:T(8,128)S(1)}, f32[3,12,128]{2,1,0:T(8,128)S(1)}, u32[]{:S(2)}, u32[]{:S(2)}) collective-permute-start(f32[3,12,128]{2,1,0:T(8,128)S(1)} %get-tuple-element.168), channel_id=1, source_target_pairs={{0,7},{1,2},{2,1},{3,4},{4,3},{5,6},{6,5},{7,0},{8,15},{9,10},{10,... | collective-permute-start | bytes 55304 | tf_op jit(solution)/shard_map/ppermute | solution.py:285
  81.7 9.5 %collective-permute-start.15 = (f32[3,12,128]{2,1,0:T(8,128)S(1)}, f32[3,12,128]{2,1,0:T(8,128)S(1)}, u32[]{:S(2)}, u32[]{:S(2)}) collective-permute-start(f32[3,12,128]{2,1,0:T(8,128)S(1)} %get-tuple-element.167), channel_id=1, source_target_pairs={{0,1},{1,0},{2,3},{3,2},{4,5},{5,4},{6,7},{7,6},{8,9},{9,8},{10,11... | collective-permute-start | bytes 55304 | tf_op jit(solution)/shard_map/ppermute | solution.py:285
  98.9 7.1 %collective-permute-start.16 = (f32[3,2,12,128]{3,2,1,0:T(8,128)S(1)}, f32[3,2,12,128]{3,2,1,0:T(8,128)S(1)}, u32[]{:S(2)}, u32[]{:S(2)}) collective-permute-start(f32[3,2,12,128]{3,2,1,0:T(8,128)S(1)} %get-tuple-element.138.own_ref.near_ref), channel_id=1, source_target_pairs={{0,248},{8,16},{16,8},{24,32},{32,24},{40,48},{48,40},{56,64},{64,... | collective-permute-start | bytes 110600 | tf_op jit(solution)/shard_map/ppermute | solution.py:285
  98.9 7.0 %collective-permute-start.17 = (f32[3,2,12,128]{3,2,1,0:T(8,128)S(1)}, f32[3,2,12,128]{3,2,1,0:T(8,128)S(1)}, u32[]{:S(2)}, u32[]{:S(2)}) collective-permute-start(f32[3,2,12,128]{3,2,1,0:T(8,128)S(1)} %get-tuple-element.138.own_ref.near_ref), channel_id=1, source_target_pairs={{0,8},{8,0},{16,24},{24,16},{32,40},{40,32},{48,56},{56,48},{64,72... | collective-permute-start | bytes 110600 | tf_op jit(solution)/shard_map/ppermute | solution.py:285
  106.1 5.4 %collective-permute-start.18 = (f32[3,3,12,128]{3,2,1,0:T(8,128)S(1)}, f32[3,3,12,128]{3,2,1,0:T(8,128)S(1)}, u32[]{:S(2)}, u32[]{:S(2)}) collective-permute-start(f32[3,3,12,128]{3,2,1,0:T(8,128)S(1)} %get-tuple-element.146), channel_id=1, source_target_pairs={{0,7},{1,2},{2,1},{3,4},{4,3},{5,6},{6,5},{7,0},{8,15},{9,10},{10,... | collective-permute-start | bytes 165896 | tf_op jit(solution)/shard_map/ppermute | solution.py:285
  108.0 3.6 %collective-permute-start.19 = (f32[3,3,12,128]{3,2,1,0:T(8,128)S(1)}, f32[3,3,12,128]{3,2,1,0:T(8,128)S(1)}, u32[]{:S(2)}, u32[]{:S(2)}) collective-permute-start(f32[3,3,12,128]{3,2,1,0:T(8,128)S(1)} %get-tuple-element.145), channel_id=1, source_target_pairs={{0,1},{1,0},{2,3},{3,2},{4,5},{5,4},{6,7},{7,6},{8,9},{9,8},{10,11... | collective-permute-start | bytes 165896 | tf_op jit(solution)/shard_map/ppermute | solution.py:285
  114.3 10.9 %collective-permute-start.20 = (f32[2,12,128]{2,1,0:T(8,128)S(1)}, f32[2,12,128]{2,1,0:T(8,128)S(1)}, u32[]{:S(2)}, u32[]{:S(2)}) collective-permute-start(f32[2,12,128]{2,1,0:T(8,128)S(1)} %rsqrt_multiply_fusion.own_slope_ref.refs_0_), channel_id=1, source_target_pairs={{0,248},{8,16},{16,8},{24,32},{32,24},{40,48},{48,40},{56,64},{64,... | collective-permute-start | bytes 36872 | tf_op jit(solution)/shard_map/ppermute | solution.py:285
  114.8 10.5 %collective-permute-start.21 = (f32[2,12,128]{2,1,0:T(8,128)S(1)}, f32[2,12,128]{2,1,0:T(8,128)S(1)}, u32[]{:S(2)}, u32[]{:S(2)}) collective-permute-start(f32[2,12,128]{2,1,0:T(8,128)S(1)} %rsqrt_multiply_fusion.own_slope_ref.refs_0_), channel_id=1, source_target_pairs={{0,8},{8,0},{16,24},{24,16},{32,40},{40,32},{48,56},{56,48},{64,72... | collective-permute-start | bytes 36872 | tf_op jit(solution)/shard_map/ppermute | solution.py:285
  125.3 11.3 %collective-permute-start.22 = (f32[3,12,128]{2,1,0:T(8,128)S(1)}, f32[3,12,128]{2,1,0:T(8,128)S(1)}, u32[]{:S(2)}, u32[]{:S(2)}) collective-permute-start(f32[3,12,128]{2,1,0:T(8,128)S(1)} %get-tuple-element.158), channel_id=1, source_target_pairs={{0,7},{1,2},{2,1},{3,4},{4,3},{5,6},{6,5},{7,0},{8,15},{9,10},{10,... | collective-permute-start | bytes 55304 | tf_op jit(solution)/shard_map/ppermute | solution.py:285
  127.1 9.5 %collective-permute-start.23 = (f32[3,12,128]{2,1,0:T(8,128)S(1)}, f32[3,12,128]{2,1,0:T(8,128)S(1)}, u32[]{:S(2)}, u32[]{:S(2)}) collective-permute-start(f32[3,12,128]{2,1,0:T(8,128)S(1)} %get-tuple-element.157), channel_id=1, source_target_pairs={{0,1},{1,0},{2,3},{3,2},{4,5},{5,4},{6,7},{7,6},{8,9},{9,8},{10,11... | collective-permute-start | bytes 55304 | tf_op jit(solution)/shard_map/ppermute | solution.py:285
